TPU v7x, 256 devices: a whole 4x4x8 slice. The times are simulated.
256 devices in a mesh: section: 4 (over x), expert: 32 (over z, y_lo, core), dp: 2 (over y_hi).
Axes of the slice: x: 4, y: 4 (y_hi: 2, y_lo: 2; y = y_hi * 2 + y_lo), z: 8, core: 2. Of those that a mesh axis runs over, the one named last changes fastest.
Arguments:
- fwd_in: bfloat16 [4, 3072, 2048], P('section', 'expert'), may hold values from -6 to 6
- fwd_routes: int32 [4, 3072, 8], P('section', 'expert'), may hold values from 0 to 31, all different within a row; in each aligned block of 96 rows (0 to 95, 96 to 191, ..., all dimensions but the last counted through in order) at most 26 rows name the same one
- fwd_numer: int32 [4, 3072, 8], P('section', 'expert'), may hold values from 1 to 255
- bwd_saved: bfloat16 [4, 3072, 2048], P('section', 'expert'), may hold values from -6 to 6
- bwd_routes: int32 [4, 3072, 8], P('section', 'expert'), may hold values from 0 to 31, all different within a row; in each aligned block of 96 rows (0 to 95, 96 to 191, ..., all dimensions but the last counted through in order) at most 26 rows name the same one
- bwd_numer: int32 [4, 3072, 8], P('section', 'expert'), may hold values from 1 to 255
- bwd_grad: bfloat16 [4, 3072, 2048], P('section', 'expert'), may hold values from -6 to 6
- w_gate: bfloat16 [4, 32, 2048, 768], P('section', 'expert', None, 'dp'), may hold values from -0.125 to 0.125
- w_up: bfloat16 [4, 32, 2048, 768], P('section', 'expert', None, 'dp'), may hold values from -0.125 to 0.125
- w_down: bfloat16 [4, 32, 768, 2048], P('section', 'expert', 'dp'), may hold values from -0.21875 to 0.21875
Outputs:
- next_fwd: bfloat16 [4, 3072, 2048], P('section', 'expert')
- next_bwd: bfloat16 [4, 3072, 2048], P('section', 'expert')
- grad_gate: bfloat16 [4, 32, 2048, 768], P('section', 'expert', None, 'dp')
- grad_up: bfloat16 [4, 32, 2048, 768], P('section', 'expert', None, 'dp')
- grad_down: bfloat16 [4, 32, 768, 2048], P('section', 'expert', 'dp')
Inputs may be any that keep to these rules, and one draw needn't show every extreme that they name: `fwd_routes`: each token names 8 different experts. In each aligned block of 96 rows (the tokens of one index of expert of one section) no expert is named more than 26 times; in some blocks some expert is named exactly 26 times. `bwd_routes`: each token names 8 different experts. In each aligned block of 96 rows (the tokens of one index of expert of one section) no expert is named more than 26 times; in some blocks some expert is named exactly 26 times.
All inputs are finite; a program needn't handle non-finite values.
Results may differ from a plain program's by a relative error of at most 0.0058.
Values may be sent and summed in bfloat16 or wider, within the bound.
A program may use at most 128 MiB of HBM per device.

v0:
```python
import jax
import jax.numpy as jnp
from jax import lax
from jax.sharding import PartitionSpec as P

EXPERTS = 32
MOST = 26


def passed_along(block, axis, distance):
    devices = range(lax.axis_size(axis))
    route = [((i - distance) % len(devices), i) for i in devices]
    return lax.ppermute(block, axis, route)


def slot_ranks(routes):
    flat_routes = routes.reshape(-1)
    onehot_table = (flat_routes[:, None] == jnp.arange(EXPERTS, dtype=jnp.int32)[None, :]).astype(
        jnp.int32
    )
    earlier = jnp.cumsum(onehot_table, 0) - onehot_table
    return (flat_routes, jnp.sum(earlier * onehot_table, 1))


def combine_weights(numerators):
    counted = numerators.astype(jnp.float32)
    return counted / jnp.sum(counted, -1, keepdims=True)


def packed_rows(rows, positions, groups):
    filled = jnp.zeros((EXPERTS * MOST, rows.shape[-1]), rows.dtype).at[positions].set(rows)
    return filled.reshape(groups, EXPERTS // groups, MOST, rows.shape[-1])


def handoff(value, direction):
    return passed_along(value, "section", direction)


def project(rows, gate_weight, up_weight):
    gate_value = jnp.einsum("semd,edf->semf", rows, gate_weight, preferred_element_type=jnp.float32)
    up_value = jnp.einsum("semd,edf->semf", rows, up_weight, preferred_element_type=jnp.float32)
    return (gate_value, up_value)


def local_backward(gate_value, up_value, grad_rows, down_weight):
    silu_gate = jax.nn.silu(gate_value)
    sigmoid_gate = jax.nn.sigmoid(gate_value)
    hidden = (silu_gate * up_value).astype(jnp.bfloat16)
    hidden_grad = jnp.einsum(
        "semd,efd->semf", grad_rows, down_weight, preferred_element_type=jnp.float32
    )
    up_grad = (hidden_grad * silu_gate).astype(jnp.bfloat16)
    gate_grad = (
        hidden_grad * up_value * sigmoid_gate * (1.0 + gate_value * (1.0 - sigmoid_gate))
    ).astype(jnp.bfloat16)
    return (hidden, gate_grad, up_grad)


def rows_back(gate_grad, up_grad, gate_weight, up_weight):
    return jnp.einsum(
        "semf,edf->semd", gate_grad, gate_weight, preferred_element_type=jnp.float32
    ) + jnp.einsum("semf,edf->semd", up_grad, up_weight, preferred_element_type=jnp.float32)


def weight_terms(saved_rows, grad_rows, back_hidden, gate_grad, up_grad):
    gate_term = jnp.einsum(
        "semd,semf->edf", saved_rows, gate_grad, preferred_element_type=jnp.float32
    )
    up_term = jnp.einsum("semd,semf->edf", saved_rows, up_grad, preferred_element_type=jnp.float32)
    down_term = jnp.einsum(
        "semf,semd->efd", back_hidden, grad_rows, preferred_element_type=jnp.float32
    )
    return (gate_term, up_term, down_term)


def mix_rows(base, returned, positions, weights, choices_per):
    width = base.shape[-1]
    picked = (
        returned.reshape(-1, width)[positions].reshape(-1, choices_per, width).astype(jnp.float32)
    )
    return (base.astype(jnp.float32) + jnp.sum(weights[:, :, None] * picked, 1)).astype(
        jnp.bfloat16
    )


def local(
    fwd_in, fwd_routes, fwd_numer, bwd_saved, bwd_routes, bwd_numer, bwd_grad, w_gate, w_up, w_down
):
    groups = lax.axis_size("expert")
    inputs = fwd_in[0]
    saved = bwd_saved[0]
    grad_in = bwd_grad[0]
    model_width = inputs.shape[-1]
    choices_per = fwd_routes.shape[-1]
    fwd_flat, fwd_rank = slot_ranks(fwd_routes[0])
    back_flat, back_rank = slot_ranks(bwd_routes[0])
    fwd_positions = fwd_flat * MOST + fwd_rank
    back_positions = back_flat * MOST + back_rank
    mixing = combine_weights(fwd_numer[0])
    back_mixing = combine_weights(bwd_numer[0])
    unit_weights = jnp.ones_like(back_mixing)
    scaled_grad = (back_mixing[:, :, None] * grad_in.astype(jnp.float32)[:, None, :]).astype(
        jnp.bfloat16
    )
    send_inputs = packed_rows(jnp.repeat(inputs, choices_per, 0), fwd_positions, groups)
    send_saved = packed_rows(jnp.repeat(saved, choices_per, 0), back_positions, groups)
    send_grad = packed_rows(scaled_grad.reshape(-1, model_width), back_positions, groups)
    gate_half = w_gate[0]
    up_half = w_up[0]
    down_half = w_down[0]
    recv_inputs, recv_saved, recv_grad = (
        lax.all_to_all(send_inputs, "expert", split_axis=0, concat_axis=0, tiled=True),
        lax.all_to_all(send_saved, "expert", split_axis=0, concat_axis=0, tiled=True),
        lax.all_to_all(send_grad, "expert", split_axis=0, concat_axis=0, tiled=True),
    )
    gate_value, up_value = project(recv_inputs, gate_half, up_half)
    hidden = (jax.nn.silu(gate_value) * up_value).astype(jnp.bfloat16)
    out_term = jnp.einsum("semf,efd->semd", hidden, down_half, preferred_element_type=jnp.float32)
    back_gate, back_up = project(recv_saved, gate_half, up_half)
    back_hidden, gate_grad, up_grad = local_backward(back_gate, back_up, recv_grad, down_half)
    grad_term = rows_back(gate_grad, up_grad, gate_half, up_half)
    gate_term, up_term, down_term = weight_terms(
        recv_saved, recv_grad, back_hidden, gate_grad, up_grad
    )
    gate_sum = gate_term.astype(jnp.bfloat16)
    up_sum = up_term.astype(jnp.bfloat16)
    down_sum = down_term.astype(jnp.bfloat16)
    out_total, grad_total = (
        lax.psum_scatter(out_term, "dp", scatter_dimension=3, tiled=True),
        lax.psum_scatter(grad_term, "dp", scatter_dimension=3, tiled=True),
    )
    out_part = out_total.astype(jnp.bfloat16)
    grad_part = grad_total.astype(jnp.bfloat16)
    out_rows, row_grad = (
        lax.all_gather(out_part, "dp", axis=3, tiled=True),
        lax.all_gather(grad_part, "dp", axis=3, tiled=True),
    )
    back_out, back_grad = (
        lax.all_to_all(out_rows, "expert", split_axis=0, concat_axis=0, tiled=True),
        lax.all_to_all(row_grad, "expert", split_axis=0, concat_axis=0, tiled=True),
    )
    layer_out = mix_rows(inputs, back_out, fwd_positions, mixing, choices_per)
    input_grad = mix_rows(grad_in, back_grad, back_positions, unit_weights, choices_per)
    next_fwd = handoff(layer_out[None], 1)
    next_bwd = handoff(input_grad[None], -1)
    return (next_fwd, next_bwd, gate_sum[None], up_sum[None], down_sum[None])


def solution(mesh):
    in_specs = (
        P("section", "expert", None),
        P("section", "expert", None),
        P("section", "expert", None),
        P("section", "expert", None),
        P("section", "expert", None),
        P("section", "expert", None),
        P("section", "expert", None),
        P("section", "expert", None, "dp"),
        P("section", "expert", None, "dp"),
        P("section", "expert", "dp", None),
    )
    out_specs = (
        P("section", "expert", None),
        P("section", "expert", None),
        P("section", "expert", None, "dp"),
        P("section", "expert", None, "dp"),
        P("section", "expert", "dp", None),
    )
    return jax.shard_map(local, mesh=mesh, in_specs=in_specs, out_specs=out_specs, check_vma=False)
```

profile of v0, /device:TPU:8, one launch (start us, length us, event | category | flops | bytes accessed | tf_op | source)
XLA Modules:
  0.0 709.0 jit_solution(1238418212273189136)
XLA Ops:
  7.2 0.8 broadcast_multiply_fusion.1
  8.0 0.8 copy.33
  9.2 1.7 reduce-window.14
  11.4 9.4 %scatter_custom_fusion = bf16[832,2048]{1,0:T(8,128)(2,1)} fusion(s32[768]{0:T(1024)S(1)} %fusion.125, bf16[]{:T(256)} %constant.9.clone.1, bf16[96,2048]{1,0:T(8,128)(2,1)} %bitcast.260), kind=kCustom, calls=%fused_computation.34 | custom fusion | bytes 3801090 | tf_op jit(solution)/shard_map/scatter | solution.py:31
  20.7 4.8 reshape.252
  25.6 106.8 %all_to_all.25 = bf16[32,1,26,2048]{3,2,1,0:T(8,128)(2,1)S(1)} all-to-all(bf16[32,1,26,2048]{3,2,1,0:T(8,128)(2,1)} %bitcast.259), channel_id=1, replica_groups=mesh['section'=4,'expert'=32,'dp'=2] {'expert'}, dimensions={0} | all-to-all | bytes 6815744 | tf_op jit(solution)/shard_map/all_to_all | solution.py:112
  132.4 1.9 copy-done.2
  134.3 3.1 fusion.59
  137.4 9.4 %convolution_bitcast_fusion = f32[32,1,26,2048]{3,0,2,1:T(8,128)} fusion(bf16[1,1,384,2048]{3,2,1,0:T(8,128)(2,1)S(1)} %copy-done.16, bf16[1,1,2048,384]{3,2,1,0:T(8,128)(2,1)S(1)} %copy-done, bf16[32,1,26,2048]{3,2,1,0:T(8,128)(2,1)} %copy-done.2, f32[32,1,26,384]{3,0,2,1:T(8,128)} %fusion.59), kind=kOutput, calls=%fused_computation.11 | convolution fusion | flops 2619162624 | bytes 14647296 | tf_op jit(solution)/shard_map/semf,efd->semd/dot_general | solution.py:118
  147.9 1.7 reduce-window.16
  150.1 9.0 %scatter_custom_fusion.2 = bf16[832,2048]{1,0:T(8,128)(2,1)} fusion(s32[768]{0:T(1024)S(1)} %fusion.126, bf16[]{:T(256)} %constant.9.clone.1, bf16[96,2048]{1,0:T(8,128)(2,1)S(1)} %bitcast.261), kind=kCustom, calls=%fused_computation.32 | custom fusion | bytes 3801090 | tf_op jit(solution)/shard_map/scatter | solution.py:31
  159.1 4.8 reshape.263
  163.9 5.6 all-to-all-start.3
  170.0 12.7 %scatter_custom_fusion.1 = bf16[832,2048]{1,0:T(8,128)(2,1)} fusion(s32[768]{0:T(1024)S(1)} %fusion.126, f32[96,2048]{1,0:T(8,128)S(1)} %convert_bitcast_fusion, f32[768]{0:T(1024)S(1)} %div.39, bf16[]{:T(256)} %constant.9.clone.1), kind=kCustom, calls=%fused_computation.28 | custom fusion | flops 3145728 | bytes 4198402 | tf_op jit(solution)/shard_map/scatter | solution.py:31
  182.7 4.9 reshape.260
  187.5 78.4 %all-to-all-done.3 = bf16[32,1,26,2048]{3,2,1,0:T(8,128)(2,1)} async-done(((bf16[32,1,26,2048]{3,2,1,0:T(8,128)(2,1)}), bf16[32,1,26,2048]{3,2,1,0:T(8,128)(2,1)}, u32[]{:S(2)}, u32[]{:S(2)}) %all-to-all-start.3) | async-done | bytes 3407904 | tf_op jit(solution)/shard_map/all_to_all | solution.py:113
  265.9 4.9 all-to-all-start.2
  270.9 6.8 reduce-scatter.3.cloned.1.call-done
  277.7 3.5 convert_element_type.113
  281.4 5.3 fusion.79
  286.7 5.3 fusion.74
  292.0 75.5 %all-to-all-done.2 = bf16[32,1,26,2048]{3,2,1,0:T(8,128)(2,1)} async-done(((bf16[32,1,26,2048]{3,2,1,0:T(8,128)(2,1)}), bf16[32,1,26,2048]{3,2,1,0:T(8,128)(2,1)}, u32[]{:S(2)}, u32[]{:S(2)}) %all-to-all-start.2) | async-done | bytes 3407904 | tf_op jit(solution)/shard_map/all_to_all | solution.py:114
  367.4 5.9 fusion.110
  373.4 2.0 fusion.48
  375.4 4.8 add_bitcast_fusion
  380.3 5.8 copy.38
  386.1 5.2 all-to-all-start.1
  391.4 118.5 %reduce-scatter.5.cloned.1.call-done = f32[32,1,26,1024]{3,0,2,1:T(8,128)} async-done(((f32[32,1,26,2048]{3,0,2,1:T(8,128)}), f32[32,1,26,1024]{3,0,2,1:T(8,128)}) %reduce-scatter.5.cloned.1.call-update) | async-done | bytes 3407888 | tf_op jit(solution)/shard_map/reduce_scatter | solution.py:130
  509.9 3.5 convert_element_type.127
  513.4 54.1 %all-gather.5.cloned.1.call-done = bf16[32,1,26,2048]{3,0,2,1:T(8,128)(2,1)} async-done(((bf16[32,1,26,1024]{3,0,2,1:T(8,128)(2,1)}), bf16[32,1,26,2048]{3,0,2,1:T(8,128)(2,1)}) %all-gather.5.cloned.1.call-update) | async-done | bytes 3407888 | tf_op jit(solution)/shard_map/all_gather | solution.py:136
  567.5 5.9 copy.48
  573.4 8.8 %all-to-all-start.4 = ((bf16[32,1,26,2048]{3,2,1,0:T(8,128)(2,1)}), bf16[32,1,26,2048]{3,2,1,0:T(8,128)(2,1)}, u32[]{:S(2)}, u32[]{:S(2)}) async-start(bf16[32,1,26,2048]{3,2,1,0:T(8,128)(2,1)} %copy.48), calls=%async_computation.6 | async-start | bytes 8388608 | tf_op jit(solution)/shard_map/all_to_all | solution.py:140
  582.4 6.6 fusion.39
  589.0 6.4 fusion.42
  595.5 3.3 reshape.258
  598.8 4.3 gather_fusion
  603.1 4.9 fusion
  608.1 0.8 fusion.109
  608.9 1.7 collective-permute-start
  610.6 65.7 %all-to-all-done.4 = bf16[32,1,26,2048]{3,2,1,0:T(8,128)(2,1)} async-done(((bf16[32,1,26,2048]{3,2,1,0:T(8,128)(2,1)}), bf16[32,1,26,2048]{3,2,1,0:T(8,128)(2,1)}, u32[]{:S(2)}, u32[]{:S(2)}) %all-to-all-start.4) | async-done | bytes 3407904 | tf_op jit(solution)/shard_map/all_to_all | solution.py:140
  676.3 3.3 reshape.267
  679.7 4.3 gather_fusion.1
  683.9 4.1 convert_reduce_fusion
  688.2 2.8 collective-permute-start.1
  690.9 6.6 fusion.36
  697.5 1.9 collective-permute-done.1
  699.5 1.8 copy.105
  701.2 0.7 copy.106
  (82 shorter events, 3.5 us)
Async XLA Ops:
  7.2 130.2 %copy-start = (bf16[1,1,2048,384]{3,2,1,0:T(8,128)(2,1)S(1)}, bf16[1,1,2048,384]{3,2,1,0:T(8,128)(2,1)}, u32[]{:S(2)}) copy-start(bf16[1,1,2048,384]{3,2,1,0:T(8,128)(2,1)} %param.18) | copy-start | bytes 4718596
  7.2 270.5 %reduce-scatter.3.cloned.1.call-start = ((), (), s32[]{:S(2)}) async-start(), calls=%async_computation.7 | async-start | bytes 10223616 | tf_op jit(solution)/shard_map/reduce_scatter | solution.py:129
  25.6 108.7 %copy-start.6 = (bf16[1,1,2048,384]{3,2,1,0:T(8,128)(2,1)S(1)}, bf16[1,1,2048,384]{3,2,1,0:T(8,128)(2,1)}, u32[]{:S(2)}) copy-start(bf16[1,1,2048,384]{3,2,1,0:T(8,128)(2,1)} %param.17) | copy-start | bytes 4718596
  132.4 1.9 copy-start.2
  134.3 3.1 copy-start.16
  146.8 0.7 copy-start.15
  146.8 3.4 copy-start.12
  163.9 5.6 copy-start.13
  163.9 6.0 copy-start.4
  163.9 102.0 %all-to-all-start.3 = ((bf16[32,1,26,2048]{3,2,1,0:T(8,128)(2,1)}), bf16[32,1,26,2048]{3,2,1,0:T(8,128)(2,1)}, u32[]{:S(2)}, u32[]{:S(2)}) async-start(bf16[32,1,26,2048]{3,2,1,0:T(8,128)(2,1)} %bitcast.258), calls=%async_computation.4 | async-start | bytes 8388608 | tf_op jit(solution)/shard_map/all_to_all | solution.py:113
  265.9 101.5 %all-to-all-start.2 = ((bf16[32,1,26,2048]{3,2,1,0:T(8,128)(2,1)}), bf16[32,1,26,2048]{3,2,1,0:T(8,128)(2,1)}, u32[]{:S(2)}, u32[]{:S(2)}) async-start(bf16[32,1,26,2048]{3,2,1,0:T(8,128)(2,1)} %bitcast.257), calls=%async_computation.3 | async-start | bytes 8388608 | tf_op jit(solution)/shard_map/all_to_all | solution.py:114
  270.8 10.6 %copy-start.7 = (bf16[1,1,2048,384]{3,2,1,0:T(8,128)(2,1)S(1)}, bf16[1,1,2048,384]{3,2,1,0:T(8,128)(2,1)}, u32[]{:S(2)}) copy-start(bf16[1,1,2048,384]{3,2,1,0:T(8,128)(2,1)} %param.17) | copy-start | bytes 4718596
  270.8 109.4 %all-gather.3.cloned.1.call-start = ((), (), s32[]{:S(2)}) async-start(), calls=%async_computation.8 | async-start | bytes 5111808 | tf_op jit(solution)/shard_map/all_gather | solution.py:135
  281.2 228.7 %reduce-scatter.5.cloned.1.call-start = ((), (), s32[]{:S(2)}) async-start(), calls=%async_computation.9 | async-start | bytes 10223616 | tf_op jit(solution)/shard_map/reduce_scatter | solution.py:130
  373.4 2.0 copy-start.8
  373.4 2.0 copy-start.10
  386.1 187.3 %all-to-all-start.1 = ((bf16[32,1,26,2048]{3,2,1,0:T(8,128)(2,1)}), bf16[32,1,26,2048]{3,2,1,0:T(8,128)(2,1)}, u32[]{:S(2)}, u32[]{:S(2)}) async-start(bf16[32,1,26,2048]{3,2,1,0:T(8,128)(2,1)} %copy.38), calls=%async_computation.2 | async-start | bytes 8388608 | tf_op jit(solution)/shard_map/all_to_all | solution.py:139
  391.3 176.2 %all-gather.5.cloned.1.call-start = ((), (), s32[]{:S(2)}) async-start(), calls=%async_computation.10 | async-start | bytes 5111808 | tf_op jit(solution)/shard_map/all_gather | solution.py:136
  573.4 8.8 %copy-start.14 = (s32[1,96,8]{1,2,0:T(8,128)S(1)}, s32[1,96,8]{1,2,0:T(8,128)}, u32[]{:S(2)}) copy-start(s32[1,96,8]{1,2,0:T(8,128)} %param.12) | copy-start | bytes 9220
  573.4 9.0 %copy-start.11 = (bf16[32,26,384]{2,0,1:T(8,128)(2,1)S(1)}, bf16[32,26,384]{2,0,1:T(8,128)(2,1)}, u32[]{:S(2)}) copy-start(bf16[32,26,384]{2,0,1:T(8,128)(2,1)} %copy-done.10) | copy-start | bytes 1916932
  573.4 102.9 %all-to-all-start.4 = ((bf16[32,1,26,2048]{3,2,1,0:T(8,128)(2,1)}), bf16[32,1,26,2048]{3,2,1,0:T(8,128)(2,1)}, u32[]{:S(2)}, u32[]{:S(2)}) async-start(bf16[32,1,26,2048]{3,2,1,0:T(8,128)(2,1)} %copy.48), calls=%async_computation.6 | async-start | bytes 8388608 | tf_op jit(solution)/shard_map/all_to_all | solution.py:140
  582.4 6.6 copy-start.17
  582.4 6.6 copy-start.18
  603.1 5.0 copy-start.3
  608.9 88.6 %collective-permute-start = (bf16[1,96,2048]{2,1,0:T(8,128)(2,1)}, bf16[1,96,2048]{2,1,0:T(8,128)(2,1)}, u32[]{:S(2)}, u32[]{:S(2)}) collective-permute-start(bf16[1,96,2048]{2,1,0:T(8,128)(2,1)} %fusion.109), channel_id=1, source_target_pairs={{192,0},{0,64},{64,128},{128,192},{193,1},{1,65},{65,129},{129,193... | collective-permute-start | bytes 1179656 | tf_op jit(solution)/shard_map/ppermute | solution.py:13
  683.9 4.1 copy-start.5
  683.9 7.0 copy-start.9
  688.2 11.3 %collective-permute-start.1 = (bf16[1,96,2048]{2,1,0:T(8,128)(2,1)S(1)}, bf16[1,96,2048]{2,1,0:T(8,128)(2,1)S(1)}, u32[]{:S(2)}, u32[]{:S(2)}) collective-permute-start(bf16[1,96,2048]{2,1,0:T(8,128)(2,1)S(1)} %fusion.108), channel_id=1, source_target_pairs={{64,0},{128,64},{192,128},{0,192},{65,1},{129,65},{193,129},{1,193... | collective-permute-start | bytes 1179656 | tf_op jit(solution)/shard_map/ppermute | solution.py:13
  690.9 11.1 %copy-start.1 = (bf16[1,1,2048,384]{3,2,1,0:T(8,128)(2,1)S(1)}, bf16[1,1,2048,384]{3,2,1,0:T(8,128)(2,1)}, u32[]{:S(2)}) copy-start(bf16[1,1,2048,384]{3,2,1,0:T(8,128)(2,1)} %param.18) | copy-start | bytes 4718596
Sparse Core Ops, SparseCore 0:
  146.9 130.7 reduce-scatter.2
  281.3 83.8 all-gather.2
  380.3 129.4 reduce-scatter.4
  513.5 53.9 all-gather.4
where the time goes:
time: 717 us; the launch traced here: 709 us
  waiting for transfers between devices  401 us (56%)
  blocking collectives  107 us (15%)
  local copies, waits for them, and re-layouts  67.6 us (9%)
  matrix products  55.4 us (8%)
  other arithmetic  34.4 us (5%)
  starting transfers between devices  29.3 us (4%)
  between operations  14.6 us (2%)
    reduce_scatter x1, waiting for transfers between devices, local(): lax.psum_scatter(grad_term, 'dp', scatter_dimension=3, tiled=True)  118 us
    all_to_all x1, blocking collectives, local(): lax.all_to_all(send_inputs, 'expert', split_axis=0, concat_axis=0, tiled=...  107 us
    all_to_all x1, waiting for transfers between devices, local(): lax.all_to_all(send_saved, 'expert', split_axis=0, concat_axis=0, tiled=T...  78.4 us
    all_to_all x1, waiting for transfers between devices, local(): lax.all_to_all(send_grad, 'expert', split_axis=0, concat_axis=0, tiled=True)  75.5 us
    all_to_all x1, waiting for transfers between devices, local(): lax.all_to_all(row_grad, 'expert', split_axis=0, concat_axis=0, tiled=True)  65.7 us
    all_gather x1, waiting for transfers between devices, local(): lax.all_gather(grad_part, 'dp', axis=3, tiled=True)  54.1 us
    scatter x2, local copies, waits for them, and re-layouts, packed_rows(): jnp.zeros((EXPERTS * MOST, rows.shape[-1]), rows.dtype).at[positions]  18.3 us
    reshape x3, local copies, waits for them, and re-layouts, packed_rows(): return filled.reshape(groups, EXPERTS // groups, MOST, rows.shape[-1])  14.5 us
  transfers between devices with their start and end apart: 10, of which 7 were waited for; matrix products, arithmetic and copies ran while one was open for 17% of the time, Pallas kernels for 0%

commit v1 on v0

--- a/solution.py
+++ b/solution.py
@@ -11,6 +11,10 @@
     devices = range(lax.axis_size(axis))
     route = [((i - distance) % len(devices), i) for i in devices]
     return lax.ppermute(block, axis, route)
+
+
+def swapped(block):
+    return lax.ppermute(block, "dp", [(0, 1), (1, 0)])
 
 
 def slot_ranks(routes):
@@ -56,12 +60,6 @@
     return (hidden, gate_grad, up_grad)
 
 
-def rows_back(gate_grad, up_grad, gate_weight, up_weight):
-    return jnp.einsum(
-        "semf,edf->semd", gate_grad, gate_weight, preferred_element_type=jnp.float32
-    ) + jnp.einsum("semf,edf->semd", up_grad, up_weight, preferred_element_type=jnp.float32)
-
-
 def weight_terms(saved_rows, grad_rows, back_hidden, gate_grad, up_grad):
     gate_term = jnp.einsum(
         "semd,semf->edf", saved_rows, gate_grad, preferred_element_type=jnp.float32
@@ -74,7 +72,7 @@
 
 
 def mix_rows(base, returned, positions, weights, choices_per):
-    width = base.shape[-1]
+    width = returned.shape[-1]
     picked = (
         returned.reshape(-1, width)[positions].reshape(-1, choices_per, width).astype(jnp.float32)
     )
@@ -91,7 +89,24 @@
     saved = bwd_saved[0]
     grad_in = bwd_grad[0]
     model_width = inputs.shape[-1]
+    half = model_width // lax.axis_size("dp")
+    mine = lax.axis_index("dp") * half
+    theirs = half - mine
     choices_per = fwd_routes.shape[-1]
+    gate_half = w_gate[0]
+    up_half = w_up[0]
+    down_half = w_down[0]
+    down_recv, gate_recv, up_recv = swapped(
+        (
+            lax.dynamic_slice_in_dim(down_half, theirs, half, 2),
+            lax.dynamic_slice_in_dim(gate_half, theirs, half, 1),
+            lax.dynamic_slice_in_dim(up_half, theirs, half, 1),
+        )
+    )
+    down_mine = jnp.concatenate([lax.dynamic_slice_in_dim(down_half, mine, half, 2), down_recv], 1)
+    gate_mine = jnp.concatenate([lax.dynamic_slice_in_dim(gate_half, mine, half, 1), gate_recv], 2)
+    up_mine = jnp.concatenate([lax.dynamic_slice_in_dim(up_half, mine, half, 1), up_recv], 2)
+
     fwd_flat, fwd_rank = slot_ranks(fwd_routes[0])
     back_flat, back_rank = slot_ranks(bwd_routes[0])
     fwd_positions = fwd_flat * MOST + fwd_rank
@@ -105,44 +120,43 @@
     send_inputs = packed_rows(jnp.repeat(inputs, choices_per, 0), fwd_positions, groups)
     send_saved = packed_rows(jnp.repeat(saved, choices_per, 0), back_positions, groups)
     send_grad = packed_rows(scaled_grad.reshape(-1, model_width), back_positions, groups)
-    gate_half = w_gate[0]
-    up_half = w_up[0]
-    down_half = w_down[0]
-    recv_inputs, recv_saved, recv_grad = (
-        lax.all_to_all(send_inputs, "expert", split_axis=0, concat_axis=0, tiled=True),
-        lax.all_to_all(send_saved, "expert", split_axis=0, concat_axis=0, tiled=True),
-        lax.all_to_all(send_grad, "expert", split_axis=0, concat_axis=0, tiled=True),
-    )
+    recv_inputs = lax.all_to_all(send_inputs, "expert", split_axis=0, concat_axis=0, tiled=True)
+    recv_saved = lax.all_to_all(send_saved, "expert", split_axis=0, concat_axis=0, tiled=True)
+    recv_grad = lax.all_to_all(send_grad, "expert", split_axis=0, concat_axis=0, tiled=True)
+
     gate_value, up_value = project(recv_inputs, gate_half, up_half)
     hidden = (jax.nn.silu(gate_value) * up_value).astype(jnp.bfloat16)
-    out_term = jnp.einsum("semf,efd->semd", hidden, down_half, preferred_element_type=jnp.float32)
+    hidden_all = jnp.concatenate([hidden, swapped(hidden)], -1)
+    out_part = jnp.einsum(
+        "semf,efd->semd", hidden_all, down_mine, preferred_element_type=jnp.float32
+    ).astype(jnp.bfloat16)
+
     back_gate, back_up = project(recv_saved, gate_half, up_half)
     back_hidden, gate_grad, up_grad = local_backward(back_gate, back_up, recv_grad, down_half)
-    grad_term = rows_back(gate_grad, up_grad, gate_half, up_half)
     gate_term, up_term, down_term = weight_terms(
         recv_saved, recv_grad, back_hidden, gate_grad, up_grad
     )
+    gate_other, up_other = swapped((gate_grad, up_grad))
+    gate_all = jnp.concatenate([gate_grad, gate_other], -1)
+    up_all = jnp.concatenate([up_grad, up_other], -1)
+    grad_part = (
+        jnp.einsum("semf,edf->semd", gate_all, gate_mine, preferred_element_type=jnp.float32)
+        + jnp.einsum("semf,edf->semd", up_all, up_mine, preferred_element_type=jnp.float32)
+    ).astype(jnp.bfloat16)
+
+    back_out = lax.all_to_all(out_part, "expert", split_axis=0, concat_axis=0, tiled=True)
+    back_grad = lax.all_to_all(grad_part, "expert", split_axis=0, concat_axis=0, tiled=True)
+    inputs_part = lax.dynamic_slice_in_dim(inputs, mine, half, 1)
+    grad_in_part = lax.dynamic_slice_in_dim(grad_in, mine, half, 1)
+    layer_out = mix_rows(inputs_part, back_out, fwd_positions, mixing, choices_per)
+    input_grad = mix_rows(grad_in_part, back_grad, back_positions, unit_weights, choices_per)
+    layer_out = lax.all_gather(layer_out, "dp", axis=1, tiled=True)
+    input_grad = lax.all_gather(input_grad, "dp", axis=1, tiled=True)
+    next_fwd = handoff(layer_out[None], 1)
+    next_bwd = handoff(input_grad[None], -1)
     gate_sum = gate_term.astype(jnp.bfloat16)
     up_sum = up_term.astype(jnp.bfloat16)
     down_sum = down_term.astype(jnp.bfloat16)
-    out_total, grad_total = (
-        lax.psum_scatter(out_term, "dp", scatter_dimension=3, tiled=True),
-        lax.psum_scatter(grad_term, "dp", scatter_dimension=3, tiled=True),
-    )
-    out_part = out_total.astype(jnp.bfloat16)
-    grad_part = grad_total.astype(jnp.bfloat16)
-    out_rows, row_grad = (
-        lax.all_gather(out_part, "dp", axis=3, tiled=True),
-        lax.all_gather(grad_part, "dp", axis=3, tiled=True),
-    )
-    back_out, back_grad = (
-        lax.all_to_all(out_rows, "expert", split_axis=0, concat_axis=0, tiled=True),
-        lax.all_to_all(row_grad, "expert", split_axis=0, concat_axis=0, tiled=True),
-    )
-    layer_out = mix_rows(inputs, back_out, fwd_positions, mixing, choices_per)
-    input_grad = mix_rows(grad_in, back_grad, back_positions, unit_weights, choices_per)
-    next_fwd = handoff(layer_out[None], 1)
-    next_bwd = handoff(input_grad[None], -1)
     return (next_fwd, next_bwd, gate_sum[None], up_sum[None], down_sum[None])
 
 

time: 717 us -> 521 us (0.73)
  waiting for transfers between devices: 401 us -> 303 us
  blocking collectives: 107 us -> 22.7 us
  starting transfers between devices: 29.3 us -> 57.5 us
  between operations: 14.6 us -> 1.27 us
  other arithmetic: 34.4 us -> 24.4 us
  local copies, waits for them, and re-layouts: 67.6 us -> 57.6 us
  matrix products: 55.4 us -> 47.8 us
    ppermute x0 -> x6, waiting for transfers between devices: none -> 127 us  [swapped(): return lax.ppermute(block, 'dp', [(0, 1), (1, 0)])]
    reduce_scatter x2 -> x0, waiting for transfers between devices: 125 us -> none  [the longest x1 118 us: local(): lax.psum_scatter(grad_term, 'dp', scatter_dimension=3, tiled=True)]
    all_to_all x1 -> x0, blocking collectives: 107 us -> none  [local(): lax.all_to_all(send_inputs, 'expert', split_axis=0, concat_axis=0, tiled=...]
    all_gather x2 -> x0, waiting for transfers between devices: 54.1 us -> none  [the longest x1 54.1 us: local(): lax.all_gather(grad_part, 'dp', axis=3, tiled=True)]
    all_to_all x2 -> x3, waiting for transfers between devices: 65.7 us -> 11.7 us  [the longest x1 11.7 us: local(): lax.all_to_all(out_part, 'expert', split_axis=0, concat_axis=0, tiled=True)]
    all_gather x0 -> x2, blocking collectives: none -> 22.7 us  [the longest x1 13.6 us: local(): input_grad = lax.all_gather(input_grad, 'dp', axis=1, tiled=True)]
    all_gather x2 -> x0, local copies, waits for them, and re-layouts: 11.7 us -> none  [the longest x1 5.89 us: local(): lax.all_gather(grad_part, 'dp', axis=3, tiled=True)]
    dot_general x3, matrix products: 16.1 us -> 4.53 us  [the longest x1 1.52 us: local(): jnp.einsum('semf,edf->semd', gate_all, gate_mine, preferred_element_type=...]
  transfers between devices with their start and end apart: 10 -> 13, of which waited for: 7 -> 10; matrix products, arithmetic and copies ran while one was open for 17% -> 19% of each run, Pallas kernels for 0% -> 0%
where the time goes in v1:
time: 521 us; the launch traced here: 514 us
  waiting for transfers between devices  303 us (58%)
  local copies, waits for them, and re-layouts  57.6 us (11%)
  starting transfers between devices  57.5 us (11%)
  matrix products  47.8 us (9%)
  other arithmetic  24.4 us (5%)
  blocking collectives  22.7 us (4%)
    ppermute x6, waiting for transfers between devices, swapped(): return lax.ppermute(block, 'dp', [(0, 1), (1, 0)])  127 us
    all_to_all x1, waiting for transfers between devices, local(): lax.all_to_all(send_saved, 'expert', split_axis=0, concat_axis=0, tiled=T...  80.2 us
    all_to_all x1, waiting for transfers between devices, local(): lax.all_to_all(send_grad, 'expert', split_axis=0, concat_axis=0, tiled=True)  79.9 us
    scatter x2, local copies, waits for them, and re-layouts, packed_rows(): jnp.zeros((EXPERTS * MOST, rows.shape[-1]), rows.dtype).at[positions]  18 us
    reshape x3, local copies, waits for them, and re-layouts, packed_rows(): return filled.reshape(groups, EXPERTS // groups, MOST, rows.shape[-1])  14.6 us
    all_gather x1, blocking collectives, local(): input_grad = lax.all_gather(input_grad, 'dp', axis=1, tiled=True)  13.6 us
    scatter x1, other arithmetic, packed_rows(): jnp.zeros((EXPERTS * MOST, rows.shape[-1]), rows.dtype).at[positions]  12.6 us
    all_to_all x1, waiting for transfers between devices, local(): lax.all_to_all(out_part, 'expert', split_axis=0, concat_axis=0, tiled=True)  11.7 us
  transfers between devices with their start and end apart: 13, of which 10 were waited for; matrix products, arithmetic and copies ran while one was open for 19% of the time, Pallas kernels for 0%

profile of v1, /device:TPU:8, one launch (start us, length us, event | category | flops | bytes accessed | tf_op | source)
XLA Modules:
  0.0 513.9 jit_solution(12449324526280599132)
XLA Ops:
  6.2 1.7 reduce-window.16
  8.2 1.7 reduce-window.14
  10.6 12.6 %scatter_custom_fusion.1 = bf16[832,2048]{1,0:T(8,128)(2,1)} fusion(s32[768]{0:T(1024)S(1)} %get-tuple-element.15, f32[96,2048]{1,0:T(8,128)S(1)} %bitcast_convert_fusion.3, f32[768]{0:T(1024)S(1)} %div.39, bf16[]{:T(256)} %constant.36.clone.1), kind=kCustom, calls=%fused_computation.24 | custom fusion | flops 3145728 | bytes 4198402 | tf_op jit(solution)/shard_map/scatter | solution.py:35
  23.2 4.8 reshape.280
  28.1 10.5 %all-to-all-start.2 = ((bf16[32,1,26,2048]{3,2,1,0:T(8,128)(2,1)}), bf16[32,1,26,2048]{3,2,1,0:T(8,128)(2,1)}, u32[]{:S(2)}, u32[]{:S(2)}) async-start(bf16[32,1,26,2048]{3,2,1,0:T(8,128)(2,1)} %bitcast.269), calls=%async_computation.2 | async-start | bytes 8388608 | tf_op jit(solution)/shard_map/all_to_all | solution.py:125
  38.6 9.0 %scatter_custom_fusion.2 = bf16[832,2048]{1,0:T(8,128)(2,1)} fusion(s32[768]{0:T(1024)S(1)} %get-tuple-element.15, bf16[]{:T(256)} %constant.36.clone.1, bf16[96,2048]{1,0:T(8,128)(2,1)S(1)} %bitcast.266), kind=kCustom, calls=%fused_computation.31 | custom fusion | bytes 3801090 | tf_op jit(solution)/shard_map/scatter | solution.py:35
  47.6 4.9 reshape.284
  52.5 79.9 %all-to-all-done.2 = bf16[32,1,26,2048]{3,2,1,0:T(8,128)(2,1)} async-done(((bf16[32,1,26,2048]{3,2,1,0:T(8,128)(2,1)}), bf16[32,1,26,2048]{3,2,1,0:T(8,128)(2,1)}, u32[]{:S(2)}, u32[]{:S(2)}) %all-to-all-start.2) | async-done | bytes 3407904 | tf_op jit(solution)/shard_map/all_to_all | solution.py:125
  132.5 7.5 %all-to-all-start.3 = ((bf16[32,1,26,2048]{3,2,1,0:T(8,128)(2,1)}), bf16[32,1,26,2048]{3,2,1,0:T(8,128)(2,1)}, u32[]{:S(2)}, u32[]{:S(2)}) async-start(bf16[32,1,26,2048]{3,2,1,0:T(8,128)(2,1)} %bitcast.268), calls=%async_computation.3 | async-start | bytes 8388608 | tf_op jit(solution)/shard_map/all_to_all | solution.py:124
  140.0 8.9 %scatter_custom_fusion = bf16[832,2048]{1,0:T(8,128)(2,1)} fusion(s32[768]{0:T(1024)S(1)} %get-tuple-element.14, bf16[]{:T(256)} %constant.36.clone.1, bf16[96,2048]{1,0:T(8,128)(2,1)S(1)} %bitcast.270), kind=kCustom, calls=%fused_computation.33 | custom fusion | bytes 3801090 | tf_op jit(solution)/shard_map/scatter | solution.py:35
  148.9 4.9 reshape.272
  153.8 80.2 %all-to-all-done.3 = bf16[32,1,26,2048]{3,2,1,0:T(8,128)(2,1)} async-done(((bf16[32,1,26,2048]{3,2,1,0:T(8,128)(2,1)}), bf16[32,1,26,2048]{3,2,1,0:T(8,128)(2,1)}, u32[]{:S(2)}, u32[]{:S(2)}) %all-to-all-start.3) | async-done | bytes 3407904 | tf_op jit(solution)/shard_map/all_to_all | solution.py:124
  234.1 7.6 %all-to-all-start = ((bf16[32,1,26,2048]{3,2,1,0:T(8,128)(2,1)}), bf16[32,1,26,2048]{3,2,1,0:T(8,128)(2,1)}, u32[]{:S(2)}, u32[]{:S(2)}) async-start(bf16[32,1,26,2048]{3,2,1,0:T(8,128)(2,1)} %bitcast.267), calls=%async_computation | async-start | bytes 8388608 | tf_op jit(solution)/shard_map/all_to_all | solution.py:123
  241.8 2.6 collective-permute-start.5
  244.4 4.2 fusion.79
  248.7 4.8 fusion.74
  253.5 5.7 %multiply_convert_fusion.2 = (bf16[32,1,26,384]{3,0,2,1:T(8,128)(2,1)S(1)}, bf16[32,1,26,384]{3,0,2,1:T(8,128)(2,1)S(1)}, f32[32,1,26,384]{3,0,2,1:T(8,128)}) fusion(f32[32,1,26,384]{3,0,2,1:T(8,128)S(1)} %fusion.74, f32[32,1,26,384]{3,0,2,1:T(8,128)S(1)} %fusion.79, bf16[1,1,2048,384]{3,2,1,0:T(8,128)(2,1)S(1)} %copy-done.4, ...), kind=kOutput, calls=%fused_computation.85 | convolution fusion | flops 1312776192 | bytes 10092544 | tf_op jit(solution)/shard_map/semd,edf->semf/dot_general | solution.py:44
  260.6 2.4 collective-permute-start.3
  264.2 21.9 %collective-permute-done.5 = bf16[1,1024,384]{2,1,0:T(8,128)(2,1)S(1)} collective-permute-done((bf16[1,1024,384]{2,1,0:T(8,128)(2,1)S(1)}, bf16[1,1024,384]{2,1,0:T(8,128)(2,1)S(1)}, u32[]{:S(2)}, u32[]{:S(2)}) %collective-permute-start.5) | collective-permute-done | bytes 786464 | tf_op jit(solution)/shard_map/ppermute | solution.py:17
  286.2 21.0 %collective-permute-done.6 = bf16[32,1,26,384]{3,0,2,1:T(8,128)(2,1)S(1)} collective-permute-done((bf16[32,1,26,384]{3,0,2,1:T(8,128)(2,1)S(1)}, bf16[32,1,26,384]{3,0,2,1:T(8,128)(2,1)S(1)}, u32[]{:S(2)}, u32[]{:S(2)}) %collective-permute-start.6) | collective-permute-done | bytes 639008 | tf_op jit(solution)/shard_map/ppermute | solution.py:17
  308.7 29.1 %collective-permute-done.3 = bf16[1,1024,384]{2,1,0:T(8,128)(2,1)S(1)} collective-permute-done((bf16[1,1024,384]{2,1,0:T(8,128)(2,1)S(1)}, bf16[1,1024,384]{2,1,0:T(8,128)(2,1)S(1)}, u32[]{:S(2)}, u32[]{:S(2)}) %collective-permute-start.3) | collective-permute-done | bytes 786464 | tf_op jit(solution)/shard_map/ppermute | solution.py:17
  337.8 13.2 %collective-permute-done.4 = bf16[32,1,26,384]{3,0,2,1:T(8,128)(2,1)S(1)} collective-permute-done((bf16[32,1,26,384]{3,0,2,1:T(8,128)(2,1)S(1)}, bf16[32,1,26,384]{3,0,2,1:T(8,128)(2,1)S(1)}, u32[]{:S(2)}, u32[]{:S(2)}) %collective-permute-start.4) | collective-permute-done | bytes 639008 | tf_op jit(solution)/shard_map/ppermute | solution.py:17
  351.0 1.5 fusion.63
  352.5 2.3 copy.48
  354.8 8.4 %all-to-all-start.4 = ((bf16[32,1,26,1024]{3,2,1,0:T(8,128)(2,1)}), bf16[32,1,26,1024]{3,2,1,0:T(8,128)(2,1)S(1)}, u32[]{:S(2)}, u32[]{:S(2)}) async-start(bf16[32,1,26,1024]{3,2,1,0:T(8,128)(2,1)} %copy.48), calls=%async_computation.4 | async-start | bytes 4194304 | tf_op jit(solution)/shard_map/all_to_all | solution.py:148
  363.2 1.6 dynamic-slice_bitcast_fusion.5
  366.2 4.3 fusion.64
  370.5 4.5 fusion.94
  375.0 2.4 collective-permute-start.1
  377.4 25.5 %collective-permute-done = bf16[1,384,1024]{2,1,0:T(8,128)(2,1)S(1)} collective-permute-done((bf16[1,384,1024]{2,1,0:T(8,128)(2,1)S(1)}, bf16[1,384,1024]{2,1,0:T(8,128)(2,1)S(1)}, u32[]{:S(2)}, u32[]{:S(2)}) %collective-permute-start) | collective-permute-done | bytes 786464 | tf_op jit(solution)/shard_map/ppermute | solution.py:17
  402.8 16.6 %collective-permute-done.1 = bf16[32,1,26,384]{3,0,2,1:T(8,128)(2,1)S(1)} collective-permute-done((bf16[32,1,26,384]{3,0,2,1:T(8,128)(2,1)S(1)}, bf16[32,1,26,384]{3,0,2,1:T(8,128)(2,1)S(1)}, u32[]{:S(2)}, u32[]{:S(2)}) %collective-permute-start.1) | collective-permute-done | bytes 639008 | tf_op jit(solution)/shard_map/ppermute | solution.py:17
  420.9 2.4 copy.38
  424.7 8.0 %all-to-all-start.1 = ((bf16[32,1,26,1024]{3,2,1,0:T(8,128)(2,1)}), bf16[32,1,26,1024]{3,2,1,0:T(8,128)(2,1)}, u32[]{:S(2)}, u32[]{:S(2)}) async-start(bf16[32,1,26,1024]{3,2,1,0:T(8,128)(2,1)} %copy.38), calls=%async_computation.1 | async-start | bytes 4194304 | tf_op jit(solution)/shard_map/all_to_all | solution.py:147
  432.9 6.8 %fusion.36 = bf16[1,1,2048,384]{3,2,1,0:T(8,128)(2,1)} fusion(bf16[32,1,26,2048]{3,2,1,0:T(8,128)(2,1)} %all-to-all-done.3, bf16[32,1,26,384]{3,0,2,1:T(8,128)(2,1)} %copy-done.13), kind=kOutput, calls=%fused_computation.41 | convolution fusion | flops 1309409280 | bytes 5619712 | tf_op jit(solution)/shard_map/semd,semf->edf/dot_general | solution.py:64
  439.6 6.5 %fusion.42 = bf16[1,1,384,2048]{3,2,1,0:T(8,128)(2,1)} fusion(bf16[32,1,26,2048]{3,2,1,0:T(8,128)(2,1)} %all-to-all-done.2, f32[32,1,26,384]{3,0,2,1:T(8,128)S(1)} %copy-done.15, f32[32,1,26,384]{3,0,2,1:T(8,128)S(1)} %copy-done.16), kind=kOutput, calls=%fused_computation.43 | convolution fusion | flops 1311326208 | bytes 7536640 | tf_op jit(solution)/shard_map/semf,semd->efd/dot_general | solution.py:68
  446.1 2.5 reshape.289
  448.7 3.6 gather_fusion.1
  452.2 2.5 convert_reduce_fusion
  454.7 13.6 %all_gather.7 = bf16[96,2048]{1,0:T(8,128)(2,1)S(1)} all-gather(bf16[96,1024]{1,0:T(8,128)(2,1)S(1)} %fusion.114), channel_id=1, replica_groups=mesh['section'=4,'expert'=32,'dp'=2] {'dp'}, dimensions={1}, use_global_device_ids=true | all-gather | bytes 589824 | tf_op jit(solution)/shard_map/all_gather | solution.py:154
  468.4 2.8 collective-permute-start.7
  471.1 11.7 %all-to-all-done.1 = bf16[32,1,26,1024]{3,2,1,0:T(8,128)(2,1)} async-done(((bf16[32,1,26,1024]{3,2,1,0:T(8,128)(2,1)}), bf16[32,1,26,1024]{3,2,1,0:T(8,128)(2,1)}, u32[]{:S(2)}, u32[]{:S(2)}) %all-to-all-start.1) | async-done | bytes 1703968 | tf_op jit(solution)/shard_map/all_to_all | solution.py:147
  482.8 2.5 reshape.277
  485.3 3.6 gather_fusion
  488.9 2.5 fusion.19
  491.4 9.1 %all_gather.6 = bf16[96,2048]{1,0:T(8,128)(2,1)S(1)} all-gather(bf16[96,1024]{1,0:T(8,128)(2,1)S(1)} %fusion.115), channel_id=1, replica_groups=mesh['section'=4,'expert'=32,'dp'=2] {'dp'}, dimensions={1}, use_global_device_ids=true | all-gather | bytes 589824 | tf_op jit(solution)/shard_map/all_gather | solution.py:153
  500.5 1.7 collective-permute-start.2
  502.2 6.5 %fusion.39 = bf16[1,1,2048,384]{3,2,1,0:T(8,128)(2,1)} fusion(bf16[32,1,26,2048]{3,2,1,0:T(8,128)(2,1)} %all-to-all-done.3, bf16[32,1,26,384]{3,0,2,1:T(8,128)(2,1)S(1)} %copy-done.12), kind=kOutput, calls=%fused_computation.42 | convolution fusion | flops 1309409280 | bytes 5619712 | tf_op jit(solution)/shard_map/semd,semf->edf/dot_general | solution.py:67
  508.7 3.4 collective-permute-done.2
  (82 shorter events, 16.7 us)
Async XLA Ops:
  0.6 37.9 %copy-start = (bf16[1,96,2048]{2,1,0:T(8,128)(2,1)S(1)}, bf16[1,96,2048]{2,1,0:T(8,128)(2,1)}, u32[]{:S(2)}) copy-start(bf16[1,96,2048]{2,1,0:T(8,128)(2,1)} %param.13) | copy-start | bytes 1179652
  0.6 9.6 %copy-start.9 = (bf16[1,96,2048]{2,1,0:T(8,128)(2,1)S(1)}, bf16[1,96,2048]{2,1,0:T(8,128)(2,1)}, u32[]{:S(2)}) copy-start(bf16[1,96,2048]{2,1,0:T(8,128)(2,1)} %param.16) | copy-start | bytes 1179652
  28.1 104.4 %all-to-all-start.2 = ((bf16[32,1,26,2048]{3,2,1,0:T(8,128)(2,1)}), bf16[32,1,26,2048]{3,2,1,0:T(8,128)(2,1)}, u32[]{:S(2)}, u32[]{:S(2)}) async-start(bf16[32,1,26,2048]{3,2,1,0:T(8,128)(2,1)} %bitcast.269), calls=%async_computation.2 | async-start | bytes 8388608 | tf_op jit(solution)/shard_map/all_to_all | solution.py:125
  132.5 7.5 %copy-start.8 = (bf16[1,96,2048]{2,1,0:T(8,128)(2,1)S(1)}, bf16[1,96,2048]{2,1,0:T(8,128)(2,1)}, u32[]{:S(2)}) copy-start(bf16[1,96,2048]{2,1,0:T(8,128)(2,1)} %param.10) | copy-start | bytes 1179652
  132.5 101.6 %all-to-all-start.3 = ((bf16[32,1,26,2048]{3,2,1,0:T(8,128)(2,1)}), bf16[32,1,26,2048]{3,2,1,0:T(8,128)(2,1)}, u32[]{:S(2)}, u32[]{:S(2)}) async-start(bf16[32,1,26,2048]{3,2,1,0:T(8,128)(2,1)} %bitcast.268), calls=%async_computation.3 | async-start | bytes 8388608 | tf_op jit(solution)/shard_map/all_to_all | solution.py:124
  234.1 7.6 %copy-start.6 = (bf16[1,1,2048,384]{3,2,1,0:T(8,128)(2,1)S(1)}, bf16[1,1,2048,384]{3,2,1,0:T(8,128)(2,1)}, u32[]{:S(2)}) copy-start(bf16[1,1,2048,384]{3,2,1,0:T(8,128)(2,1)} %param.18) | copy-start | bytes 4718596
  234.1 120.8 %all-to-all-start = ((bf16[32,1,26,2048]{3,2,1,0:T(8,128)(2,1)}), bf16[32,1,26,2048]{3,2,1,0:T(8,128)(2,1)}, u32[]{:S(2)}, u32[]{:S(2)}) async-start(bf16[32,1,26,2048]{3,2,1,0:T(8,128)(2,1)} %bitcast.267), calls=%async_computation | async-start | bytes 8388608 | tf_op jit(solution)/shard_map/all_to_all | solution.py:123
  241.8 6.8 %copy-start.3 = (bf16[1,1,384,2048]{3,2,1,0:T(8,128)(2,1)S(1)}, bf16[1,1,384,2048]{3,2,1,0:T(8,128)(2,1)}, u32[]{:S(2)}) copy-start(bf16[1,1,384,2048]{3,2,1,0:T(8,128)(2,1)} %param.19) | copy-start | bytes 4718596
  241.8 44.3 %collective-permute-start.5 = (bf16[1,1024,384]{2,1,0:T(8,128)(2,1)S(1)}, bf16[1,1024,384]{2,1,0:T(8,128)(2,1)S(1)}, u32[]{:S(2)}, u32[]{:S(2)}) collective-permute-start(bf16[1,1024,384]{2,1,0:T(8,128)(2,1)S(1)} %get-tuple-element.10), channel_id=1, source_target_pairs={{0,1},{1,0},{2,3},{3,2},{4,5},{5,4},{6,7},{7,6},{8,9},{9,8},{10,11... | collective-permute-start | bytes 2359304 | tf_op jit(solution)/shard_map/ppermute | solution.py:17
  248.7 4.8 copy-start.14
  248.7 4.8 copy-start.4
  259.2 49.5 %copy-start.11 = (bf16[32,1,26,384]{3,0,2,1:T(8,128)(2,1)}, bf16[32,1,26,384]{3,0,2,1:T(8,128)(2,1)S(1)}, u32[]{:S(2)}) copy-start(bf16[32,1,26,384]{3,0,2,1:T(8,128)(2,1)S(1)} %get-tuple-element.6) | copy-start | bytes 1916932
  259.2 91.8 %copy-start.13 = (bf16[32,1,26,384]{3,0,2,1:T(8,128)(2,1)}, bf16[32,1,26,384]{3,0,2,1:T(8,128)(2,1)S(1)}, u32[]{:S(2)}) copy-start(bf16[32,1,26,384]{3,0,2,1:T(8,128)(2,1)S(1)} %get-tuple-element.5) | copy-start | bytes 1916932
  259.2 47.9 %collective-permute-start.6 = (bf16[32,1,26,384]{3,0,2,1:T(8,128)(2,1)S(1)}, bf16[32,1,26,384]{3,0,2,1:T(8,128)(2,1)S(1)}, u32[]{:S(2)}, u32[]{:S(2)}) collective-permute-start(bf16[32,1,26,384]{3,0,2,1:T(8,128)(2,1)S(1)} %get-tuple-element.6), channel_id=1, source_target_pairs={{0,1},{1,0},{2,3},{3,2},{4,5},{5,4},{6,7},{7,6},{8,9},{9,8},{10,11... | collective-permute-start | bytes 1916936 | tf_op jit(solution)/shard_map/ppermute | solution.py:17
  260.6 77.2 %collective-permute-start.3 = (bf16[1,1024,384]{2,1,0:T(8,128)(2,1)S(1)}, bf16[1,1024,384]{2,1,0:T(8,128)(2,1)S(1)}, u32[]{:S(2)}, u32[]{:S(2)}) collective-permute-start(bf16[1,1024,384]{2,1,0:T(8,128)(2,1)S(1)} %get-tuple-element.8), channel_id=1, source_target_pairs={{0,1},{1,0},{2,3},{3,2},{4,5},{5,4},{6,7},{7,6},{8,9},{9,8},{10,11... | collective-permute-start | bytes 2359304 | tf_op jit(solution)/shard_map/ppermute | solution.py:17
  263.0 88.0 %collective-permute-start.4 = (bf16[32,1,26,384]{3,0,2,1:T(8,128)(2,1)S(1)}, bf16[32,1,26,384]{3,0,2,1:T(8,128)(2,1)S(1)}, u32[]{:S(2)}, u32[]{:S(2)}) collective-permute-start(bf16[32,1,26,384]{3,0,2,1:T(8,128)(2,1)S(1)} %get-tuple-element.5), channel_id=1, source_target_pairs={{0,1},{1,0},{2,3},{3,2},{4,5},{5,4},{6,7},{7,6},{8,9},{9,8},{10,11... | collective-permute-start | bytes 1916936 | tf_op jit(solution)/shard_map/ppermute | solution.py:17
  354.8 68.4 %all-to-all-start.4 = ((bf16[32,1,26,1024]{3,2,1,0:T(8,128)(2,1)}), bf16[32,1,26,1024]{3,2,1,0:T(8,128)(2,1)S(1)}, u32[]{:S(2)}, u32[]{:S(2)}) async-start(bf16[32,1,26,1024]{3,2,1,0:T(8,128)(2,1)} %copy.48), calls=%async_computation.4 | async-start | bytes 4194304 | tf_op jit(solution)/shard_map/all_to_all | solution.py:148
  363.2 3.0 copy-start.5
  364.9 5.6 %copy-start.7 = (bf16[1,1,2048,384]{3,2,1,0:T(8,128)(2,1)S(1)}, bf16[1,1,2048,384]{3,2,1,0:T(8,128)(2,1)}, u32[]{:S(2)}) copy-start(bf16[1,1,2048,384]{3,2,1,0:T(8,128)(2,1)} %param.18) | copy-start | bytes 4718596
  364.9 38.0 %collective-permute-start = (bf16[1,384,1024]{2,1,0:T(8,128)(2,1)S(1)}, bf16[1,384,1024]{2,1,0:T(8,128)(2,1)S(1)}, u32[]{:S(2)}, u32[]{:S(2)}) collective-permute-start(bf16[1,384,1024]{2,1,0:T(8,128)(2,1)S(1)} %get-tuple-element.12), channel_id=1, source_target_pairs={{0,1},{1,0},{2,3},{3,2},{4,5},{5,4},{6,7},{7,6},{8,9},{9,8},{10,11... | collective-permute-start | bytes 2359304 | tf_op jit(solution)/shard_map/ppermute | solution.py:17
  370.5 6.9 %copy-start.10 = (s32[1,96,8]{1,2,0:T(8,128)S(1)}, s32[1,96,8]{1,2,0:T(8,128)}, u32[]{:S(2)}) copy-start(s32[1,96,8]{1,2,0:T(8,128)} %param.12) | copy-start | bytes 9220
  375.0 44.5 %collective-permute-start.1 = (bf16[32,1,26,384]{3,0,2,1:T(8,128)(2,1)S(1)}, bf16[32,1,26,384]{3,0,2,1:T(8,128)(2,1)S(1)}, u32[]{:S(2)}, u32[]{:S(2)}) collective-permute-start(bf16[32,1,26,384]{3,0,2,1:T(8,128)(2,1)S(1)} %fusion.94), channel_id=1, source_target_pairs={{0,1},{1,0},{2,3},{3,2},{4,5},{5,4},{6,7},{7,6},{8,9},{9,8},{10,11... | collective-permute-start | bytes 1916936 | tf_op jit(solution)/shard_map/ppermute | solution.py:17
  423.3 1.4 copy-start.2
  424.7 58.2 %all-to-all-start.1 = ((bf16[32,1,26,1024]{3,2,1,0:T(8,128)(2,1)}), bf16[32,1,26,1024]{3,2,1,0:T(8,128)(2,1)}, u32[]{:S(2)}, u32[]{:S(2)}) async-start(bf16[32,1,26,1024]{3,2,1,0:T(8,128)(2,1)} %copy.38), calls=%async_computation.1 | async-start | bytes 4194304 | tf_op jit(solution)/shard_map/all_to_all | solution.py:147
  432.8 6.8 %copy-start.15 = (f32[32,1,26,384]{3,0,2,1:T(8,128)S(1)}, f32[32,1,26,384]{3,0,2,1:T(8,128)}, u32[]{:S(2)}) copy-start(f32[32,1,26,384]{3,0,2,1:T(8,128)} %copy-done.14) | copy-start | bytes 3833860
  432.8 6.8 %copy-start.16 = (f32[32,1,26,384]{3,0,2,1:T(8,128)S(1)}, f32[32,1,26,384]{3,0,2,1:T(8,128)}, u32[]{:S(2)}) copy-start(f32[32,1,26,384]{3,0,2,1:T(8,128)} %get-tuple-element.13) | copy-start | bytes 3833860
  468.4 40.4 %collective-permute-start.7 = (bf16[1,96,2048]{2,1,0:T(8,128)(2,1)S(1)}, bf16[1,96,2048]{2,1,0:T(8,128)(2,1)S(1)}, u32[]{:S(2)}, u32[]{:S(2)}) collective-permute-start(bf16[1,96,2048]{2,1,0:T(8,128)(2,1)S(1)} %bitcast.271), channel_id=1, source_target_pairs={{64,0},{128,64},{192,128},{0,192},{65,1},{129,65},{193,129},{1,193... | collective-permute-start | bytes 1179656 | tf_op jit(solution)/shard_map/ppermute | solution.py:13
  488.9 13.3 %copy-start.12 = (bf16[32,1,26,384]{3,0,2,1:T(8,128)(2,1)S(1)}, bf16[32,1,26,384]{3,0,2,1:T(8,128)(2,1)}, u32[]{:S(2)}) copy-start(bf16[32,1,26,384]{3,0,2,1:T(8,128)(2,1)} %copy-done.11) | copy-start | bytes 1916932
  500.5 11.6 %collective-permute-start.2 = (bf16[1,96,2048]{2,1,0:T(8,128)(2,1)S(1)}, bf16[1,96,2048]{2,1,0:T(8,128)(2,1)S(1)}, u32[]{:S(2)}, u32[]{:S(2)}) collective-permute-start(bf16[1,96,2048]{2,1,0:T(8,128)(2,1)S(1)} %bitcast.272), channel_id=1, source_target_pairs={{192,0},{0,64},{64,128},{128,192},{193,1},{1,65},{65,129},{129,193... | collective-permute-start | bytes 1179656 | tf_op jit(solution)/shard_map/ppermute | solution.py:13
  502.2 11.5 %copy-start.1 = (bf16[1,96,2048]{2,1,0:T(8,128)(2,1)S(1)}, bf16[1,96,2048]{2,1,0:T(8,128)(2,1)}, u32[]{:S(2)}) copy-start(bf16[1,96,2048]{2,1,0:T(8,128)(2,1)} %param.13) | copy-start | bytes 1179652

commit v2 on v1

--- a/solution.py
+++ b/solution.py
@@ -1,7 +1,13 @@
+import functools
+
 import jax
 import jax.numpy as jnp
 from jax import lax
+from jax.experimental import pallas as pl
+from jax.experimental.pallas import tpu as pltpu
 from jax.sharding import PartitionSpec as P
+
+MESH = pl.DeviceIdType.MESH
 
 EXPERTS = 32
 MOST = 26
@@ -17,6 +23,89 @@
     return lax.ppermute(block, "dp", [(0, 1), (1, 0)])
 
 
+def dispatch_kernel(n, *refs):
+    sends, swaps_out, recvs, swaps_in = refs[0:3], refs[3:6], refs[6:9], refs[9:12]
+    send_sems, recv_sems, w_send, w_recv, local_sems = refs[12:]
+    me = lax.axis_index("expert")
+    other = 1 - lax.axis_index("dp")
+
+    barrier = pltpu.get_barrier_semaphore()
+
+    def greet(o, carry):
+        pl.semaphore_signal(barrier, 1, device_id={"expert": lax.rem(me + o, n)}, device_id_type=MESH)
+        return carry
+
+    lax.fori_loop(1, n, greet, 0)
+    pl.semaphore_signal(barrier, 1, device_id={"dp": other}, device_id_type=MESH)
+    pl.semaphore_wait(barrier, n)
+
+    def copy_of(a, o):
+        target = lax.rem(me + o, n)
+        return pltpu.make_async_remote_copy(
+            src_ref=sends[a].at[target],
+            dst_ref=recvs[a].at[me],
+            send_sem=send_sems.at[a, o],
+            recv_sem=recv_sems.at[a, o],
+            device_id={"expert": target},
+            device_id_type=MESH,
+        )
+
+    swaps = [
+        pltpu.make_async_remote_copy(
+            src_ref=swaps_out[i],
+            dst_ref=swaps_in[i],
+            send_sem=w_send.at[i],
+            recv_sem=w_recv.at[i],
+            device_id={"dp": other},
+            device_id_type=MESH,
+        )
+        for i in range(3)
+    ]
+    locals_ = [pltpu.make_async_copy(sends[a].at[me], recvs[a].at[me], local_sems.at[a]) for a in range(3)]
+    for a in range(3):
+        locals_[a].start()
+
+        def start(o, carry, a=a):
+            copy_of(a, o).start()
+            return carry
+
+        lax.fori_loop(1, n, start, 0)
+        if a == 0:
+            for swap in swaps:
+                swap.start()
+    for a in range(3):
+
+        def finish(o, carry, a=a):
+            copy_of(a, o).wait()
+            return carry
+
+        lax.fori_loop(1, n, finish, 0)
+        locals_[a].wait()
+    for swap in swaps:
+        swap.wait()
+
+
+def dispatch(sends, swaps_out):
+    n = sends[0].shape[0]
+    anywhere = pl.BlockSpec(memory_space=pl.ANY)
+    shapes = [jax.ShapeDtypeStruct(x.shape, x.dtype) for x in (*sends, *swaps_out)]
+    outs = pl.pallas_call(
+        functools.partial(dispatch_kernel, n),
+        out_shape=shapes,
+        in_specs=[anywhere] * 6,
+        out_specs=[anywhere] * 6,
+        scratch_shapes=[
+            pltpu.SemaphoreType.DMA((3, n)),
+            pltpu.SemaphoreType.DMA((3, n)),
+            pltpu.SemaphoreType.DMA((3,)),
+            pltpu.SemaphoreType.DMA((3,)),
+            pltpu.SemaphoreType.DMA((3,)),
+        ],
+        compiler_params=pltpu.CompilerParams(collective_id=0, has_side_effects=True),
+    )(*sends, *swaps_out)
+    return outs[0:3], outs[3:6]
+
+
 def slot_ranks(routes):
     flat_routes = routes.reshape(-1)
     onehot_table = (flat_routes[:, None] == jnp.arange(EXPERTS, dtype=jnp.int32)[None, :]).astype(
@@ -31,9 +120,17 @@
     return counted / jnp.sum(counted, -1, keepdims=True)
 
 
-def packed_rows(rows, positions, groups):
-    filled = jnp.zeros((EXPERTS * MOST, rows.shape[-1]), rows.dtype).at[positions].set(rows)
-    return filled.reshape(groups, EXPERTS // groups, MOST, rows.shape[-1])
+def slot_table(positions, choices_per):
+    slots = jnp.arange(EXPERTS * MOST, dtype=jnp.int32)
+    return slots[:, None, None] == positions.reshape(-1, choices_per)[None, :, :]
+
+
+def packed_rows(rows, table, scale=None):
+    chosen = jnp.any(table, -1)
+    picked = jnp.dot(chosen.astype(rows.dtype), rows, preferred_element_type=jnp.float32)
+    if scale is not None:
+        picked = picked * jnp.sum(jnp.where(table, scale[None], 0.0), (1, 2))[:, None]
+    return picked.astype(rows.dtype).reshape(EXPERTS, MOST, rows.shape[-1])
 
 
 def handoff(value, direction):
@@ -96,16 +193,6 @@
     gate_half = w_gate[0]
     up_half = w_up[0]
     down_half = w_down[0]
-    down_recv, gate_recv, up_recv = swapped(
-        (
-            lax.dynamic_slice_in_dim(down_half, theirs, half, 2),
-            lax.dynamic_slice_in_dim(gate_half, theirs, half, 1),
-            lax.dynamic_slice_in_dim(up_half, theirs, half, 1),
-        )
-    )
-    down_mine = jnp.concatenate([lax.dynamic_slice_in_dim(down_half, mine, half, 2), down_recv], 1)
-    gate_mine = jnp.concatenate([lax.dynamic_slice_in_dim(gate_half, mine, half, 1), gate_recv], 2)
-    up_mine = jnp.concatenate([lax.dynamic_slice_in_dim(up_half, mine, half, 1), up_recv], 2)
 
     fwd_flat, fwd_rank = slot_ranks(fwd_routes[0])
     back_flat, back_rank = slot_ranks(bwd_routes[0])
@@ -114,15 +201,24 @@
     mixing = combine_weights(fwd_numer[0])
     back_mixing = combine_weights(bwd_numer[0])
     unit_weights = jnp.ones_like(back_mixing)
-    scaled_grad = (back_mixing[:, :, None] * grad_in.astype(jnp.float32)[:, None, :]).astype(
-        jnp.bfloat16
-    )
-    send_inputs = packed_rows(jnp.repeat(inputs, choices_per, 0), fwd_positions, groups)
-    send_saved = packed_rows(jnp.repeat(saved, choices_per, 0), back_positions, groups)
-    send_grad = packed_rows(scaled_grad.reshape(-1, model_width), back_positions, groups)
-    recv_inputs = lax.all_to_all(send_inputs, "expert", split_axis=0, concat_axis=0, tiled=True)
-    recv_saved = lax.all_to_all(send_saved, "expert", split_axis=0, concat_axis=0, tiled=True)
-    recv_grad = lax.all_to_all(send_grad, "expert", split_axis=0, concat_axis=0, tiled=True)
+    fwd_table = slot_table(fwd_positions, choices_per)
+    back_table = slot_table(back_positions, choices_per)
+    send_inputs = packed_rows(inputs, fwd_table)
+    send_saved = packed_rows(saved, back_table)
+    send_grad = packed_rows(grad_in, back_table, back_mixing)
+    received, swapped_in = dispatch(
+        (send_inputs, send_saved, send_grad),
+        (
+            lax.dynamic_slice_in_dim(down_half[0], theirs, half, 1),
+            lax.dynamic_slice_in_dim(gate_half[0], theirs, half, 0),
+            lax.dynamic_slice_in_dim(up_half[0], theirs, half, 0),
+        ),
+    )
+    recv_inputs, recv_saved, recv_grad = (x.reshape(groups, 1, MOST, model_width) for x in received)
+    down_recv, gate_recv, up_recv = (x[None] for x in swapped_in)
+    down_mine = jnp.concatenate([lax.dynamic_slice_in_dim(down_half, mine, half, 2), down_recv], 1)
+    gate_mine = jnp.concatenate([lax.dynamic_slice_in_dim(gate_half, mine, half, 1), gate_recv], 2)
+    up_mine = jnp.concatenate([lax.dynamic_slice_in_dim(up_half, mine, half, 1), up_recv], 2)
 
     gate_value, up_value = project(recv_inputs, gate_half, up_half)
     hidden = (jax.nn.silu(gate_value) * up_value).astype(jnp.bfloat16)

time: 521 us -> 547 us (1.050)
  Pallas kernels: 0 us -> 306 us
  waiting for transfers between devices: 303 us -> 86.9 us
  starting transfers between devices: 57.5 us -> 17.1 us
  other arithmetic: 24.4 us -> 14.5 us
  local copies, waits for them, and re-layouts: 57.6 us -> 48.5 us
    pallas_call x0 -> x1, Pallas kernels: none -> 306 us  [dispatch(): pl.pallas_call(functools.partial(dispatch_kernel, n), out_shape=shapes, i...]
    all_to_all x3 -> x0, waiting for transfers between devices: 160 us -> none  [the longest x1 80.2 us: local(): lax.all_to_all(send_saved, 'expert', split_axis=0, concat_axis=0, tiled=T...]
    ppermute x6 -> x3, waiting for transfers between devices: 127 us -> 56.1 us  [swapped(): return lax.ppermute(block, 'dp', [(0, 1), (1, 0)])]
    all_to_all x3 -> x0, starting transfers between devices: 25.5 us -> none  [the longest x1 10.5 us: local(): lax.all_to_all(send_grad, 'expert', split_axis=0, concat_axis=0, tiled=True)]
    scatter x2 -> x0, local copies, waits for them, and re-layouts: 18 us -> none  [packed_rows(): jnp.zeros((EXPERTS * MOST, rows.shape[-1]), rows.dtype).at[positions]]
    scatter x1 -> x0, other arithmetic: 12.6 us -> none  [packed_rows(): jnp.zeros((EXPERTS * MOST, rows.shape[-1]), rows.dtype).at[positions]]
    all_to_all x1, waiting for transfers between devices: 11.7 us -> 20.8 us  [local(): lax.all_to_all(out_part, 'expert', split_axis=0, concat_axis=0, tiled=True)]
    dot_general x0 -> x3, matrix products: none -> 8.46 us  [packed_rows(): jnp.dot(chosen.astype(rows.dtype), rows, preferred_element_type=jnp.float32)]
  transfers between devices with their start and end apart: 13 -> 7, of which waited for: 10 -> 6; matrix products, arithmetic and copies ran while one was open for 19% -> 9% of each run, Pallas kernels for 0% -> 0%
where the time goes in v2:
time: 547 us; the launch traced here: 541 us
  Pallas kernels  306 us (56%)
  waiting for transfers between devices  86.9 us (16%)
  local copies, waits for them, and re-layouts  48.5 us (9%)
  matrix products  45.9 us (8%)
  blocking collectives  20.4 us (4%)
  starting transfers between devices  17.1 us (3%)
  other arithmetic  14.5 us (3%)
    pallas_call x1, Pallas kernels, dispatch(): pl.pallas_call(functools.partial(dispatch_kernel, n), out_shape=shapes, i...  306 us
    ppermute x3, waiting for transfers between devices, swapped(): return lax.ppermute(block, 'dp', [(0, 1), (1, 0)])  56.1 us
    all_to_all x1, waiting for transfers between devices, local(): lax.all_to_all(out_part, 'expert', split_axis=0, concat_axis=0, tiled=True)  20.8 us
    reshape x3, local copies, waits for them, and re-layouts, packed_rows(): return picked.astype(rows.dtype).reshape(EXPERTS, MOST, rows.shape[-1])  14.8 us
    all_gather x1, blocking collectives, local(): input_grad = lax.all_gather(input_grad, 'dp', axis=1, tiled=True)  11.3 us
  transfers between devices with their start and end apart: 7, of which 6 were waited for; matrix products, arithmetic and copies ran while one was open for 9% of the time, Pallas kernels for 0%

profile of v2, /device:TPU:8, one launch (start us, length us, event | category | flops | bytes accessed | tf_op | source)
XLA Modules:
  0.0 540.9 jit_solution(3991413959327205916)
XLA Ops:
  4.2 1.7 reduce-window.16
  7.0 0.9 fusion.1
  8.4 1.7 reduce-window.14
  11.2 0.9 fusion.2
  12.2 2.8 convolution_convert_fusion.1
  15.0 4.9 reshape.248.refs_0_
  19.9 2.8 multiply_convert_fusion
  22.7 4.9 reshape.251.refs_2_
  27.6 2.8 convolution_convert_fusion
  30.5 5.0 reshape.250.refs_1_
  35.4 1.3 dynamic-slice_bitcast_fusion.5
  37.9 1.7 dynamic-slice_bitcast_fusion
  39.6 306.2 %shard_map.137 = (bf16[32,26,2048]{2,1,0:T(8,128)(2,1)}, bf16[32,26,2048]{2,1,0:T(8,128)(2,1)}, bf16[32,26,2048]{2,1,0:T(8,128)(2,1)}, bf16[384,1024]{1,0:T(8,12...) custom-call(bf16[32,26,2048]{2,1,0:T(8,128)(2,1)} %reshape.248.refs_0_, ...), custom_call_target="tpu_custom_call" | custom-call | tf_op jit(solution)/shard_map/pallas_call | solution.py:92
  345.8 4.7 fusion.25
  350.5 2.3 fusion.29
  353.3 2.8 fusion.20
  356.6 3.6 collective-permute-start.2
  360.2 15.0 %collective-permute-done.3 = bf16[32,1,26,384]{3,0,2,1:T(8,128)(2,1)S(1)} collective-permute-done((bf16[32,1,26,384]{3,0,2,1:T(8,128)(2,1)S(1)}, bf16[32,1,26,384]{3,0,2,1:T(8,128)(2,1)S(1)}, u32[]{:S(2)}, u32[]{:S(2)}) %collective-permute-start.3) | collective-permute-done | bytes 639008 | tf_op jit(solution)/shard_map/ppermute | solution.py:23
  375.7 11.9 %collective-permute-done.2 = bf16[32,1,26,384]{3,0,2,1:T(8,128)(2,1)S(1)} collective-permute-done((bf16[32,1,26,384]{3,0,2,1:T(8,128)(2,1)S(1)}, bf16[32,1,26,384]{3,0,2,1:T(8,128)(2,1)S(1)}, u32[]{:S(2)}, u32[]{:S(2)}) %collective-permute-start.2) | collective-permute-done | bytes 639008 | tf_op jit(solution)/shard_map/ppermute | solution.py:23
  388.0 0.9 copy-done.17
  389.1 1.7 fusion.8
  390.9 1.7 fusion.37
  392.6 2.4 copy.105
  395.0 8.0 %all-to-all-start.1 = ((bf16[32,1,26,1024]{3,2,1,0:T(8,128)(2,1)}), bf16[32,1,26,1024]{3,2,1,0:T(8,128)(2,1)S(1)}, u32[]{:S(2)}, u32[]{:S(2)}) async-start(bf16[32,1,26,1024]{3,2,1,0:T(8,128)(2,1)} %copy.105), calls=%async_computation.1 | async-start | bytes 4194304 | tf_op jit(solution)/shard_map/all_to_all | solution.py:244
  403.0 5.1 fusion.27
  408.2 2.4 fusion.15
  411.5 1.0 copy.95
  413.0 29.3 %collective-permute-done = bf16[32,1,26,384]{3,0,2,1:T(8,128)(2,1)} collective-permute-done((bf16[32,1,26,384]{3,0,2,1:T(8,128)(2,1)}, bf16[32,1,26,384]{3,0,2,1:T(8,128)(2,1)}, u32[]{:S(2)}, u32[]{:S(2)}) %collective-permute-start) | collective-permute-done | bytes 639008 | tf_op jit(solution)/shard_map/ppermute | solution.py:23
  442.3 1.3 copy.96
  443.9 0.9 copy-done.15
  445.0 1.7 fusion.36
  446.7 2.3 copy.98
  448.9 4.2 all-to-all-done.1
  453.1 1.4 copy-done.2
  454.5 5.4 all-to-all-start
  459.9 6.1 %fusion.4 = bf16[1,1,2048,384]{3,2,1,0:T(8,128)(2,1)} fusion(bf16[32,26,2048]{2,1,0:T(8,128)(2,1)} %get-tuple-element.15, bf16[32,1,26,384]{3,2,0,1:T(8,128)(2,1)} %copy-done.3), kind=kOutput, calls=%fused_computation.18 | convolution fusion | flops 1309409280 | bytes 5619712 | tf_op jit(solution)/shard_map/semd,semf->edf/dot_general | solution.py:164
  466.0 3.1 fusion.5
  469.1 2.5 reshape.262
  471.7 3.6 gather_fusion.1
  475.2 2.5 convert_reduce_fusion
  477.8 11.3 %all_gather.7 = bf16[96,2048]{1,0:T(8,128)(2,1)} all-gather(bf16[96,1024]{1,0:T(8,128)(2,1)S(1)} %fusion.47), channel_id=1, replica_groups=mesh['section'=4,'expert'=32,'dp'=2] {'dp'}, dimensions={1}, use_global_device_ids=true | all-gather | bytes 589824 | tf_op jit(solution)/shard_map/all_gather | solution.py:250
  489.2 20.8 %all-to-all-done = bf16[32,1,26,1024]{3,2,1,0:T(8,128)(2,1)} async-done(((bf16[32,1,26,1024]{3,2,1,0:T(8,128)(2,1)}), bf16[32,1,26,1024]{3,2,1,0:T(8,128)(2,1)}, u32[]{:S(2)}, u32[]{:S(2)}) %all-to-all-start) | async-done | bytes 1703968 | tf_op jit(solution)/shard_map/all_to_all | solution.py:243
  510.0 2.5 reshape.256
  512.6 3.6 gather_fusion
  516.1 2.5 fusion
  518.7 9.1 %all_gather.6 = bf16[96,2048]{1,0:T(8,128)(2,1)S(1)} all-gather(bf16[96,1024]{1,0:T(8,128)(2,1)S(1)} %fusion.48), channel_id=1, replica_groups=mesh['section'=4,'expert'=32,'dp'=2] {'dp'}, dimensions={1}, use_global_device_ids=true | all-gather | bytes 589824 | tf_op jit(solution)/shard_map/all_gather | solution.py:249
  527.7 5.8 %fusion.3 = bf16[1,1,2048,384]{3,2,1,0:T(8,128)(2,1)} fusion(bf16[32,26,2048]{2,1,0:T(8,128)(2,1)} %get-tuple-element.15, bf16[32,1,26,384]{3,2,0,1:T(8,128)(2,1)S(1)} %get-tuple-element.18), kind=kOutput, calls=%fused_computation.17 | convolution fusion | flops 1309409280 | bytes 5619712 | tf_op jit(solution)/shard_map/semd,semf->edf/dot_general | solution.py:161
  533.5 5.7 %collective-permute-done.1 = bf16[1,96,2048]{2,1,0:T(8,128)(2,1)S(1)} collective-permute-done((bf16[1,96,2048]{2,1,0:T(8,128)(2,1)S(1)}, bf16[1,96,2048]{2,1,0:T(8,128)(2,1)S(1)}, u32[]{:S(2)}, u32[]{:S(2)}) %collective-permute-start.1) | collective-permute-done | bytes 393248 | tf_op jit(solution)/shard_map/ppermute | solution.py:19
  (108 shorter events, 12.7 us)
Async XLA Ops:
  0.6 27.0 %copy-start = (bf16[1,96,2048]{2,1,0:T(8,128)(2,1)S(1)}, bf16[1,96,2048]{2,1,0:T(8,128)(2,1)}, u32[]{:S(2)}) copy-start(bf16[1,96,2048]{2,1,0:T(8,128)(2,1)} %param.13) | copy-start | bytes 1179652
  0.6 11.5 %copy-start.13 = (bf16[1,96,2048]{2,1,0:T(8,128)(2,1)S(1)}, bf16[1,96,2048]{2,1,0:T(8,128)(2,1)}, u32[]{:S(2)}) copy-start(bf16[1,96,2048]{2,1,0:T(8,128)(2,1)} %param.10) | copy-start | bytes 1179652
  15.0 4.9 copy-start.11
  30.5 5.0 copy-start.6
  35.4 2.0 copy-start.7
  35.4 2.4 copy-start.8
  345.8 4.7 copy-start.9
  345.8 4.7 copy-start.21
  350.5 2.4 copy-start.28
  350.5 2.8 copy-start.22
  352.9 3.2 copy-start.30
  356.1 19.3 %copy-start.3 = (bf16[32,1,26,384]{3,2,0,1:T(8,128)(2,1)}, bf16[32,1,26,384]{3,2,0,1:T(8,128)(2,1)S(1)}, u32[]{:S(2)}) copy-start(bf16[32,1,26,384]{3,2,0,1:T(8,128)(2,1)S(1)} %get-tuple-element.17) | copy-start | bytes 1916932
  356.3 18.9 %collective-permute-start.3 = (bf16[32,1,26,384]{3,0,2,1:T(8,128)(2,1)S(1)}, bf16[32,1,26,384]{3,0,2,1:T(8,128)(2,1)S(1)}, u32[]{:S(2)}, u32[]{:S(2)}) collective-permute-start(bf16[32,1,26,384]{3,0,2,1:T(8,128)(2,1)S(1)} %copy.102), channel_id=1, source_target_pairs={{0,1},{1,0},{2,3},{3,2},{4,5},{5,4},{6,7},{7,6},{8,9},{9,8},{10,11... | collective-permute-start | bytes 1916936 | tf_op jit(solution)/shard_map/ppermute | solution.py:23
  356.6 30.9 %collective-permute-start.2 = (bf16[32,1,26,384]{3,0,2,1:T(8,128)(2,1)S(1)}, bf16[32,1,26,384]{3,0,2,1:T(8,128)(2,1)S(1)}, u32[]{:S(2)}, u32[]{:S(2)}) collective-permute-start(bf16[32,1,26,384]{3,0,2,1:T(8,128)(2,1)S(1)} %copy.99), channel_id=1, source_target_pairs={{0,1},{1,0},{2,3},{3,2},{4,5},{5,4},{6,7},{7,6},{8,9},{9,8},{10,11... | collective-permute-start | bytes 1916936 | tf_op jit(solution)/shard_map/ppermute | solution.py:23
  387.8 1.1 copy-start.17
  387.8 1.4 copy-start.27
  389.1 1.7 copy-start.16
  389.1 1.7 copy-start.26
  395.0 58.2 %all-to-all-start.1 = ((bf16[32,1,26,1024]{3,2,1,0:T(8,128)(2,1)}), bf16[32,1,26,1024]{3,2,1,0:T(8,128)(2,1)S(1)}, u32[]{:S(2)}, u32[]{:S(2)}) async-start(bf16[32,1,26,1024]{3,2,1,0:T(8,128)(2,1)} %copy.105), calls=%async_computation.1 | async-start | bytes 4194304 | tf_op jit(solution)/shard_map/all_to_all | solution.py:244
  403.0 5.2 copy-start.10
  403.0 5.2 copy-start.24
  408.2 4.4 copy-start.20
  408.2 4.5 copy-start.18
  410.6 0.9 copy-start.4
  411.5 1.3 copy-start.19
  412.6 29.7 %collective-permute-start = (bf16[32,1,26,384]{3,0,2,1:T(8,128)(2,1)}, bf16[32,1,26,384]{3,0,2,1:T(8,128)(2,1)}, u32[]{:S(2)}, u32[]{:S(2)}) collective-permute-start(bf16[32,1,26,384]{3,0,2,1:T(8,128)(2,1)} %copy.95), channel_id=1, source_target_pairs={{0,1},{1,0},{2,3},{3,2},{4,5},{5,4},{6,7},{7,6},{8,9},{9,8},{10,11... | collective-permute-start | bytes 1916936 | tf_op jit(solution)/shard_map/ppermute | solution.py:23
  412.9 30.7 %copy-start.5 = (bf16[32,1,26,384]{3,2,0,1:T(8,128)(2,1)S(1)}, bf16[32,1,26,384]{3,2,0,1:T(8,128)(2,1)}, u32[]{:S(2)}) copy-start(bf16[32,1,26,384]{3,2,0,1:T(8,128)(2,1)} %copy-done.4) | copy-start | bytes 1916932
  443.6 1.1 copy-start.15
  443.6 1.4 copy-start.25
  453.1 1.4 copy-start.2
  454.5 55.5 %all-to-all-start = ((bf16[32,1,26,1024]{3,2,1,0:T(8,128)(2,1)}), bf16[32,1,26,1024]{3,2,1,0:T(8,128)(2,1)}, u32[]{:S(2)}, u32[]{:S(2)}) async-start(bf16[32,1,26,1024]{3,2,1,0:T(8,128)(2,1)} %copy.98), calls=%async_computation | async-start | bytes 4194304 | tf_op jit(solution)/shard_map/all_to_all | solution.py:243
  459.9 6.1 %copy-start.23 = (bf16[32,26,2048]{2,1,0:T(8,128)(2,1)S(1)}, bf16[32,26,2048]{2,1,0:T(8,128)(2,1)}, u32[]{:S(2)}) copy-start(bf16[32,26,2048]{2,1,0:T(8,128)(2,1)} %get-tuple-element.14) | copy-start | bytes 10223620
  459.9 6.1 %copy-start.29 = (f32[32,26,384]{2,1,0:T(8,128)S(1)}, f32[32,26,384]{2,1,0:T(8,128)}, u32[]{:S(2)}) copy-start(f32[32,26,384]{2,1,0:T(8,128)} %copy-done.28) | copy-start | bytes 3833860
  459.9 6.1 %copy-start.31 = (f32[32,26,384]{2,1,0:T(8,128)S(1)}, f32[32,26,384]{2,1,0:T(8,128)}, u32[]{:S(2)}) copy-start(f32[32,26,384]{2,1,0:T(8,128)} %copy-done.30) | copy-start | bytes 3833860
  475.2 2.5 copy-start.12
  489.2 44.3 %collective-permute-start.4 = (bf16[1,96,2048]{2,1,0:T(8,128)(2,1)}, bf16[1,96,2048]{2,1,0:T(8,128)(2,1)S(1)}, u32[]{:S(2)}, u32[]{:S(2)}) collective-permute-start(bf16[1,96,2048]{2,1,0:T(8,128)(2,1)} %bitcast.65), channel_id=1, source_target_pairs={{64,0},{128,64},{192,128},{0,192},{65,1},{129,65},{193,129},{1,193... | collective-permute-start | bytes 1179656 | tf_op jit(solution)/shard_map/ppermute | solution.py:19
  516.1 2.5 copy-start.14
  527.7 11.5 %collective-permute-start.1 = (bf16[1,96,2048]{2,1,0:T(8,128)(2,1)S(1)}, bf16[1,96,2048]{2,1,0:T(8,128)(2,1)S(1)}, u32[]{:S(2)}, u32[]{:S(2)}) collective-permute-start(bf16[1,96,2048]{2,1,0:T(8,128)(2,1)S(1)} %bitcast.256), channel_id=1, source_target_pairs={{192,0},{0,64},{64,128},{128,192},{193,1},{1,65},{65,129},{129,193... | collective-permute-start | bytes 1179656 | tf_op jit(solution)/shard_map/ppermute | solution.py:19
  527.7 12.9 %copy-start.1 = (bf16[1,96,2048]{2,1,0:T(8,128)(2,1)S(1)}, bf16[1,96,2048]{2,1,0:T(8,128)(2,1)}, u32[]{:S(2)}) copy-start(bf16[1,96,2048]{2,1,0:T(8,128)(2,1)} %param.13) | copy-start | bytes 1179652

commit v3 on v2

--- a/solution.py
+++ b/solution.py
@@ -23,9 +23,12 @@
     return lax.ppermute(block, "dp", [(0, 1), (1, 0)])
 
 
-def dispatch_kernel(n, *refs):
-    sends, swaps_out, recvs, swaps_in = refs[0:3], refs[3:6], refs[6:9], refs[9:12]
-    send_sems, recv_sems, w_send, w_recv, local_sems = refs[12:]
+def exchange_kernel(n, spread, swapped_count, *refs):
+    sends = refs[0:spread]
+    swaps_out = refs[spread:spread + swapped_count]
+    recvs = refs[spread + swapped_count:2 * spread + swapped_count]
+    swaps_in = refs[2 * spread + swapped_count:2 * (spread + swapped_count)]
+    send_sems, recv_sems, w_send, w_recv, local_sems = refs[2 * (spread + swapped_count):]
     me = lax.axis_index("expert")
     other = 1 - lax.axis_index("dp")
 
@@ -36,8 +39,9 @@
         return carry
 
     lax.fori_loop(1, n, greet, 0)
-    pl.semaphore_signal(barrier, 1, device_id={"dp": other}, device_id_type=MESH)
-    pl.semaphore_wait(barrier, n)
+    if swapped_count:
+        pl.semaphore_signal(barrier, 1, device_id={"dp": other}, device_id_type=MESH)
+    pl.semaphore_wait(barrier, n if swapped_count else n - 1)
 
     def copy_of(a, o):
         target = lax.rem(me + o, n)
@@ -59,10 +63,14 @@
             device_id={"dp": other},
             device_id_type=MESH,
         )
-        for i in range(3)
+        for i in range(swapped_count)
     ]
-    locals_ = [pltpu.make_async_copy(sends[a].at[me], recvs[a].at[me], local_sems.at[a]) for a in range(3)]
-    for a in range(3):
+    for swap in swaps:
+        swap.start()
+    locals_ = [
+        pltpu.make_async_copy(sends[a].at[me], recvs[a].at[me], local_sems.at[a]) for a in range(spread)
+    ]
+    for a in range(spread):
         locals_[a].start()
 
         def start(o, carry, a=a):
@@ -70,10 +78,7 @@
             return carry
 
         lax.fori_loop(1, n, start, 0)
-        if a == 0:
-            for swap in swaps:
-                swap.start()
-    for a in range(3):
+    for a in range(spread):
 
         def finish(o, carry, a=a):
             copy_of(a, o).wait()
@@ -85,25 +90,27 @@
         swap.wait()
 
 
-def dispatch(sends, swaps_out):
+def exchange(sends, swaps_out, collective_id):
     n = sends[0].shape[0]
     anywhere = pl.BlockSpec(memory_space=pl.ANY)
-    shapes = [jax.ShapeDtypeStruct(x.shape, x.dtype) for x in (*sends, *swaps_out)]
+    arrays = (*sends, *swaps_out)
+    moved = sum(x.size * x.dtype.itemsize for x in arrays)
     outs = pl.pallas_call(
-        functools.partial(dispatch_kernel, n),
-        out_shape=shapes,
-        in_specs=[anywhere] * 6,
-        out_specs=[anywhere] * 6,
+        functools.partial(exchange_kernel, n, len(sends), len(swaps_out)),
+        out_shape=[jax.ShapeDtypeStruct(x.shape, x.dtype) for x in arrays],
+        in_specs=[anywhere] * len(arrays),
+        out_specs=[anywhere] * len(arrays),
         scratch_shapes=[
-            pltpu.SemaphoreType.DMA((3, n)),
-            pltpu.SemaphoreType.DMA((3, n)),
-            pltpu.SemaphoreType.DMA((3,)),
-            pltpu.SemaphoreType.DMA((3,)),
-            pltpu.SemaphoreType.DMA((3,)),
+            pltpu.SemaphoreType.DMA((len(sends), n)),
+            pltpu.SemaphoreType.DMA((len(sends), n)),
+            pltpu.SemaphoreType.DMA((max(1, len(swaps_out)),)),
+            pltpu.SemaphoreType.DMA((max(1, len(swaps_out)),)),
+            pltpu.SemaphoreType.DMA((len(sends),)),
         ],
-        compiler_params=pltpu.CompilerParams(collective_id=0, has_side_effects=True),
-    )(*sends, *swaps_out)
-    return outs[0:3], outs[3:6]
+        compiler_params=pltpu.CompilerParams(collective_id=collective_id, has_side_effects=True),
+        cost_estimate=pl.CostEstimate(flops=0, bytes_accessed=2 * moved, transcendentals=0),
+    )(*arrays)
+    return outs[: len(sends)], outs[len(sends):]
 
 
 def slot_ranks(routes):
@@ -126,11 +133,11 @@
 
 
 def packed_rows(rows, table, scale=None):
-    chosen = jnp.any(table, -1)
-    picked = jnp.dot(chosen.astype(rows.dtype), rows, preferred_element_type=jnp.float32)
+    chosen = jnp.any(table, -1).reshape(EXPERTS, MOST, -1)
+    picked = jnp.einsum("ecm,md->ecd", chosen.astype(rows.dtype), rows, preferred_element_type=jnp.float32)
     if scale is not None:
-        picked = picked * jnp.sum(jnp.where(table, scale[None], 0.0), (1, 2))[:, None]
-    return picked.astype(rows.dtype).reshape(EXPERTS, MOST, rows.shape[-1])
+        picked = picked * jnp.sum(jnp.where(table, scale[None], 0.0), (1, 2)).reshape(EXPERTS, MOST, 1)
+    return picked.astype(rows.dtype)
 
 
 def handoff(value, direction):
@@ -206,33 +213,28 @@
     send_inputs = packed_rows(inputs, fwd_table)
     send_saved = packed_rows(saved, back_table)
     send_grad = packed_rows(grad_in, back_table, back_mixing)
-    received, swapped_in = dispatch(
-        (send_inputs, send_saved, send_grad),
+    (recv_saved, recv_grad), swapped_in = exchange(
+        (send_saved, send_grad),
         (
             lax.dynamic_slice_in_dim(down_half[0], theirs, half, 1),
             lax.dynamic_slice_in_dim(gate_half[0], theirs, half, 0),
             lax.dynamic_slice_in_dim(up_half[0], theirs, half, 0),
         ),
-    )
-    recv_inputs, recv_saved, recv_grad = (x.reshape(groups, 1, MOST, model_width) for x in received)
+        0,
+    )
+    recv_saved, recv_grad = (x.reshape(groups, 1, MOST, model_width) for x in (recv_saved, recv_grad))
     down_recv, gate_recv, up_recv = (x[None] for x in swapped_in)
     down_mine = jnp.concatenate([lax.dynamic_slice_in_dim(down_half, mine, half, 2), down_recv], 1)
     gate_mine = jnp.concatenate([lax.dynamic_slice_in_dim(gate_half, mine, half, 1), gate_recv], 2)
     up_mine = jnp.concatenate([lax.dynamic_slice_in_dim(up_half, mine, half, 1), up_recv], 2)
 
-    gate_value, up_value = project(recv_inputs, gate_half, up_half)
-    hidden = (jax.nn.silu(gate_value) * up_value).astype(jnp.bfloat16)
-    hidden_all = jnp.concatenate([hidden, swapped(hidden)], -1)
-    out_part = jnp.einsum(
-        "semf,efd->semd", hidden_all, down_mine, preferred_element_type=jnp.float32
-    ).astype(jnp.bfloat16)
-
     back_gate, back_up = project(recv_saved, gate_half, up_half)
     back_hidden, gate_grad, up_grad = local_backward(back_gate, back_up, recv_grad, down_half)
     gate_term, up_term, down_term = weight_terms(
         recv_saved, recv_grad, back_hidden, gate_grad, up_grad
     )
-    gate_other, up_other = swapped((gate_grad, up_grad))
+    (recv_inputs,), (gate_other, up_other) = exchange((send_inputs,), (gate_grad, up_grad), 1)
+    recv_inputs = recv_inputs.reshape(groups, 1, MOST, model_width)
     gate_all = jnp.concatenate([gate_grad, gate_other], -1)
     up_all = jnp.concatenate([up_grad, up_other], -1)
     grad_part = (
@@ -240,8 +242,14 @@
         + jnp.einsum("semf,edf->semd", up_all, up_mine, preferred_element_type=jnp.float32)
     ).astype(jnp.bfloat16)
 
-    back_out = lax.all_to_all(out_part, "expert", split_axis=0, concat_axis=0, tiled=True)
-    back_grad = lax.all_to_all(grad_part, "expert", split_axis=0, concat_axis=0, tiled=True)
+    gate_value, up_value = project(recv_inputs, gate_half, up_half)
+    hidden = (jax.nn.silu(gate_value) * up_value).astype(jnp.bfloat16)
+    (back_grad,), (hidden_other,) = exchange((grad_part.reshape(groups, MOST, half),), (hidden,), 2)
+    hidden_all = jnp.concatenate([hidden, hidden_other], -1)
+    out_part = jnp.einsum(
+        "semf,efd->semd", hidden_all, down_mine, preferred_element_type=jnp.float32
+    ).astype(jnp.bfloat16)
+    (back_out,), _ = exchange((out_part.reshape(groups, MOST, half),), (), 3)
     inputs_part = lax.dynamic_slice_in_dim(inputs, mine, half, 1)
     grad_in_part = lax.dynamic_slice_in_dim(grad_in, mine, half, 1)
     layer_out = mix_rows(inputs_part, back_out, fwd_positions, mixing, choices_per)

time: 547 us -> 557 us (1.018)
  Pallas kernels: 306 us -> 416 us
  waiting for transfers between devices: 86.9 us -> 0.01 us
  starting transfers between devices: 17.1 us -> 3.24 us
  local copies, waits for them, and re-layouts: 48.5 us -> 41 us
  other arithmetic: 14.5 us -> 20.3 us
    pallas_call x1 -> x4, Pallas kernels: 306 us -> 416 us  [exchange(): pl.pallas_call(functools.partial(exchange_kernel, n, len(sends), len(swap...]
    ppermute x3 -> x0, waiting for transfers between devices: 56.1 us -> none  [swapped(): return lax.ppermute(block, 'dp', [(0, 1), (1, 0)])]
    all_to_all x2 -> x0, waiting for transfers between devices: 25.1 us -> none  [the longest x1 20.8 us: local(): lax.all_to_all(out_part, 'expert', split_axis=0, concat_axis=0, tiled=True)]
    all_to_all x2 -> x0, starting transfers between devices: 13.4 us -> none  [the longest x1 8.03 us: local(): lax.all_to_all(grad_part, 'expert', split_axis=0, concat_axis=0, tiled=True)]
    reshape x3 -> x2, local copies, waits for them, and re-layouts: 14.8 us -> 1.72 us  [packed_rows(): chosen = jnp.any(table, -1).reshape(EXPERTS, MOST, -1)]
    ppermute x2, waiting for transfers between devices: 5.69 us -> 0.01 us  [passed_along(): return lax.ppermute(block, axis, route)]
  transfers between devices with their start and end apart: 7 -> 2, of which waited for: 6 -> 0; matrix products, arithmetic and copies ran while one was open for 9% -> 4% of each run, Pallas kernels for 0% -> 0%
where the time goes in v3:
time: 557 us; the launch traced here: 548 us
  Pallas kernels  416 us (75%)
  matrix products  48 us (9%)
  local copies, waits for them, and re-layouts  41 us (7%)
  other arithmetic  20.3 us (4%)
  blocking collectives  18 us (3%)
    pallas_call x4, Pallas kernels, exchange(): pl.pallas_call(functools.partial(exchange_kernel, n, len(sends), len(swap...  416 us
  transfers between devices with their start and end apart: 2, of which 0 were waited for; matrix products, arithmetic and copies ran while one was open for 4% of the time, Pallas kernels for 0%

profile of v3, /device:TPU:8, one launch (start us, length us, event | category | flops | bytes accessed | tf_op | source)
XLA Modules:
  0.0 547.8 jit_solution(1774498987643191310)
XLA Ops:
  0.7 0.8 copy.107
  1.7 1.7 reduce-window.14
  5.1 0.9 fusion.1
  8.4 1.0 convolution_convert_fusion.1
  9.5 3.9 copy.116.refs_0_
  13.4 1.3 dynamic-slice_bitcast_fusion.5
  15.9 1.8 dynamic-slice_bitcast_fusion
  17.6 3.2 multiply_convert_fusion.refs_1_
  20.8 204.3 %shard_map.137 = (bf16[32,26,2048]{2,1,0:T(8,128)(2,1)}, bf16[32,26,2048]{2,1,0:T(8,128)(2,1)}, bf16[384,1024]{1,0:T(8,128)(2,1)}, bf16[1024,384]{1,0:T(8,128)(2,1)}, bf16[1024,384]{1,0:T(8,128)(2,1)}) custom-call(bf16[32,26,2048]{2,1,0:T(8,128)(2,1)} %copy.116.refs_0_, bf16[32,26,2048]{2,1,0:T(8,128)(2,1)} %multiply_convert_fusion.refs_1_, ...), custom_call_target="tpu_custom_call" | custom-call | bytes 18350080 | tf_op jit(solution)/shard_map/pallas_call | solution.py:98
  225.1 5.8 %fusion.19 = f32[32,26,384]{2,1,0:T(8,128)} fusion(bf16[32,26,2048]{2,1,0:T(8,128)(2,1)} %get-tuple-element.17, bf16[1,1,2048,384]{3,2,1,0:T(8,128)(2,1)S(1)} %copy-done.6), kind=kOutput, calls=%fused_computation.42 | convolution fusion | flops 1308622848 | bytes 6258688 | tf_op jit(solution)/shard_map/semd,edf->semf/dot_general | solution.py:148
  231.0 3.5 fusion.29
  235.1 0.9 eq.97
  236.0 0.9 eq.93
  237.6 4.7 reduce-window.16
  242.2 1.1 slice_reduce_fusion
  243.4 1.0 fusion.56
  245.1 1.4 broadcast_multiply_fusion
  246.6 1.6 fusion.2
  248.1 1.7 copy.121
  249.8 1.6 reshape.256
  251.5 1.9 convolution_convert_fusion
  253.5 3.9 copy.123.refs_0_
  257.4 4.0 fusion.34
  261.4 103.0 %shard_map.138 = (bf16[32,26,2048]{2,1,0:T(8,128)(2,1)}, bf16[32,1,26,384]{3,2,1,0:T(8,128)(2,1)}, bf16[32,1,26,384]{3,2,1,0:T(8,128)(2,1)}) custom-call(bf16[32,26,2048]{2,1,0:T(8,128)(2,1)} %copy.123.refs_0_, bf16[32,1,26,384]{3,2,1,0:T(8,128)(2,1)} %get-tuple-element.26.refs_1_, bf16[32,1,26,384]{3,2,1,0:T(8,128)(2,1)} %get-tuple-element.25.refs_2_), custom_call_target="tpu_custom_call" | custom-call | bytes 9371648 | tf_op jit(solution)/shard_map/pallas_call | solution.py:98
  364.4 4.7 fusion.17
  369.1 3.4 fusion.16.refs_1_
  372.7 0.9 copy-done.3
  374.1 0.9 copy-done.21
  375.2 1.7 fusion.9
  377.0 1.7 convolution_add_fusion
  378.7 2.3 copy.148
  381.0 54.3 %shard_map.139 = (bf16[32,26,1024]{2,1,0:T(8,128)(2,1)}, bf16[32,1,26,384]{3,2,1,0:T(8,128)(2,1)}) custom-call(bf16[32,26,1024]{2,1,0:T(8,128)(2,1)} %bitcast.259, bf16[32,1,26,384]{3,2,1,0:T(8,128)(2,1)} %fusion.16.refs_1_), custom_call_target="tpu_custom_call" | custom-call | bytes 4685824 | tf_op jit(solution)/shard_map/pallas_call | solution.py:98
  435.3 4.2 convert_bitcast_fusion.refs_0_
  439.6 54.2 %shard_map.140 = bf16[32,26,1024]{2,1,0:T(8,128)(2,1)} custom-call(bf16[32,26,1024]{2,1,0:T(8,128)(2,1)} %convert_bitcast_fusion.refs_0_), custom_call_target="tpu_custom_call" | custom-call | bytes 3407872 | tf_op jit(solution)/shard_map/pallas_call | solution.py:98
  493.8 2.5 reshape.267
  496.8 3.7 gather_fusion
  500.5 2.5 fusion
  503.1 9.6 %all_gather.6 = bf16[96,2048]{1,0:T(8,128)(2,1)} all-gather(bf16[96,1024]{1,0:T(8,128)(2,1)S(1)} %fusion.50), channel_id=1, replica_groups=mesh['section'=4,'expert'=32,'dp'=2] {'dp'}, dimensions={1}, use_global_device_ids=true | all-gather | bytes 589824 | tf_op jit(solution)/shard_map/all_gather | solution.py:257
  512.7 1.8 collective-permute-start
  514.4 2.5 reshape.268
  517.0 3.6 gather_fusion.1
  520.5 2.6 convert_reduce_fusion
  523.2 8.4 %all_gather.7 = bf16[96,2048]{1,0:T(8,128)(2,1)S(1)} all-gather(bf16[96,1024]{1,0:T(8,128)(2,1)S(1)} %fusion.49), channel_id=1, replica_groups=mesh['section'=4,'expert'=32,'dp'=2] {'dp'}, dimensions={1}, use_global_device_ids=true | all-gather | bytes 589824 | tf_op jit(solution)/shard_map/all_gather | solution.py:258
  531.7 1.5 collective-permute-start.1
  533.1 5.8 %fusion.5 = bf16[1,1,384,2048]{3,2,1,0:T(8,128)(2,1)} fusion(bf16[32,26,2048]{2,1,0:T(8,128)(2,1)} %get-tuple-element.16, f32[32,26,384]{2,1,0:T(8,128)} %fusion.29, f32[32,26,384]{2,1,0:T(8,128)S(1)} %copy-done.36), kind=kOutput, calls=%fused_computation.19 | convolution fusion | flops 1311326208 | bytes 7536640 | tf_op jit(solution)/shard_map/semf,semd->efd/dot_general | solution.py:172
  538.9 3.6 fusion.3
  542.5 3.6 fusion.4
  546.1 0.7 copy.151
  (108 shorter events, 9.7 us)
Async XLA Ops:
  0.6 7.8 %copy-start = (bf16[1,96,2048]{2,1,0:T(8,128)(2,1)S(1)}, bf16[1,96,2048]{2,1,0:T(8,128)(2,1)}, u32[]{:S(2)}) copy-start(bf16[1,96,2048]{2,1,0:T(8,128)(2,1)} %param.13) | copy-start | bytes 1179652
  3.8 0.6 copy-start.24
  6.4 2.0 copy-start.10
  9.5 3.9 copy-start.5
  13.4 2.0 copy-start.6
  13.4 2.4 copy-start.7
  15.9 1.8 copy-start.11
  15.9 1.8 copy-start.14
  225.1 5.8 %copy-start.8 = (bf16[1,1,2048,384]{3,2,1,0:T(8,128)(2,1)S(1)}, bf16[1,1,2048,384]{3,2,1,0:T(8,128)(2,1)}, u32[]{:S(2)}) copy-start(bf16[1,1,2048,384]{3,2,1,0:T(8,128)(2,1)} %param.18) | copy-start | bytes 4718596
  225.1 5.8 %copy-start.28 = (bf16[32,26,2048]{2,1,0:T(8,128)(2,1)S(1)}, bf16[32,26,2048]{2,1,0:T(8,128)(2,1)}, u32[]{:S(2)}) copy-start(bf16[32,26,2048]{2,1,0:T(8,128)(2,1)} %get-tuple-element.17) | copy-start | bytes 10223620
  231.0 3.5 copy-start.27
  234.4 17.1 %copy-start.12 = (bf16[1,96,2048]{2,1,0:T(8,128)(2,1)S(1)}, bf16[1,96,2048]{2,1,0:T(8,128)(2,1)}, u32[]{:S(2)}) copy-start(bf16[1,96,2048]{2,1,0:T(8,128)(2,1)} %param.10) | copy-start | bytes 1179652
  253.4 4.0 copy-start.30
  253.4 3.9 copy-start.35
  253.4 3.9 copy-start.37
  364.4 4.7 copy-start.9
  364.4 4.7 copy-start.31
  369.1 3.4 copy-start.2
  369.1 3.4 copy-start.19
  372.5 1.1 copy-start.3
  372.5 1.4 copy-start.18
  373.9 1.1 copy-start.21
  373.9 1.4 copy-start.34
  375.2 1.7 copy-start.20
  375.2 1.7 copy-start.33
  381.0 54.3 %copy-start.16 = (bf16[1,384,1024]{2,1,0:T(8,128)(2,1)S(1)}, bf16[1,384,1024]{2,1,0:T(8,128)(2,1)}, u32[]{:S(2)}) copy-start(bf16[1,384,1024]{2,1,0:T(8,128)(2,1)} %get-tuple-element.31) | copy-start | bytes 2359300
  381.0 54.3 %copy-start.17 = (bf16[32,1,26,384]{3,2,1,0:T(8,128)(2,1)S(1)}, bf16[32,1,26,384]{3,2,1,0:T(8,128)(2,1)}, u32[]{:S(2)}) copy-start(bf16[32,1,26,384]{3,2,1,0:T(8,128)(2,1)} %fusion.16.refs_1_) | copy-start | bytes 1916932
  381.0 54.4 %copy-start.32 = (bf16[384,1024]{1,0:T(8,128)(2,1)S(1)}, bf16[384,1024]{1,0:T(8,128)(2,1)}, u32[]{:S(2)}) copy-start(bf16[384,1024]{1,0:T(8,128)(2,1)} %get-tuple-element.15) | copy-start | bytes 2359300
  493.8 2.6 copy-start.23
  493.8 2.7 copy-start.22
  493.8 2.8 copy-start.25
  493.8 2.8 copy-start.26
  500.5 2.5 copy-start.13
  512.7 33.4 %collective-permute-start = (bf16[1,96,2048]{2,1,0:T(8,128)(2,1)}, bf16[1,96,2048]{2,1,0:T(8,128)(2,1)S(1)}, u32[]{:S(2)}, u32[]{:S(2)}) collective-permute-start(bf16[1,96,2048]{2,1,0:T(8,128)(2,1)} %bitcast.66), channel_id=1, source_target_pairs={{192,0},{0,64},{64,128},{128,192},{193,1},{1,65},{65,129},{129,193... | collective-permute-start | bytes 1179656 | tf_op jit(solution)/shard_map/ppermute | solution.py:19
  520.5 2.6 copy-start.15
  520.5 12.6 %copy-start.36 = (f32[32,26,384]{2,1,0:T(8,128)S(1)}, f32[32,26,384]{2,1,0:T(8,128)}, u32[]{:S(2)}) copy-start(f32[32,26,384]{2,1,0:T(8,128)} %fusion.19) | copy-start | bytes 3833860
  531.6 7.3 %copy-start.4 = (bf16[32,1,26,384]{3,2,1,0:T(8,128)(2,1)S(1)}, bf16[32,1,26,384]{3,2,1,0:T(8,128)(2,1)}, u32[]{:S(2)}) copy-start(bf16[32,1,26,384]{3,2,1,0:T(8,128)(2,1)} %get-tuple-element.26.refs_1_) | copy-start | bytes 1916932
  531.7 7.3 %copy-start.29 = (bf16[32,26,2048]{2,1,0:T(8,128)(2,1)S(1)}, bf16[32,26,2048]{2,1,0:T(8,128)(2,1)}, u32[]{:S(2)}) copy-start(bf16[32,26,2048]{2,1,0:T(8,128)(2,1)} %get-tuple-element.17) | copy-start | bytes 10223620
  531.7 14.4 %collective-permute-start.1 = (bf16[1,96,2048]{2,1,0:T(8,128)(2,1)S(1)}, bf16[1,96,2048]{2,1,0:T(8,128)(2,1)S(1)}, u32[]{:S(2)}, u32[]{:S(2)}) collective-permute-start(bf16[1,96,2048]{2,1,0:T(8,128)(2,1)S(1)} %bitcast.260), channel_id=1, source_target_pairs={{64,0},{128,64},{192,128},{0,192},{65,1},{129,65},{193,129},{1,193... | collective-permute-start | bytes 1179656 | tf_op jit(solution)/shard_map/ppermute | solution.py:19
  542.5 5.1 copy-start.1

commit v4 on v3

--- a/solution.py
+++ b/solution.py
@@ -211,10 +211,8 @@
     fwd_table = slot_table(fwd_positions, choices_per)
     back_table = slot_table(back_positions, choices_per)
     send_inputs = packed_rows(inputs, fwd_table)
-    send_saved = packed_rows(saved, back_table)
-    send_grad = packed_rows(grad_in, back_table, back_mixing)
-    (recv_saved, recv_grad), swapped_in = exchange(
-        (send_saved, send_grad),
+    (recv_inputs,), swapped_in = exchange(
+        (send_inputs,),
         (
             lax.dynamic_slice_in_dim(down_half[0], theirs, half, 1),
             lax.dynamic_slice_in_dim(gate_half[0], theirs, half, 0),
@@ -222,19 +220,29 @@
         ),
         0,
     )
-    recv_saved, recv_grad = (x.reshape(groups, 1, MOST, model_width) for x in (recv_saved, recv_grad))
+    recv_inputs = recv_inputs.reshape(groups, 1, MOST, model_width)
     down_recv, gate_recv, up_recv = (x[None] for x in swapped_in)
     down_mine = jnp.concatenate([lax.dynamic_slice_in_dim(down_half, mine, half, 2), down_recv], 1)
     gate_mine = jnp.concatenate([lax.dynamic_slice_in_dim(gate_half, mine, half, 1), gate_recv], 2)
     up_mine = jnp.concatenate([lax.dynamic_slice_in_dim(up_half, mine, half, 1), up_recv], 2)
+    send_saved = packed_rows(saved, back_table).reshape(groups, 1, MOST, model_width)
+    send_grad = packed_rows(grad_in, back_table, back_mixing).reshape(groups, 1, MOST, model_width)
+    recv_saved = lax.all_to_all(send_saved, "expert", split_axis=0, concat_axis=0, tiled=True)
+    recv_grad = lax.all_to_all(send_grad, "expert", split_axis=0, concat_axis=0, tiled=True)
+
+    gate_value, up_value = project(recv_inputs, gate_half, up_half)
+    hidden = (jax.nn.silu(gate_value) * up_value).astype(jnp.bfloat16)
+    hidden_all = jnp.concatenate([hidden, swapped(hidden)], -1)
+    out_part = jnp.einsum(
+        "semf,efd->semd", hidden_all, down_mine, preferred_element_type=jnp.float32
+    ).astype(jnp.bfloat16)
 
     back_gate, back_up = project(recv_saved, gate_half, up_half)
     back_hidden, gate_grad, up_grad = local_backward(back_gate, back_up, recv_grad, down_half)
     gate_term, up_term, down_term = weight_terms(
         recv_saved, recv_grad, back_hidden, gate_grad, up_grad
     )
-    (recv_inputs,), (gate_other, up_other) = exchange((send_inputs,), (gate_grad, up_grad), 1)
-    recv_inputs = recv_inputs.reshape(groups, 1, MOST, model_width)
+    gate_other, up_other = swapped((gate_grad, up_grad))
     gate_all = jnp.concatenate([gate_grad, gate_other], -1)
     up_all = jnp.concatenate([up_grad, up_other], -1)
     grad_part = (
@@ -242,14 +250,8 @@
         + jnp.einsum("semf,edf->semd", up_all, up_mine, preferred_element_type=jnp.float32)
     ).astype(jnp.bfloat16)
 
-    gate_value, up_value = project(recv_inputs, gate_half, up_half)
-    hidden = (jax.nn.silu(gate_value) * up_value).astype(jnp.bfloat16)
-    (back_grad,), (hidden_other,) = exchange((grad_part.reshape(groups, MOST, half),), (hidden,), 2)
-    hidden_all = jnp.concatenate([hidden, hidden_other], -1)
-    out_part = jnp.einsum(
-        "semf,efd->semd", hidden_all, down_mine, preferred_element_type=jnp.float32
-    ).astype(jnp.bfloat16)
-    (back_out,), _ = exchange((out_part.reshape(groups, MOST, half),), (), 3)
+    back_out = lax.all_to_all(out_part, "expert", split_axis=0, concat_axis=0, tiled=True)
+    back_grad = lax.all_to_all(grad_part, "expert", split_axis=0, concat_axis=0, tiled=True)
     inputs_part = lax.dynamic_slice_in_dim(inputs, mine, half, 1)
     grad_in_part = lax.dynamic_slice_in_dim(grad_in, mine, half, 1)
     layer_out = mix_rows(inputs_part, back_out, fwd_positions, mixing, choices_per)

time: 557 us -> 520 us (0.934)
  Pallas kernels: 416 us -> 169 us
  waiting for transfers between devices: 0.01 us -> 155 us
  starting transfers between devices: 3.24 us -> 49.8 us
    pallas_call x4 -> x1, Pallas kernels: 416 us -> 169 us  [exchange(): pl.pallas_call(functools.partial(exchange_kernel, n, len(sends), len(swap...]
    all_to_all x0 -> x4, waiting for transfers between devices: none -> 127 us  [the longest x1 89.1 us: local(): lax.all_to_all(send_grad, 'expert', split_axis=0, concat_axis=0, tiled=True)]
    all_to_all x0 -> x4, starting transfers between devices: none -> 38.9 us  [the longest x1 12.6 us: local(): lax.all_to_all(out_part, 'expert', split_axis=0, concat_axis=0, tiled=True)]
    ppermute x0 -> x3, waiting for transfers between devices: none -> 17.7 us  [swapped(): return lax.ppermute(block, 'dp', [(0, 1), (1, 0)])]
    ppermute x2, waiting for transfers between devices: 0.01 us -> 10.5 us  [passed_along(): return lax.ppermute(block, axis, route)]
    reshape x0 -> x2, local copies, waits for them, and re-layouts: none -> 7.83 us  [the longest x1 3.92 us: local(): packed_rows(saved, back_table).reshape(groups, 1, MOST, model_width)]
    convert_element_type x0 -> x5, local copies, waits for them, and re-layouts: none -> 6.94 us  [the longest x1 2.34 us: local(): out_part = jnp.einsum('semf,efd->semd', hidden_all, down_mine, preferred_...]
    ppermute x0 -> x3, starting transfers between devices: none -> 6.3 us  [swapped(): return lax.ppermute(block, 'dp', [(0, 1), (1, 0)])]
  transfers between devices with their start and end apart: 2 -> 9, of which waited for: 0 -> 7; matrix products, arithmetic and copies ran while one was open for 4% -> 16% of each run, Pallas kernels for 0% -> 33%
where the time goes in v4:
time: 520 us; the launch traced here: 511 us
  Pallas kernels  169 us (32%)
  waiting for transfers between devices  155 us (30%)
  starting transfers between devices  49.8 us (10%)
  matrix products  49.6 us (10%)
  local copies, waits for them, and re-layouts  46.2 us (9%)
  blocking collectives  22.8 us (4%)
  other arithmetic  17 us (3%)
    pallas_call x1, Pallas kernels, exchange(): pl.pallas_call(functools.partial(exchange_kernel, n, len(sends), len(swap...  169 us
    all_to_all x1, waiting for transfers between devices, local(): lax.all_to_all(send_grad, 'expert', split_axis=0, concat_axis=0, tiled=True)  89.1 us
    all_to_all x1, waiting for transfers between devices, local(): lax.all_to_all(out_part, 'expert', split_axis=0, concat_axis=0, tiled=True)  26.7 us
    ppermute x3, waiting for transfers between devices, swapped(): return lax.ppermute(block, 'dp', [(0, 1), (1, 0)])  17.7 us
    all_gather x1, blocking collectives, local(): layer_out = lax.all_gather(layer_out, 'dp', axis=1, tiled=True)  13.8 us
    all_to_all x1, starting transfers between devices, local(): lax.all_to_all(out_part, 'expert', split_axis=0, concat_axis=0, tiled=True)  12.6 us
    all_to_all x1, waiting for transfers between devices, local(): lax.all_to_all(grad_part, 'expert', split_axis=0, concat_axis=0, tiled=True)  11.3 us
    ppermute x2, waiting for transfers between devices, passed_along(): return lax.ppermute(block, axis, route)  10.5 us
  transfers between devices with their start and end apart: 9, of which 7 were waited for; matrix products, arithmetic and copies ran while one was open for 16% of the time, Pallas kernels for 33%

profile of v4, /device:TPU:8, one launch (start us, length us, event | category | flops | bytes accessed | tf_op | source)
XLA Modules:
  0.0 511.4 jit_solution(10886069905560260813)
XLA Ops:
  3.2 1.7 reduce-window.16
  8.9 3.9 copy.165
  12.9 10.1 %all-to-all-start.1 = ((bf16[32,1,26,2048]{3,2,1,0:T(8,128)(2,1)}), bf16[32,1,26,2048]{3,2,1,0:T(8,128)(2,1)}, u32[]{:S(2)}, u32[]{:S(2)}) async-start(bf16[32,1,26,2048]{3,2,1,0:T(8,128)(2,1)} %copy.165), calls=%async_computation.1 | async-start | bytes 8388608 | tf_op jit(solution)/shard_map/all_to_all | solution.py:231
  24.0 3.9 copy.169
  28.0 89.1 %all-to-all-done.1 = bf16[32,1,26,2048]{3,2,1,0:T(8,128)(2,1)} async-done(((bf16[32,1,26,2048]{3,2,1,0:T(8,128)(2,1)}), bf16[32,1,26,2048]{3,2,1,0:T(8,128)(2,1)}, u32[]{:S(2)}, u32[]{:S(2)}) %all-to-all-start.1) | async-done | bytes 3407904 | tf_op jit(solution)/shard_map/all_to_all | solution.py:231
  117.1 7.7 %all-to-all-start.2 = ((bf16[32,1,26,2048]{3,2,1,0:T(8,128)(2,1)}), bf16[32,1,26,2048]{3,2,1,0:T(8,128)(2,1)}, u32[]{:S(2)}, u32[]{:S(2)}) async-start(bf16[32,1,26,2048]{3,2,1,0:T(8,128)(2,1)} %copy.169), calls=%async_computation.2 | async-start | bytes 8388608 | tf_op jit(solution)/shard_map/all_to_all | solution.py:230
  125.1 1.7 reduce-window.14
  130.3 3.9 copy.152.refs_0_
  134.2 1.3 dynamic-slice_bitcast_fusion.5
  136.2 1.3 dynamic-slice_bitcast_fusion.1
  138.2 1.3 dynamic-slice_bitcast_fusion
  139.5 169.1 %shard_map.137 = (bf16[32,26,2048]{2,1,0:T(8,128)(2,1)}, bf16[384,1024]{1,0:T(8,128)(2,1)}, bf16[1024,384]{1,0:T(8,128)(2,1)}, bf16[1024,384]{1,0:T(8,128)(2,1)}) custom-call(bf16[32,26,2048]{2,1,0:T(8,128)(2,1)} %copy.152.refs_0_, bf16[384,1024]{1,0:T(8,128)(2,1)} %get-tuple-element.20.refs_1_, bf16[1024,384]{1,0:T(8,128)(2,1)} %get-tuple-element.18.refs_2_, ...), custom_call_target="tpu_custom_call" | custom-call | bytes 11534336 | tf_op jit(solution)/shard_map/pallas_call | solution.py:98
  308.6 4.7 fusion.52
  313.3 2.4 fusion.41
  315.9 2.4 collective-permute-start
  318.3 15.2 %collective-permute-done = bf16[32,1,26,384]{3,0,2,1:T(8,128)(2,1)S(1)} collective-permute-done((bf16[32,1,26,384]{3,0,2,1:T(8,128)(2,1)S(1)}, bf16[32,1,26,384]{3,0,2,1:T(8,128)(2,1)S(1)}, u32[]{:S(2)}, u32[]{:S(2)}) %collective-permute-start) | collective-permute-done | bytes 639008 | tf_op jit(solution)/shard_map/ppermute | solution.py:23
  335.2 1.7 fusion.60
  336.8 2.3 copy.156
  339.2 12.6 %all-to-all-start = ((bf16[32,1,26,1024]{3,2,1,0:T(8,128)(2,1)}), bf16[32,1,26,1024]{3,2,1,0:T(8,128)(2,1)}, u32[]{:S(2)}, u32[]{:S(2)}) async-start(bf16[32,1,26,1024]{3,2,1,0:T(8,128)(2,1)} %copy.156), calls=%async_computation | async-start | bytes 4194304 | tf_op jit(solution)/shard_map/all_to_all | solution.py:253
  351.8 4.2 fusion.6
  356.0 4.7 fusion.8
  360.8 4.8 fusion.10
  365.6 2.6 fusion.46
  368.2 1.1 copy.176
  370.3 2.3 collective-permute-start.2
  372.6 1.6 collective-permute-start.3
  375.1 26.7 %all-to-all-done = bf16[32,1,26,1024]{3,2,1,0:T(8,128)(2,1)} async-done(((bf16[32,1,26,1024]{3,2,1,0:T(8,128)(2,1)}), bf16[32,1,26,1024]{3,2,1,0:T(8,128)(2,1)}, u32[]{:S(2)}, u32[]{:S(2)}) %all-to-all-start) | async-done | bytes 1703968 | tf_op jit(solution)/shard_map/all_to_all | solution.py:253
  401.9 2.5 reshape.254
  404.4 3.6 gather_fusion
  407.9 2.4 fusion.13
  410.4 2.4 collective-permute-done.3
  412.8 1.3 copy.177
  416.6 1.7 fusion.35
  418.4 1.7 fusion.61
  420.1 2.3 copy.179
  422.4 8.5 %all-to-all-start.3 = ((bf16[32,1,26,1024]{3,2,1,0:T(8,128)(2,1)}), bf16[32,1,26,1024]{3,2,1,0:T(8,128)(2,1)}, u32[]{:S(2)}, u32[]{:S(2)}) async-start(bf16[32,1,26,1024]{3,2,1,0:T(8,128)(2,1)} %copy.179), calls=%async_computation.3 | async-start | bytes 4194304 | tf_op jit(solution)/shard_map/all_to_all | solution.py:254
  430.9 13.8 %all_gather.6 = bf16[96,2048]{1,0:T(8,128)(2,1)S(1)} all-gather(bf16[96,1024]{1,0:T(8,128)(2,1)S(1)} %fusion.77), channel_id=1, replica_groups=mesh['section'=4,'expert'=32,'dp'=2] {'dp'}, dimensions={1}, use_global_device_ids=true | all-gather | bytes 589824 | tf_op jit(solution)/shard_map/all_gather | solution.py:259
  444.7 1.7 collective-permute-start.1
  446.5 9.6 %collective-permute-done.1 = bf16[1,96,2048]{2,1,0:T(8,128)(2,1)S(1)} collective-permute-done((bf16[1,96,2048]{2,1,0:T(8,128)(2,1)S(1)}, bf16[1,96,2048]{2,1,0:T(8,128)(2,1)S(1)}, u32[]{:S(2)}, u32[]{:S(2)}) %collective-permute-start.1) | collective-permute-done | bytes 393248 | tf_op jit(solution)/shard_map/ppermute | solution.py:19
  456.1 7.0 %fusion.24 = bf16[1,1,2048,384]{3,2,1,0:T(8,128)(2,1)} fusion(bf16[32,1,26,2048]{3,2,1,0:T(8,128)(2,1)} %all-to-all-done.2, bf16[32,26,384]{2,1,0:T(8,128)(2,1)S(1)} %bitcast.276), kind=kOutput, calls=%fused_computation.32 | convolution fusion | flops 1309409280 | bytes 5619712 | tf_op jit(solution)/shard_map/semd,semf->edf/dot_general | solution.py:168
  463.1 6.7 %fusion.30 = bf16[1,1,384,2048]{3,2,1,0:T(8,128)(2,1)} fusion(bf16[32,1,26,2048]{3,2,1,0:T(8,128)(2,1)} %all-to-all-done.1, f32[32,26,384]{2,0,1:T(8,128)S(1)} %copy-done.11, f32[32,26,384]{2,0,1:T(8,128)S(1)} %copy-done.9), kind=kOutput, calls=%fused_computation.34 | convolution fusion | flops 1311326208 | bytes 7536640 | tf_op jit(solution)/shard_map/semf,semd->efd/dot_general | solution.py:172
  469.8 11.3 %all-to-all-done.3 = bf16[32,1,26,1024]{3,2,1,0:T(8,128)(2,1)} async-done(((bf16[32,1,26,1024]{3,2,1,0:T(8,128)(2,1)}), bf16[32,1,26,1024]{3,2,1,0:T(8,128)(2,1)}, u32[]{:S(2)}, u32[]{:S(2)}) %all-to-all-start.3) | async-done | bytes 1703968 | tf_op jit(solution)/shard_map/all_to_all | solution.py:254
  481.2 2.5 reshape.266
  483.7 3.6 gather_fusion.1
  487.3 2.5 convert_reduce_fusion
  489.8 9.1 %all_gather.7 = bf16[96,2048]{1,0:T(8,128)(2,1)S(1)} all-gather(bf16[96,1024]{1,0:T(8,128)(2,1)S(1)} %fusion.76), channel_id=1, replica_groups=mesh['section'=4,'expert'=32,'dp'=2] {'dp'}, dimensions={1}, use_global_device_ids=true | all-gather | bytes 589824 | tf_op jit(solution)/shard_map/all_gather | solution.py:260
  498.9 3.0 collective-permute-start.4
  501.9 6.9 %fusion.27 = bf16[1,1,2048,384]{3,2,1,0:T(8,128)(2,1)} fusion(bf16[32,1,26,2048]{3,2,1,0:T(8,128)(2,1)} %all-to-all-done.2, bf16[32,26,384]{2,1,0:T(8,128)(2,1)S(1)} %bitcast.275), kind=kOutput, calls=%fused_computation.33 | convolution fusion | flops 1309409280 | bytes 5619712 | tf_op jit(solution)/shard_map/semd,semf->edf/dot_general | solution.py:171
  (110 shorter events, 21.3 us)
Async XLA Ops:
  0.6 22.4 %copy-start = (bf16[1,96,2048]{2,1,0:T(8,128)(2,1)S(1)}, bf16[1,96,2048]{2,1,0:T(8,128)(2,1)}, u32[]{:S(2)}) copy-start(bf16[1,96,2048]{2,1,0:T(8,128)(2,1)} %param.13) | copy-start | bytes 1179652
  0.6 7.3 %copy-start.14 = (bf16[1,96,2048]{2,1,0:T(8,128)(2,1)S(1)}, bf16[1,96,2048]{2,1,0:T(8,128)(2,1)}, u32[]{:S(2)}) copy-start(bf16[1,96,2048]{2,1,0:T(8,128)(2,1)} %param.16) | copy-start | bytes 1179652
  12.9 104.2 %all-to-all-start.1 = ((bf16[32,1,26,2048]{3,2,1,0:T(8,128)(2,1)}), bf16[32,1,26,2048]{3,2,1,0:T(8,128)(2,1)}, u32[]{:S(2)}, u32[]{:S(2)}) async-start(bf16[32,1,26,2048]{3,2,1,0:T(8,128)(2,1)} %copy.165), calls=%async_computation.1 | async-start | bytes 8388608 | tf_op jit(solution)/shard_map/all_to_all | solution.py:231
  28.0 96.9 %copy-start.22 = (s32[1,96,8]{1,2,0:T(8,128)S(1)}, s32[1,96,8]{1,2,0:T(8,128)}, u32[]{:S(2)}) copy-start(s32[1,96,8]{1,2,0:T(8,128)} %param.11) | copy-start | bytes 9220
  117.1 222.1 %all-to-all-start.2 = ((bf16[32,1,26,2048]{3,2,1,0:T(8,128)(2,1)}), bf16[32,1,26,2048]{3,2,1,0:T(8,128)(2,1)}, u32[]{:S(2)}, u32[]{:S(2)}) async-start(bf16[32,1,26,2048]{3,2,1,0:T(8,128)(2,1)} %copy.169), calls=%async_computation.2 | async-start | bytes 8388608 | tf_op jit(solution)/shard_map/all_to_all | solution.py:230
  124.8 4.4 copy-start.12
  130.3 3.9 copy-start.6
  134.2 2.0 copy-start.4
  136.2 2.0 copy-start.5
  308.6 4.7 copy-start.23
  315.9 17.6 %collective-permute-start = (bf16[32,1,26,384]{3,0,2,1:T(8,128)(2,1)S(1)}, bf16[32,1,26,384]{3,0,2,1:T(8,128)(2,1)S(1)}, u32[]{:S(2)}, u32[]{:S(2)}) collective-permute-start(bf16[32,1,26,384]{3,0,2,1:T(8,128)(2,1)S(1)} %copy.153), channel_id=1, source_target_pairs={{0,1},{1,0},{2,3},{3,2},{4,5},{5,4},{6,7},{7,6},{8,9},{9,8},{10,11... | collective-permute-start | bytes 1916936 | tf_op jit(solution)/shard_map/ppermute | solution.py:23
  333.8 1.1 copy-start.18
  333.8 1.4 copy-start.26
  339.2 12.6 %copy-start.21 = (s32[1,96,8]{1,2,0:T(8,128)S(1)}, s32[1,96,8]{1,2,0:T(8,128)}, u32[]{:S(2)}) copy-start(s32[1,96,8]{1,2,0:T(8,128)} %param.12) | copy-start | bytes 9220
  339.2 62.7 %all-to-all-start = ((bf16[32,1,26,1024]{3,2,1,0:T(8,128)(2,1)}), bf16[32,1,26,1024]{3,2,1,0:T(8,128)(2,1)}, u32[]{:S(2)}, u32[]{:S(2)}) async-start(bf16[32,1,26,1024]{3,2,1,0:T(8,128)(2,1)} %copy.156), calls=%async_computation | async-start | bytes 4194304 | tf_op jit(solution)/shard_map/all_to_all | solution.py:253
  356.0 9.6 %copy-start.8 = (f32[32,26,384]{2,0,1:T(8,128)}, f32[32,26,384]{2,0,1:T(8,128)S(1)}, u32[]{:S(2)}) copy-start(f32[32,26,384]{2,0,1:T(8,128)S(1)} %fusion.6) | copy-start | bytes 3833860
  356.0 4.7 copy-start.7
  360.7 4.8 copy-start.10
  368.2 1.1 copy-start.2
  368.2 6.8 %copy-start.20 = (s32[1,96,8]{2,1,0:T(8,128)S(1)}, s32[1,96,8]{2,1,0:T(8,128)}, u32[]{:S(2)}) copy-start(s32[1,96,8]{2,1,0:T(8,128)} %get-tuple-element.23) | copy-start | bytes 9220
  370.3 44.0 %collective-permute-start.2 = (bf16[32,1,26,384]{3,0,2,1:T(8,128)(2,1)}, bf16[32,1,26,384]{3,0,2,1:T(8,128)(2,1)S(1)}, u32[]{:S(2)}, u32[]{:S(2)}) collective-permute-start(bf16[32,1,26,384]{3,0,2,1:T(8,128)(2,1)} %copy.173), channel_id=1, source_target_pairs={{0,1},{1,0},{2,3},{3,2},{4,5},{5,4},{6,7},{7,6},{8,9},{9,8},{10,11... | collective-permute-start | bytes 1916936 | tf_op jit(solution)/shard_map/ppermute | solution.py:23
  372.6 40.2 %collective-permute-start.3 = (bf16[32,1,26,384]{3,0,2,1:T(8,128)(2,1)}, bf16[32,1,26,384]{3,0,2,1:T(8,128)(2,1)}, u32[]{:S(2)}, u32[]{:S(2)}) collective-permute-start(bf16[32,1,26,384]{3,0,2,1:T(8,128)(2,1)} %copy.176), channel_id=1, source_target_pairs={{0,1},{1,0},{2,3},{3,2},{4,5},{5,4},{6,7},{7,6},{8,9},{9,8},{10,11... | collective-permute-start | bytes 1916936 | tf_op jit(solution)/shard_map/ppermute | solution.py:23
  414.1 1.1 copy-start.3
  415.3 1.1 copy-start.17
  415.3 1.4 copy-start.25
  416.6 1.7 copy-start.16
  416.6 1.7 copy-start.24
  422.4 8.5 %copy-start.13 = (bf16[1,96,2048]{2,1,0:T(8,128)(2,1)S(1)}, bf16[1,96,2048]{2,1,0:T(8,128)(2,1)}, u32[]{:S(2)}) copy-start(bf16[1,96,2048]{2,1,0:T(8,128)(2,1)} %param.10) | copy-start | bytes 1179652
  422.4 24.0 %copy-start.19 = (s32[1,96,8]{2,1,0:T(8,128)S(1)}, s32[1,96,8]{2,1,0:T(8,128)}, u32[]{:S(2)}) copy-start(s32[1,96,8]{2,1,0:T(8,128)} %get-tuple-element.21) | copy-start | bytes 9220
  422.4 58.8 %all-to-all-start.3 = ((bf16[32,1,26,1024]{3,2,1,0:T(8,128)(2,1)}), bf16[32,1,26,1024]{3,2,1,0:T(8,128)(2,1)}, u32[]{:S(2)}, u32[]{:S(2)}) async-start(bf16[32,1,26,1024]{3,2,1,0:T(8,128)(2,1)} %copy.179), calls=%async_computation.3 | async-start | bytes 4194304 | tf_op jit(solution)/shard_map/all_to_all | solution.py:254
  444.7 11.4 %collective-permute-start.1 = (bf16[1,96,2048]{2,1,0:T(8,128)(2,1)S(1)}, bf16[1,96,2048]{2,1,0:T(8,128)(2,1)S(1)}, u32[]{:S(2)}, u32[]{:S(2)}) collective-permute-start(bf16[1,96,2048]{2,1,0:T(8,128)(2,1)S(1)} %bitcast.277), channel_id=1, source_target_pairs={{192,0},{0,64},{64,128},{128,192},{193,1},{1,65},{65,129},{129,193... | collective-permute-start | bytes 1179656 | tf_op jit(solution)/shard_map/ppermute | solution.py:19
  456.1 7.0 %copy-start.9 = (f32[32,26,384]{2,0,1:T(8,128)S(1)}, f32[32,26,384]{2,0,1:T(8,128)}, u32[]{:S(2)}) copy-start(f32[32,26,384]{2,0,1:T(8,128)} %copy-done.8) | copy-start | bytes 3833860
  456.1 7.0 %copy-start.11 = (f32[32,26,384]{2,0,1:T(8,128)S(1)}, f32[32,26,384]{2,0,1:T(8,128)}, u32[]{:S(2)}) copy-start(f32[32,26,384]{2,0,1:T(8,128)} %copy-done.10) | copy-start | bytes 3833860
  487.3 2.5 copy-start.15
  498.9 10.7 %collective-permute-start.4 = (bf16[1,96,2048]{2,1,0:T(8,128)(2,1)S(1)}, bf16[1,96,2048]{2,1,0:T(8,128)(2,1)S(1)}, u32[]{:S(2)}, u32[]{:S(2)}) collective-permute-start(bf16[1,96,2048]{2,1,0:T(8,128)(2,1)S(1)} %bitcast.278), channel_id=1, source_target_pairs={{64,0},{128,64},{192,128},{0,192},{65,1},{129,65},{193,129},{1,193... | collective-permute-start | bytes 1179656 | tf_op jit(solution)/shard_map/ppermute | solution.py:19
  501.9 9.3 %copy-start.1 = (bf16[1,96,2048]{2,1,0:T(8,128)(2,1)S(1)}, bf16[1,96,2048]{2,1,0:T(8,128)(2,1)}, u32[]{:S(2)}) copy-start(bf16[1,96,2048]{2,1,0:T(8,128)(2,1)} %param.13) | copy-start | bytes 1179652

commit v5 on v4

--- a/solution.py
+++ b/solution.py
@@ -141,7 +141,12 @@
 
 
 def handoff(value, direction):
-    return passed_along(value, "section", direction)
+    sections = lax.axis_size("section")
+    same = passed_along(value, "section", direction)
+    route = [(i * 2 + j, ((i + direction) % sections) * 2 + 1 - j) for i in range(sections) for j in range(2)]
+    crossed = lax.ppermute(value, ("section", "dp"), route)
+    first = lax.axis_index("dp") == 0
+    return jnp.concatenate([jnp.where(first, same, crossed), jnp.where(first, crossed, same)], 1)
 
 
 def project(rows, gate_weight, up_weight):
@@ -227,6 +232,7 @@
     up_mine = jnp.concatenate([lax.dynamic_slice_in_dim(up_half, mine, half, 1), up_recv], 2)
     send_saved = packed_rows(saved, back_table).reshape(groups, 1, MOST, model_width)
     send_grad = packed_rows(grad_in, back_table, back_mixing).reshape(groups, 1, MOST, model_width)
+    recv_inputs, send_saved, send_grad = lax.optimization_barrier((recv_inputs, send_saved, send_grad))
     recv_saved = lax.all_to_all(send_saved, "expert", split_axis=0, concat_axis=0, tiled=True)
     recv_grad = lax.all_to_all(send_grad, "expert", split_axis=0, concat_axis=0, tiled=True)
 
@@ -256,10 +262,8 @@
     grad_in_part = lax.dynamic_slice_in_dim(grad_in, mine, half, 1)
     layer_out = mix_rows(inputs_part, back_out, fwd_positions, mixing, choices_per)
     input_grad = mix_rows(grad_in_part, back_grad, back_positions, unit_weights, choices_per)
-    layer_out = lax.all_gather(layer_out, "dp", axis=1, tiled=True)
-    input_grad = lax.all_gather(input_grad, "dp", axis=1, tiled=True)
-    next_fwd = handoff(layer_out[None], 1)
-    next_bwd = handoff(input_grad[None], -1)
+    next_fwd = handoff(layer_out, 1)[None]
+    next_bwd = handoff(input_grad, -1)[None]
     gate_sum = gate_term.astype(jnp.bfloat16)
     up_sum = up_term.astype(jnp.bfloat16)
     down_sum = down_term.astype(jnp.bfloat16)

time: 520 us -> 516 us (level)
  the two profiles are of different devices: /device:TPU:8 before, /device:TPU:6 now
where the time goes in v5:
time: 516 us; the launch traced here: 507 us
  waiting for transfers between devices  235 us (46%)
  Pallas kernels  105 us (20%)
  matrix products  53.2 us (10%)
  local copies, waits for them, and re-layouts  49 us (9%)
  starting transfers between devices  42.1 us (8%)
  other arithmetic  20.4 us (4%)
    pallas_call x1, Pallas kernels, exchange(): pl.pallas_call(functools.partial(exchange_kernel, n, len(sends), len(swap...  105 us
    all_to_all x1, waiting for transfers between devices, local(): lax.all_to_all(send_grad, 'expert', split_axis=0, concat_axis=0, tiled=True)  90.8 us
    all_to_all x1, waiting for transfers between devices, local(): lax.all_to_all(send_saved, 'expert', split_axis=0, concat_axis=0, tiled=T...  46.8 us
    all_to_all x1, waiting for transfers between devices, local(): lax.all_to_all(grad_part, 'expert', split_axis=0, concat_axis=0, tiled=True)  34 us
    ppermute x3, waiting for transfers between devices, swapped(): return lax.ppermute(block, 'dp', [(0, 1), (1, 0)])  32.5 us
    all_to_all x1, waiting for transfers between devices, local(): lax.all_to_all(out_part, 'expert', split_axis=0, concat_axis=0, tiled=True)  27.3 us
    optimization_barrier x2, local copies, waits for them, and re-layouts, local(): lax.optimization_barrier((recv_inputs, send_saved, send_grad))  11.8 us
  transfers between devices with their start and end apart: 11, of which 7 were waited for; matrix products, arithmetic and copies ran while one was open for 15% of the time, Pallas kernels for 0%

profile of v5, /device:TPU:6, one launch (start us, length us, event | category | flops | bytes accessed | tf_op | source)
XLA Modules:
  0.0 506.8 jit_solution(3719223246200631811)
XLA Ops:
  4.2 1.7 reduce-window.16
  9.6 1.7 reduce-window.14
  14.8 3.9 copy.152.refs_0_
  18.6 1.3 dynamic-slice_bitcast_fusion.5
  21.1 1.8 dynamic-slice_bitcast_fusion
  22.8 2.8 fusion.18
  25.6 2.8 fusion.19
  28.4 105.4 %shard_map.137 = (bf16[32,26,2048]{2,1,0:T(8,128)(2,1)}, bf16[384,1024]{1,0:T(8,128)(2,1)}, bf16[1024,384]{1,0:T(8,128)(2,1)}, bf16[1024,384]{1,0:T(8,128)(2,1)}) custom-call(bf16[32,26,2048]{2,1,0:T(8,128)(2,1)} %copy.152.refs_0_, bf16[384,1024]{1,0:T(8,128)(2,1)} %get-tuple-element.26.refs_1_, bf16[1024,384]{1,0:T(8,128)(2,1)} %get-tuple-element.35.refs_2_, ...), custom_call_target="tpu_custom_call" | custom-call | bytes 11534336 | tf_op jit(solution)/shard_map/pallas_call | solution.py:98
  133.8 5.9 %copy.166 = bf16[32,1,26,2048]{3,2,1,0:T(8,128)(2,1)} copy(bf16[32,1,26,2048]{3,0,2,1:T(8,128)(2,1)} %fusion.19) | data formatting | bytes 6815744 | tf_op jit(solution)/shard_map/optimization_barrier | solution.py:235
  139.7 7.5 %all-to-all-start.1 = ((bf16[32,1,26,2048]{3,2,1,0:T(8,128)(2,1)}), bf16[32,1,26,2048]{3,2,1,0:T(8,128)(2,1)}, u32[]{:S(2)}, u32[]{:S(2)}) async-start(bf16[32,1,26,2048]{3,2,1,0:T(8,128)(2,1)} %copy.166), calls=%async_computation.1 | async-start | bytes 8388608 | tf_op jit(solution)/shard_map/all_to_all | solution.py:237
  147.2 5.9 %copy.169 = bf16[32,1,26,2048]{3,2,1,0:T(8,128)(2,1)} copy(bf16[32,1,26,2048]{3,0,2,1:T(8,128)(2,1)} %fusion.18) | data formatting | bytes 6815744 | tf_op jit(solution)/shard_map/optimization_barrier | solution.py:235
  153.1 90.8 %all-to-all-done.1 = bf16[32,1,26,2048]{3,2,1,0:T(8,128)(2,1)} async-done(((bf16[32,1,26,2048]{3,2,1,0:T(8,128)(2,1)}), bf16[32,1,26,2048]{3,2,1,0:T(8,128)(2,1)}, u32[]{:S(2)}, u32[]{:S(2)}) %all-to-all-start.1) | async-done | bytes 3407904 | tf_op jit(solution)/shard_map/all_to_all | solution.py:237
  243.9 4.8 all-to-all-start.2
  248.8 4.7 fusion.4
  253.5 2.4 fusion.45
  256.1 4.4 collective-permute-start
  260.5 32.5 %collective-permute-done = bf16[32,1,26,384]{3,0,2,1:T(8,128)(2,1)S(1)} collective-permute-done((bf16[32,1,26,384]{3,0,2,1:T(8,128)(2,1)S(1)}, bf16[32,1,26,384]{3,0,2,1:T(8,128)(2,1)S(1)}, u32[]{:S(2)}, u32[]{:S(2)}) %collective-permute-start) | collective-permute-done | bytes 639008 | tf_op jit(solution)/shard_map/ppermute | solution.py:23
  294.6 1.7 fusion.62
  296.3 2.3 copy.165
  298.6 46.8 %all-to-all-done.2 = bf16[32,1,26,2048]{3,2,1,0:T(8,128)(2,1)} async-done(((bf16[32,1,26,2048]{3,2,1,0:T(8,128)(2,1)}), bf16[32,1,26,2048]{3,2,1,0:T(8,128)(2,1)}, u32[]{:S(2)}, u32[]{:S(2)}) %all-to-all-start.2) | async-done | bytes 3407904 | tf_op jit(solution)/shard_map/all_to_all | solution.py:236
  345.4 5.0 all-to-all-start
  350.6 4.3 fusion.10
  354.9 4.7 fusion.12
  359.7 4.8 fusion.14
  364.5 2.6 fusion.50
  367.1 1.1 copy.176
  368.2 4.3 collective-permute-start.4
  374.8 27.3 %all-to-all-done = bf16[32,1,26,1024]{3,2,1,0:T(8,128)(2,1)} async-done(((bf16[32,1,26,1024]{3,2,1,0:T(8,128)(2,1)}), bf16[32,1,26,1024]{3,2,1,0:T(8,128)(2,1)}, u32[]{:S(2)}, u32[]{:S(2)}) %all-to-all-start) | async-done | bytes 1703968 | tf_op jit(solution)/shard_map/all_to_all | solution.py:259
  402.1 2.5 reshape.262
  404.6 3.6 gather_fusion
  408.2 2.5 fusion.17
  411.4 4.0 collective-permute-start.2
  415.4 1.5 collective-permute-start.1
  417.4 1.3 copy.174
  420.1 1.7 fusion.39
  421.8 1.7 fusion.63
  423.5 2.3 copy.179
  425.8 7.0 %all-to-all-start.3 = ((bf16[32,1,26,1024]{3,2,1,0:T(8,128)(2,1)}), bf16[32,1,26,1024]{3,2,1,0:T(8,128)(2,1)}, u32[]{:S(2)}, u32[]{:S(2)}) async-start(bf16[32,1,26,1024]{3,2,1,0:T(8,128)(2,1)} %copy.179), calls=%async_computation.3 | async-start | bytes 4194304 | tf_op jit(solution)/shard_map/all_to_all | solution.py:260
  435.4 7.0 %fusion.28 = bf16[1,1,2048,384]{3,2,1,0:T(8,128)(2,1)} fusion(bf16[32,1,26,2048]{3,2,1,0:T(8,128)(2,1)} %all-to-all-done.2, bf16[32,26,384]{2,1,0:T(8,128)(2,1)S(1)} %bitcast.284), kind=kOutput, calls=%fused_computation.36 | convolution fusion | flops 1309409280 | bytes 5619712 | tf_op jit(solution)/shard_map/semd,semf->edf/dot_general | solution.py:173
  442.4 6.7 %fusion.34 = bf16[1,1,384,2048]{3,2,1,0:T(8,128)(2,1)} fusion(bf16[32,1,26,2048]{3,2,1,0:T(8,128)(2,1)} %all-to-all-done.1, f32[32,26,384]{2,0,1:T(8,128)S(1)} %copy-done.12, f32[32,26,384]{2,0,1:T(8,128)S(1)} %copy-done.10), kind=kOutput, calls=%fused_computation.38 | convolution fusion | flops 1311326208 | bytes 7536640 | tf_op jit(solution)/shard_map/semf,semd->efd/dot_general | solution.py:177
  449.1 34.0 %all-to-all-done.3 = bf16[32,1,26,1024]{3,2,1,0:T(8,128)(2,1)} async-done(((bf16[32,1,26,1024]{3,2,1,0:T(8,128)(2,1)}), bf16[32,1,26,1024]{3,2,1,0:T(8,128)(2,1)}, u32[]{:S(2)}, u32[]{:S(2)}) %all-to-all-start.3) | async-done | bytes 1703968 | tf_op jit(solution)/shard_map/all_to_all | solution.py:260
  483.1 2.5 reshape.270
  485.7 3.6 gather_fusion.1
  489.2 2.5 convert_reduce_fusion
  491.8 2.4 collective-permute-start.6
  495.1 6.9 %fusion.31 = bf16[1,1,2048,384]{3,2,1,0:T(8,128)(2,1)} fusion(bf16[32,1,26,2048]{3,2,1,0:T(8,128)(2,1)} %all-to-all-done.2, bf16[32,26,384]{2,1,0:T(8,128)(2,1)S(1)} %bitcast.283), kind=kOutput, calls=%fused_computation.37 | convolution fusion | flops 1309409280 | bytes 5619712 | tf_op jit(solution)/shard_map/semd,semf->edf/dot_general | solution.py:176
  501.9 1.3 collective-permute-done.6
  503.3 2.5 collective-permute-done.5
  (125 shorter events, 22.7 us)
Async XLA Ops:
  0.6 22.2 %copy-start = (bf16[1,96,2048]{2,1,0:T(8,128)(2,1)S(1)}, bf16[1,96,2048]{2,1,0:T(8,128)(2,1)}, u32[]{:S(2)}) copy-start(bf16[1,96,2048]{2,1,0:T(8,128)(2,1)} %param.13) | copy-start | bytes 1179652
  1.6 12.1 %copy-start.14 = (bf16[1,96,2048]{2,1,0:T(8,128)(2,1)S(1)}, bf16[1,96,2048]{2,1,0:T(8,128)(2,1)}, u32[]{:S(2)}) copy-start(bf16[1,96,2048]{2,1,0:T(8,128)(2,1)} %param.10) | copy-start | bytes 1179652
  6.3 2.1 copy-start.24
  11.7 0.7 copy-start.26
  14.7 3.9 copy-start.4
  18.6 2.0 copy-start.5
  18.6 2.4 copy-start.6
  21.1 1.8 copy-start.13
  22.8 2.8 copy-start.16
  139.7 104.2 %all-to-all-start.1 = ((bf16[32,1,26,2048]{3,2,1,0:T(8,128)(2,1)}), bf16[32,1,26,2048]{3,2,1,0:T(8,128)(2,1)}, u32[]{:S(2)}, u32[]{:S(2)}) async-start(bf16[32,1,26,2048]{3,2,1,0:T(8,128)(2,1)} %copy.166), calls=%async_computation.1 | async-start | bytes 8388608 | tf_op jit(solution)/shard_map/all_to_all | solution.py:237
  243.9 101.5 %all-to-all-start.2 = ((bf16[32,1,26,2048]{3,2,1,0:T(8,128)(2,1)}), bf16[32,1,26,2048]{3,2,1,0:T(8,128)(2,1)}, u32[]{:S(2)}, u32[]{:S(2)}) async-start(bf16[32,1,26,2048]{3,2,1,0:T(8,128)(2,1)} %copy.169), calls=%async_computation.2 | async-start | bytes 8388608 | tf_op jit(solution)/shard_map/all_to_all | solution.py:236
  248.8 4.7 copy-start.7
  248.8 4.7 copy-start.29
  256.1 36.9 %collective-permute-start = (bf16[32,1,26,384]{3,0,2,1:T(8,128)(2,1)S(1)}, bf16[32,1,26,384]{3,0,2,1:T(8,128)(2,1)S(1)}, u32[]{:S(2)}, u32[]{:S(2)}) collective-permute-start(bf16[32,1,26,384]{3,0,2,1:T(8,128)(2,1)S(1)} %copy.162), channel_id=1, source_target_pairs={{0,1},{1,0},{2,3},{3,2},{4,5},{5,4},{6,7},{7,6},{8,9},{9,8},{10,11... | collective-permute-start | bytes 1916936 | tf_op jit(solution)/shard_map/ppermute | solution.py:23
  293.2 1.1 copy-start.18
  293.2 1.4 copy-start.32
  298.6 51.8 %copy-start.22 = (s32[1,96,8]{2,1,0:T(8,128)S(1)}, s32[1,96,8]{2,1,0:T(8,128)}, u32[]{:S(2)}) copy-start(s32[1,96,8]{2,1,0:T(8,128)} %get-tuple-element.33) | copy-start | bytes 9220
  298.6 51.9 %copy-start.28 = (s32[1,96,8]{1,2,0:T(8,128)S(1)}, s32[1,96,8]{1,2,0:T(8,128)}, u32[]{:S(2)}) copy-start(s32[1,96,8]{1,2,0:T(8,128)} %param.12) | copy-start | bytes 9220
  345.4 56.7 %all-to-all-start = ((bf16[32,1,26,1024]{3,2,1,0:T(8,128)(2,1)}), bf16[32,1,26,1024]{3,2,1,0:T(8,128)(2,1)}, u32[]{:S(2)}, u32[]{:S(2)}) async-start(bf16[32,1,26,1024]{3,2,1,0:T(8,128)(2,1)} %copy.165), calls=%async_computation | async-start | bytes 4194304 | tf_op jit(solution)/shard_map/all_to_all | solution.py:259
  350.5 4.4 copy-start.8
  354.9 9.5 %copy-start.9 = (f32[32,26,384]{2,0,1:T(8,128)}, f32[32,26,384]{2,0,1:T(8,128)S(1)}, u32[]{:S(2)}) copy-start(f32[32,26,384]{2,0,1:T(8,128)S(1)} %fusion.10) | copy-start | bytes 3833860
  359.6 4.8 copy-start.11
  364.5 8.0 %copy-start.27 = (s32[768]{0:T(1024)S(1)}, s32[768]{0:T(1024)}, u32[]{:S(2)}) copy-start(s32[768]{0:T(1024)} %copy-done.26) | copy-start | bytes 9220
  367.1 5.4 %copy-start.2 = (bf16[32,1,26,384]{3,2,0,1:T(8,128)(2,1)}, bf16[32,1,26,384]{3,2,0,1:T(8,128)(2,1)S(1)}, u32[]{:S(2)}) copy-start(bf16[32,1,26,384]{3,2,0,1:T(8,128)(2,1)S(1)} %get-tuple-element.20) | copy-start | bytes 1916932
  367.1 7.6 %copy-start.21 = (s32[1,96,8]{2,1,0:T(8,128)S(1)}, s32[1,96,8]{2,1,0:T(8,128)}, u32[]{:S(2)}) copy-start(s32[1,96,8]{2,1,0:T(8,128)} %get-tuple-element.31) | copy-start | bytes 9220
  368.2 48.7 %collective-permute-start.4 = (bf16[32,1,26,384]{3,0,2,1:T(8,128)(2,1)}, bf16[32,1,26,384]{3,0,2,1:T(8,128)(2,1)S(1)}, u32[]{:S(2)}, u32[]{:S(2)}) collective-permute-start(bf16[32,1,26,384]{3,0,2,1:T(8,128)(2,1)} %copy.176), channel_id=1, source_target_pairs={{0,1},{1,0},{2,3},{3,2},{4,5},{5,4},{6,7},{7,6},{8,9},{9,8},{10,11... | collective-permute-start | bytes 1916936 | tf_op jit(solution)/shard_map/ppermute | solution.py:23
  373.6 43.8 %collective-permute-start.3 = (bf16[32,1,26,384]{3,0,2,1:T(8,128)(2,1)}, bf16[32,1,26,384]{3,0,2,1:T(8,128)(2,1)}, u32[]{:S(2)}, u32[]{:S(2)}) collective-permute-start(bf16[32,1,26,384]{3,0,2,1:T(8,128)(2,1)} %copy.173), channel_id=1, source_target_pairs={{0,1},{1,0},{2,3},{3,2},{4,5},{5,4},{6,7},{7,6},{8,9},{9,8},{10,11... | collective-permute-start | bytes 1916936 | tf_op jit(solution)/shard_map/ppermute | solution.py:23
  408.2 2.5 copy-start.15
  411.4 21.5 %collective-permute-start.2 = (bf16[96,1024]{1,0:T(8,128)(2,1)}, bf16[96,1024]{1,0:T(8,128)(2,1)S(1)}, u32[]{:S(2)}, u32[]{:S(2)}) collective-permute-start(bf16[96,1024]{1,0:T(8,128)(2,1)} %fusion.81), channel_id=1, source_target_pairs={{0,65},{1,64},{64,129},{65,128},{128,193},{129,192},{192,1},{193,0... | collective-permute-start | bytes 589832 | tf_op jit(solution)/shard_map/ppermute | solution.py:147
  415.4 18.2 %collective-permute-start.1 = (bf16[96,1024]{1,0:T(8,128)(2,1)}, bf16[96,1024]{1,0:T(8,128)(2,1)}, u32[]{:S(2)}, u32[]{:S(2)}) collective-permute-start(bf16[96,1024]{1,0:T(8,128)(2,1)} %fusion.81), channel_id=1, source_target_pairs={{192,0},{0,64},{64,128},{128,192},{193,1},{1,65},{65,129},{129,193... | collective-permute-start | bytes 589832 | tf_op jit(solution)/shard_map/ppermute | solution.py:19
  417.1 1.6 copy-start.3
  418.7 1.1 copy-start.20
  418.7 1.4 copy-start.31
  420.1 1.7 copy-start.19
  420.1 1.7 copy-start.30
  425.8 7.0 %copy-start.25 = (s32[768]{0:T(1024)S(1)}, s32[768]{0:T(1024)}, u32[]{:S(2)}) copy-start(s32[768]{0:T(1024)} %copy-done.24) | copy-start | bytes 9220
  425.8 57.3 %all-to-all-start.3 = ((bf16[32,1,26,1024]{3,2,1,0:T(8,128)(2,1)}), bf16[32,1,26,1024]{3,2,1,0:T(8,128)(2,1)}, u32[]{:S(2)}, u32[]{:S(2)}) async-start(bf16[32,1,26,1024]{3,2,1,0:T(8,128)(2,1)} %copy.179), calls=%async_computation.3 | async-start | bytes 4194304 | tf_op jit(solution)/shard_map/all_to_all | solution.py:260
  432.9 0.7 copy-start.23
  435.4 7.0 %copy-start.10 = (f32[32,26,384]{2,0,1:T(8,128)S(1)}, f32[32,26,384]{2,0,1:T(8,128)}, u32[]{:S(2)}) copy-start(f32[32,26,384]{2,0,1:T(8,128)} %copy-done.9) | copy-start | bytes 3833860
  435.4 7.0 %copy-start.12 = (f32[32,26,384]{2,0,1:T(8,128)S(1)}, f32[32,26,384]{2,0,1:T(8,128)}, u32[]{:S(2)}) copy-start(f32[32,26,384]{2,0,1:T(8,128)} %copy-done.11) | copy-start | bytes 3833860
  489.2 2.5 copy-start.17
  491.8 11.5 %collective-permute-start.6 = (bf16[96,1024]{1,0:T(8,128)(2,1)S(1)}, bf16[96,1024]{1,0:T(8,128)(2,1)S(1)}, u32[]{:S(2)}, u32[]{:S(2)}) collective-permute-start(bf16[96,1024]{1,0:T(8,128)(2,1)S(1)} %fusion.80), channel_id=1, source_target_pairs={{0,193},{1,192},{64,1},{65,0},{128,65},{129,64},{192,129},{193,128... | collective-permute-start | bytes 589832 | tf_op jit(solution)/shard_map/ppermute | solution.py:147
  494.2 11.6 %collective-permute-start.5 = (bf16[96,1024]{1,0:T(8,128)(2,1)S(1)}, bf16[96,1024]{1,0:T(8,128)(2,1)S(1)}, u32[]{:S(2)}, u32[]{:S(2)}) collective-permute-start(bf16[96,1024]{1,0:T(8,128)(2,1)S(1)} %fusion.80), channel_id=1, source_target_pairs={{64,0},{128,64},{192,128},{0,192},{65,1},{129,65},{193,129},{1,193... | collective-permute-start | bytes 589832 | tf_op jit(solution)/shard_map/ppermute | solution.py:19
  495.1 11.6 %copy-start.1 = (bf16[1,96,2048]{2,1,0:T(8,128)(2,1)S(1)}, bf16[1,96,2048]{2,1,0:T(8,128)(2,1)}, u32[]{:S(2)}) copy-start(bf16[1,96,2048]{2,1,0:T(8,128)(2,1)} %param.13) | copy-start | bytes 1179652

commit v6 on v5

--- a/solution.py
+++ b/solution.py
@@ -127,16 +127,16 @@
     return counted / jnp.sum(counted, -1, keepdims=True)
 
 
-def slot_table(positions, choices_per):
-    slots = jnp.arange(EXPERTS * MOST, dtype=jnp.int32)
+def slot_table(positions, choices_per, depth=MOST):
+    slots = jnp.arange(EXPERTS * depth, dtype=jnp.int32)
     return slots[:, None, None] == positions.reshape(-1, choices_per)[None, :, :]
 
 
-def packed_rows(rows, table, scale=None):
-    chosen = jnp.any(table, -1).reshape(EXPERTS, MOST, -1)
+def packed_rows(rows, table, scale=None, depth=MOST):
+    chosen = jnp.any(table, -1).reshape(EXPERTS, depth, -1)
     picked = jnp.einsum("ecm,md->ecd", chosen.astype(rows.dtype), rows, preferred_element_type=jnp.float32)
     if scale is not None:
-        picked = picked * jnp.sum(jnp.where(table, scale[None], 0.0), (1, 2)).reshape(EXPERTS, MOST, 1)
+        picked = picked * jnp.sum(jnp.where(table, scale[None], 0.0), (1, 2)).reshape(EXPERTS, depth, 1)
     return picked.astype(rows.dtype)
 
 
@@ -208,39 +208,35 @@
 
     fwd_flat, fwd_rank = slot_ranks(fwd_routes[0])
     back_flat, back_rank = slot_ranks(bwd_routes[0])
-    fwd_positions = fwd_flat * MOST + fwd_rank
     back_positions = back_flat * MOST + back_rank
     mixing = combine_weights(fwd_numer[0])
     back_mixing = combine_weights(bwd_numer[0])
     unit_weights = jnp.ones_like(back_mixing)
-    fwd_table = slot_table(fwd_positions, choices_per)
     back_table = slot_table(back_positions, choices_per)
-    send_inputs = packed_rows(inputs, fwd_table)
-    (recv_inputs,), swapped_in = exchange(
-        (send_inputs,),
-        (
-            lax.dynamic_slice_in_dim(down_half[0], theirs, half, 1),
-            lax.dynamic_slice_in_dim(gate_half[0], theirs, half, 0),
-            lax.dynamic_slice_in_dim(up_half[0], theirs, half, 0),
-        ),
-        0,
-    )
-    recv_inputs = recv_inputs.reshape(groups, 1, MOST, model_width)
-    down_recv, gate_recv, up_recv = (x[None] for x in swapped_in)
-    down_mine = jnp.concatenate([lax.dynamic_slice_in_dim(down_half, mine, half, 2), down_recv], 1)
-    gate_mine = jnp.concatenate([lax.dynamic_slice_in_dim(gate_half, mine, half, 1), gate_recv], 2)
-    up_mine = jnp.concatenate([lax.dynamic_slice_in_dim(up_half, mine, half, 1), up_recv], 2)
-    send_saved = packed_rows(saved, back_table).reshape(groups, 1, MOST, model_width)
-    send_grad = packed_rows(grad_in, back_table, back_mixing).reshape(groups, 1, MOST, model_width)
-    recv_inputs, send_saved, send_grad = lax.optimization_barrier((recv_inputs, send_saved, send_grad))
-    recv_saved = lax.all_to_all(send_saved, "expert", split_axis=0, concat_axis=0, tiled=True)
-    recv_grad = lax.all_to_all(send_grad, "expert", split_axis=0, concat_axis=0, tiled=True)
-
-    gate_value, up_value = project(recv_inputs, gate_half, up_half)
+    send_saved = packed_rows(saved, back_table)
+    send_grad = packed_rows(grad_in, back_table, back_mixing)
+    (recv_saved, recv_grad), (gate_other, up_other, down_other) = exchange(
+        (send_saved, send_grad), (gate_half[0], up_half[0], down_half[0]), 0
+    )
+    recv_saved, recv_grad = (x.reshape(groups, 1, MOST, model_width) for x in (recv_saved, recv_grad))
+    gate_full = jnp.concatenate([gate_half[0], gate_other], 1)
+    up_full = jnp.concatenate([up_half[0], up_other], 1)
+    down_full = jnp.concatenate([down_half[0], down_other], 0)
+    gate_mine = lax.dynamic_slice_in_dim(gate_full, mine, half, 0)[None]
+    up_mine = lax.dynamic_slice_in_dim(up_full, mine, half, 0)[None]
+
+    share = MOST // 2
+    side = lax.axis_index("dp")
+    fwd_mine = (fwd_rank >= share).astype(jnp.int32) == side
+    fwd_local = jnp.where(fwd_mine, fwd_flat * share + fwd_rank - side * share, -1)
+    fwd_table = slot_table(fwd_local, choices_per, share)
+    send_inputs = packed_rows(inputs, fwd_table, depth=share)
+    recv_inputs = lax.all_to_all(send_inputs, "expert", split_axis=0, concat_axis=0, tiled=True)
+    gate_value = jnp.einsum("smd,df->smf", recv_inputs, gate_full, preferred_element_type=jnp.float32)
+    up_value = jnp.einsum("smd,df->smf", recv_inputs, up_full, preferred_element_type=jnp.float32)
     hidden = (jax.nn.silu(gate_value) * up_value).astype(jnp.bfloat16)
-    hidden_all = jnp.concatenate([hidden, swapped(hidden)], -1)
-    out_part = jnp.einsum(
-        "semf,efd->semd", hidden_all, down_mine, preferred_element_type=jnp.float32
+    out_rows = jnp.einsum(
+        "smf,fd->smd", hidden, down_full, preferred_element_type=jnp.float32
     ).astype(jnp.bfloat16)
 
     back_gate, back_up = project(recv_saved, gate_half, up_half)
@@ -248,21 +244,29 @@
     gate_term, up_term, down_term = weight_terms(
         recv_saved, recv_grad, back_hidden, gate_grad, up_grad
     )
-    gate_other, up_other = swapped((gate_grad, up_grad))
-    gate_all = jnp.concatenate([gate_grad, gate_other], -1)
-    up_all = jnp.concatenate([up_grad, up_other], -1)
+    gate_swap, up_swap = swapped((gate_grad, up_grad))
+    gate_all = jnp.concatenate([gate_grad, gate_swap], -1)
+    up_all = jnp.concatenate([up_grad, up_swap], -1)
     grad_part = (
         jnp.einsum("semf,edf->semd", gate_all, gate_mine, preferred_element_type=jnp.float32)
         + jnp.einsum("semf,edf->semd", up_all, up_mine, preferred_element_type=jnp.float32)
     ).astype(jnp.bfloat16)
 
-    back_out = lax.all_to_all(out_part, "expert", split_axis=0, concat_axis=0, tiled=True)
+    back_out = lax.all_to_all(out_rows, "expert", split_axis=0, concat_axis=0, tiled=True)
+    picked = back_out.reshape(-1, model_width)[jnp.maximum(fwd_local, 0)].reshape(-1, choices_per, model_width)
+    weights = jnp.where(fwd_mine, mixing.reshape(-1), 0.0).reshape(-1, choices_per)
+    partial = jnp.sum(weights[:, :, None] * picked.astype(jnp.float32), 1)
+    partial_other = swapped(partial)
+    first = side == 0
+    layer_out = (
+        (inputs.astype(jnp.float32) + jnp.where(first, partial, partial_other))
+        + jnp.where(first, partial_other, partial)
+    ).astype(jnp.bfloat16)
+    next_fwd = passed_along(layer_out, "section", 1)[None]
+
     back_grad = lax.all_to_all(grad_part, "expert", split_axis=0, concat_axis=0, tiled=True)
-    inputs_part = lax.dynamic_slice_in_dim(inputs, mine, half, 1)
     grad_in_part = lax.dynamic_slice_in_dim(grad_in, mine, half, 1)
-    layer_out = mix_rows(inputs_part, back_out, fwd_positions, mixing, choices_per)
     input_grad = mix_rows(grad_in_part, back_grad, back_positions, unit_weights, choices_per)
-    next_fwd = handoff(layer_out, 1)[None]
     next_bwd = handoff(input_grad, -1)[None]
     gate_sum = gate_term.astype(jnp.bfloat16)
     up_sum = up_term.astype(jnp.bfloat16)

time: 516 us -> 447 us (0.87)
  the two profiles are of different devices: /device:TPU:6 before, /device:TPU:8 now
where the time goes in v6:
time: 447 us; the launch traced here: 439 us
  Pallas kernels  224 us (50%)
  waiting for transfers between devices  66.8 us (15%)
  matrix products  51 us (11%)
  starting transfers between devices  40.2 us (9%)
  local copies, waits for them, and re-layouts  38.1 us (9%)
  other arithmetic  17.1 us (4%)
    pallas_call x1, Pallas kernels, exchange(): pl.pallas_call(functools.partial(exchange_kernel, n, len(sends), len(swap...  224 us
    all_to_all x1, waiting for transfers between devices, local(): lax.all_to_all(out_rows, 'expert', split_axis=0, concat_axis=0, tiled=True)  32.6 us
    all_to_all x1, waiting for transfers between devices, local(): lax.all_to_all(grad_part, 'expert', split_axis=0, concat_axis=0, tiled=True)  24.2 us
    all_to_all x1, starting transfers between devices, local(): lax.all_to_all(out_rows, 'expert', split_axis=0, concat_axis=0, tiled=True)  12.3 us
    all_to_all x1, starting transfers between devices, local(): lax.all_to_all(send_inputs, 'expert', split_axis=0, concat_axis=0, tiled=...  10.2 us
  transfers between devices with their start and end apart: 9, of which 4 were waited for; matrix products, arithmetic and copies ran while one was open for 21% of the time, Pallas kernels for 51%

profile of v6, /device:TPU:8, one launch (start us, length us, event | category | flops | bytes accessed | tf_op | source)
XLA Modules:
  0.0 438.6 jit_solution(9675272207832292508)
XLA Ops:
  1.7 1.7 reduce-window.14
  4.7 1.6 convolution_convert_fusion.1
  6.3 2.3 copy.135
  8.6 10.2 %all-to-all-start = ((bf16[32,13,2048]{2,1,0:T(8,128)(2,1)}), bf16[32,13,2048]{2,1,0:T(8,128)(2,1)S(1)}, u32[]{:S(2)}, u32[]{:S(2)}) async-start(bf16[32,13,2048]{2,1,0:T(8,128)(2,1)} %copy.135), calls=%async_computation | async-start | bytes 4194304 | tf_op jit(solution)/shard_map/all_to_all | solution.py:234
  19.2 1.7 reduce-window.16
  21.4 0.9 fusion.11
  23.3 1.0 convolution_convert_fusion
  24.4 3.9 copy.145.refs_0_
  28.3 3.2 multiply_convert_fusion.refs_1_
  31.5 224.2 %shard_map.137 = (bf16[32,26,2048]{2,1,0:T(8,128)(2,1)}, bf16[32,26,2048]{2,1,0:T(8,128)(2,1)}, bf16[2048,384]{1,0:T(8,128)(2,1)}, bf16[2048,384]{1,0:T(8,128)(2,1)}, bf16[384,2048]{1,0:T(8,128)(2,1)}) custom-call(bf16[32,26,2048]{2,1,0:T(8,128)(2,1)} %copy.145.refs_0_, bf16[32,26,2048]{2,1,0:T(8,128)(2,1)} %multiply_convert_fusion.refs_1_, ...), custom_call_target="tpu_custom_call" | custom-call | bytes 23068672 | tf_op jit(solution)/shard_map/pallas_call | solution.py:98
  255.7 5.1 %fusion.22 = f32[32,26,384]{2,1,0:T(8,128)S(1)} fusion(bf16[32,26,2048]{2,1,0:T(8,128)(2,1)} %get-tuple-element.14, bf16[1,1,2048,384]{3,2,1,0:T(8,128)(2,1)} %param.17), kind=kOutput, calls=%fused_computation.40 | convolution fusion | flops 1308622848 | bytes 6258688 | tf_op jit(solution)/shard_map/semd,edf->semf/dot_general | solution.py:153
  260.9 2.3 fusion.24
  264.1 2.8 fusion.32
  266.9 0.9 copy-done.3
  267.8 1.1 copy.152
  268.9 2.3 collective-permute-start.3
  271.2 1.1 copy.149
  272.2 1.5 collective-permute-start.2
  273.7 5.5 %fusion.5 = f32[32,13,768]{2,0,1:T(8,128)} fusion(bf16[2048,384]{1,0:T(8,128)(2,1)} %get-tuple-element.10, bf16[2048,384]{1,0:T(8,128)(2,1)} %bitcast.216, bf16[32,13,2048]{2,1,0:T(8,128)(2,1)S(1)} %all-to-all-done), kind=kOutput, calls=%fused_computation.16 | convolution fusion | flops 1314914304 | bytes 6127616 | tf_op jit(solution)/shard_map/smd,df->smf/dot_general | solution.py:235
  279.2 8.2 %fusion.10 = bf16[32,13,2048]{2,0,1:T(8,128)(2,1)} fusion(bf16[384,2048]{1,0:T(8,128)(2,1)} %get-tuple-element.12, bf16[384,2048]{1,0:T(8,128)(2,1)} %bitcast.214, bf16[2048,384]{1,0:T(8,128)(2,1)} %get-tuple-element.11, bf16[2048,384]{1,0:T(8,128)(2,1)} %bitcast.219, bf16[32,13,2048]{2,1,0:T(8,128)(2,1)S(1)} %all-to-all-done, f32[32,13,768]{2,0,1:T(8,128)} %fusion.5), kind=kOutput, calls=%fused_computation.25 | convolution fusion | flops 2632597504 | bytes 10977280 | tf_op jit(solution)/shard_map/smf,fd->smd/dot_general | solution.py:238
  287.4 3.7 copy.148
  291.1 12.3 %all-to-all-start.1 = ((bf16[32,13,2048]{2,1,0:T(8,128)(2,1)}), bf16[32,13,2048]{2,1,0:T(8,128)(2,1)S(1)}, u32[]{:S(2)}, u32[]{:S(2)}) async-start(bf16[32,13,2048]{2,1,0:T(8,128)(2,1)} %copy.148), calls=%async_computation.1 | async-start | bytes 4194304 | tf_op jit(solution)/shard_map/all_to_all | solution.py:255
  303.4 6.2 %fusion.14 = bf16[1,1,384,2048]{3,2,1,0:T(8,128)(2,1)} fusion(bf16[32,26,2048]{2,1,0:T(8,128)(2,1)} %get-tuple-element.13, f32[32,26,384]{2,1,0:T(8,128)} %copy-done.20, f32[32,26,384]{2,1,0:T(8,128)} %copy-done.19), kind=kOutput, calls=%fused_computation.32 | convolution fusion | flops 1311326208 | bytes 7536640 | tf_op jit(solution)/shard_map/semf,semd->efd/dot_general | solution.py:177
  310.2 1.3 copy.153
  311.5 1.3 copy.150
  313.3 1.2 copy-done.6
  315.0 1.7 fusion.20
  316.9 1.7 fusion.38
  318.6 2.4 copy.155
  320.9 32.6 %all-to-all-done.1 = bf16[32,13,2048]{2,1,0:T(8,128)(2,1)S(1)} async-done(((bf16[32,13,2048]{2,1,0:T(8,128)(2,1)}), bf16[32,13,2048]{2,1,0:T(8,128)(2,1)S(1)}, u32[]{:S(2)}, u32[]{:S(2)}) %all-to-all-start.1) | async-done | bytes 1703968 | tf_op jit(solution)/shard_map/all_to_all | solution.py:255
  353.6 1.3 copy-done.2
  354.9 5.1 %all-to-all-start.2 = ((bf16[32,1,26,1024]{3,2,1,0:T(8,128)(2,1)}), bf16[32,1,26,1024]{3,2,1,0:T(8,128)(2,1)}, u32[]{:S(2)}, u32[]{:S(2)}) async-start(bf16[32,1,26,1024]{3,2,1,0:T(8,128)(2,1)} %copy.155), calls=%async_computation.2 | async-start | bytes 4194304 | tf_op jit(solution)/shard_map/all_to_all | solution.py:267
  360.0 5.9 %fusion.13 = bf16[1,1,2048,384]{3,2,1,0:T(8,128)(2,1)} fusion(bf16[32,26,2048]{2,1,0:T(8,128)(2,1)} %get-tuple-element.14, bf16[32,1,26,384]{3,2,0,1:T(8,128)(2,1)} %copy-done.3), kind=kOutput, calls=%fused_computation.31 | convolution fusion | flops 1309409280 | bytes 5619712 | tf_op jit(solution)/shard_map/semd,semf->edf/dot_general | solution.py:176
  365.9 1.8 reshape.253
  367.8 4.3 gather_fusion
  372.0 5.7 %fusion = f32[96,2048]{1,0:T(8,128)} fusion(bf16[768,2048]{1,0:T(8,128)(2,1)} %gather_fusion, f32[96,8]{1,0:T(8,128)S(1)} %fusion.74), kind=kLoop, calls=%fused_computation.4 | loop fusion | flops 4521984 | bytes 3935232 | tf_op jit(solution)/shard_map/reduce_sum | solution.py:258
  377.8 2.2 collective-permute-start
  380.0 5.7 %fusion.12 = bf16[1,1,2048,384]{3,2,1,0:T(8,128)(2,1)} fusion(bf16[32,26,2048]{2,1,0:T(8,128)(2,1)} %get-tuple-element.14, bf16[32,1,26,384]{3,2,0,1:T(8,128)(2,1)S(1)} %get-tuple-element.16), kind=kOutput, calls=%fused_computation.30 | convolution fusion | flops 1309409280 | bytes 5619712 | tf_op jit(solution)/shard_map/semd,semf->edf/dot_general | solution.py:173
  385.8 24.2 %all-to-all-done.2 = bf16[32,1,26,1024]{3,2,1,0:T(8,128)(2,1)} async-done(((bf16[32,1,26,1024]{3,2,1,0:T(8,128)(2,1)}), bf16[32,1,26,1024]{3,2,1,0:T(8,128)(2,1)}, u32[]{:S(2)}, u32[]{:S(2)}) %all-to-all-start.2) | async-done | bytes 1703968 | tf_op jit(solution)/shard_map/all_to_all | solution.py:267
  410.1 2.5 reshape.256
  412.6 3.6 gather_fusion.1
  416.2 2.5 convert_reduce_fusion
  418.8 2.9 collective-permute-start.4
  421.7 2.6 collective-permute-start.5
  424.3 1.6 add_convert_fusion.1
  425.9 1.1 collective-permute-start.1
  427.0 5.1 %collective-permute-done.5 = bf16[96,1024]{1,0:T(8,128)(2,1)S(1)} collective-permute-done((bf16[96,1024]{1,0:T(8,128)(2,1)S(1)}, bf16[96,1024]{1,0:T(8,128)(2,1)S(1)}, u32[]{:S(2)}, u32[]{:S(2)}) %collective-permute-start.5) | collective-permute-done | bytes 196640 | tf_op jit(solution)/shard_map/ppermute | solution.py:147
  432.9 4.8 %collective-permute-done.1 = bf16[96,2048]{1,0:T(8,128)(2,1)S(1)} collective-permute-done((bf16[96,2048]{1,0:T(8,128)(2,1)S(1)}, bf16[96,2048]{1,0:T(8,128)(2,1)S(1)}, u32[]{:S(2)}, u32[]{:S(2)}) %collective-permute-start.1) | collective-permute-done | bytes 393248 | tf_op jit(solution)/shard_map/ppermute | solution.py:19
  (89 shorter events, 8.3 us)
Async XLA Ops:
  0.6 22.7 %copy-start = (bf16[1,96,2048]{2,1,0:T(8,128)(2,1)S(1)}, bf16[1,96,2048]{2,1,0:T(8,128)(2,1)}, u32[]{:S(2)}) copy-start(bf16[1,96,2048]{2,1,0:T(8,128)(2,1)} %param.13) | copy-start | bytes 1179652
  8.6 10.2 %copy-start.13 = (s32[1,96,8]{1,2,0:T(8,128)S(1)}, s32[1,96,8]{1,2,0:T(8,128)}, u32[]{:S(2)}) copy-start(s32[1,96,8]{1,2,0:T(8,128)} %param.14) | copy-start | bytes 9220
  8.6 14.0 %copy-start.12 = (s32[1,96,8]{1,2,0:T(8,128)S(1)}, s32[1,96,8]{1,2,0:T(8,128)}, u32[]{:S(2)}) copy-start(s32[1,96,8]{1,2,0:T(8,128)} %param.15) | copy-start | bytes 9220
  8.6 265.1 %all-to-all-start = ((bf16[32,13,2048]{2,1,0:T(8,128)(2,1)}), bf16[32,13,2048]{2,1,0:T(8,128)(2,1)S(1)}, u32[]{:S(2)}, u32[]{:S(2)}) async-start(bf16[32,13,2048]{2,1,0:T(8,128)(2,1)} %copy.135), calls=%async_computation | async-start | bytes 4194304 | tf_op jit(solution)/shard_map/all_to_all | solution.py:234
  24.4 3.9 copy-start.10
  255.6 5.2 %copy-start.7 = (bf16[1,1,2048,384]{3,2,1,0:T(8,128)(2,1)S(1)}, bf16[1,1,2048,384]{3,2,1,0:T(8,128)(2,1)}, u32[]{:S(2)}) copy-start(bf16[1,1,2048,384]{3,2,1,0:T(8,128)(2,1)} %param.18) | copy-start | bytes 4718596
  255.7 5.2 %copy-start.15 = (bf16[32,26,2048]{2,1,0:T(8,128)(2,1)S(1)}, bf16[32,26,2048]{2,1,0:T(8,128)(2,1)}, u32[]{:S(2)}) copy-start(bf16[32,26,2048]{2,1,0:T(8,128)(2,1)} %get-tuple-element.14) | copy-start | bytes 10223620
  260.8 2.4 copy-start.19
  260.8 2.4 copy-start.5
  260.9 3.2 copy-start.16
  263.2 3.7 copy-start.20
  266.9 0.9 copy-start.3
  268.9 41.3 %collective-permute-start.3 = (bf16[32,1,26,384]{3,0,2,1:T(8,128)(2,1)}, bf16[32,1,26,384]{3,0,2,1:T(8,128)(2,1)}, u32[]{:S(2)}, u32[]{:S(2)}) collective-permute-start(bf16[32,1,26,384]{3,0,2,1:T(8,128)(2,1)} %copy.152), channel_id=1, source_target_pairs={{0,1},{1,0},{2,3},{3,2},{4,5},{5,4},{6,7},{7,6},{8,9},{9,8},{10,11... | collective-permute-start | bytes 1916936 | tf_op jit(solution)/shard_map/ppermute | solution.py:23
  272.2 39.3 %collective-permute-start.2 = (bf16[32,1,26,384]{3,0,2,1:T(8,128)(2,1)}, bf16[32,1,26,384]{3,0,2,1:T(8,128)(2,1)}, u32[]{:S(2)}, u32[]{:S(2)}) collective-permute-start(bf16[32,1,26,384]{3,0,2,1:T(8,128)(2,1)} %copy.149), channel_id=1, source_target_pairs={{0,1},{1,0},{2,3},{3,2},{4,5},{5,4},{6,7},{7,6},{8,9},{9,8},{10,11... | collective-permute-start | bytes 1916936 | tf_op jit(solution)/shard_map/ppermute | solution.py:23
  291.1 62.5 %all-to-all-start.1 = ((bf16[32,13,2048]{2,1,0:T(8,128)(2,1)}), bf16[32,13,2048]{2,1,0:T(8,128)(2,1)S(1)}, u32[]{:S(2)}, u32[]{:S(2)}) async-start(bf16[32,13,2048]{2,1,0:T(8,128)(2,1)} %copy.148), calls=%async_computation.1 | async-start | bytes 4194304 | tf_op jit(solution)/shard_map/all_to_all | solution.py:255
  303.4 6.4 %copy-start.14 = (s32[1,96,8]{1,2,0:T(8,128)S(1)}, s32[1,96,8]{1,2,0:T(8,128)}, u32[]{:S(2)}) copy-start(s32[1,96,8]{1,2,0:T(8,128)} %param.12) | copy-start | bytes 9220
  309.9 2.9 copy-start.4
  313.1 1.4 copy-start.6
  313.1 1.9 copy-start.18
  315.0 1.7 copy-start.8
  315.0 1.9 copy-start.17
  353.6 1.3 copy-start.2
  354.9 55.2 %all-to-all-start.2 = ((bf16[32,1,26,1024]{3,2,1,0:T(8,128)(2,1)}), bf16[32,1,26,1024]{3,2,1,0:T(8,128)(2,1)}, u32[]{:S(2)}, u32[]{:S(2)}) async-start(bf16[32,1,26,1024]{3,2,1,0:T(8,128)(2,1)} %copy.155), calls=%async_computation.2 | async-start | bytes 4194304 | tf_op jit(solution)/shard_map/all_to_all | solution.py:267
  377.8 46.5 %collective-permute-start = (f32[96,2048]{1,0:T(8,128)}, f32[96,2048]{1,0:T(8,128)}, u32[]{:S(2)}, u32[]{:S(2)}) collective-permute-start(f32[96,2048]{1,0:T(8,128)} %fusion), channel_id=1, source_target_pairs={{0,1},{1,0},{2,3},{3,2},{4,5},{5,4},{6,7},{7,6},{8,9},{9,8},{10,11... | collective-permute-start | bytes 2359304 | tf_op jit(solution)/shard_map/ppermute | solution.py:23
  416.2 2.5 copy-start.11
  416.2 8.1 %copy-start.9 = (bf16[1,96,2048]{2,1,0:T(8,128)(2,1)S(1)}, bf16[1,96,2048]{2,1,0:T(8,128)(2,1)}, u32[]{:S(2)}) copy-start(bf16[1,96,2048]{2,1,0:T(8,128)(2,1)} %param.10) | copy-start | bytes 1179652
  418.8 8.2 %collective-permute-start.4 = (bf16[96,1024]{1,0:T(8,128)(2,1)S(1)}, bf16[96,1024]{1,0:T(8,128)(2,1)S(1)}, u32[]{:S(2)}, u32[]{:S(2)}) collective-permute-start(bf16[96,1024]{1,0:T(8,128)(2,1)S(1)} %fusion.61), channel_id=1, source_target_pairs={{64,0},{128,64},{192,128},{0,192},{65,1},{129,65},{193,129},{1,193... | collective-permute-start | bytes 589832 | tf_op jit(solution)/shard_map/ppermute | solution.py:19
  421.7 10.3 %collective-permute-start.5 = (bf16[96,1024]{1,0:T(8,128)(2,1)S(1)}, bf16[96,1024]{1,0:T(8,128)(2,1)S(1)}, u32[]{:S(2)}, u32[]{:S(2)}) collective-permute-start(bf16[96,1024]{1,0:T(8,128)(2,1)S(1)} %fusion.61), channel_id=1, source_target_pairs={{0,193},{1,192},{64,1},{65,0},{128,65},{129,64},{192,129},{193,128... | collective-permute-start | bytes 589832 | tf_op jit(solution)/shard_map/ppermute | solution.py:147
  424.3 14.1 %copy-start.1 = (bf16[1,96,2048]{2,1,0:T(8,128)(2,1)S(1)}, bf16[1,96,2048]{2,1,0:T(8,128)(2,1)}, u32[]{:S(2)}) copy-start(bf16[1,96,2048]{2,1,0:T(8,128)(2,1)} %param.13) | copy-start | bytes 1179652
  425.9 11.8 %collective-permute-start.1 = (bf16[96,2048]{1,0:T(8,128)(2,1)S(1)}, bf16[96,2048]{1,0:T(8,128)(2,1)S(1)}, u32[]{:S(2)}, u32[]{:S(2)}) collective-permute-start(bf16[96,2048]{1,0:T(8,128)(2,1)S(1)} %add_convert_fusion.1), channel_id=1, source_target_pairs={{192,0},{0,64},{64,128},{128,192},{193,1},{1,65},{65,129},{129,193... | collective-permute-start | bytes 1179656 | tf_op jit(solution)/shard_map/ppermute | solution.py:19

commit v7 on v6

--- a/solution.py
+++ b/solution.py
@@ -222,8 +222,6 @@
     gate_full = jnp.concatenate([gate_half[0], gate_other], 1)
     up_full = jnp.concatenate([up_half[0], up_other], 1)
     down_full = jnp.concatenate([down_half[0], down_other], 0)
-    gate_mine = lax.dynamic_slice_in_dim(gate_full, mine, half, 0)[None]
-    up_mine = lax.dynamic_slice_in_dim(up_full, mine, half, 0)[None]
 
     share = MOST // 2
     side = lax.axis_index("dp")
@@ -244,30 +242,48 @@
     gate_term, up_term, down_term = weight_terms(
         recv_saved, recv_grad, back_hidden, gate_grad, up_grad
     )
-    gate_swap, up_swap = swapped((gate_grad, up_grad))
-    gate_all = jnp.concatenate([gate_grad, gate_swap], -1)
-    up_all = jnp.concatenate([up_grad, up_swap], -1)
-    grad_part = (
-        jnp.einsum("semf,edf->semd", gate_all, gate_mine, preferred_element_type=jnp.float32)
-        + jnp.einsum("semf,edf->semd", up_all, up_mine, preferred_element_type=jnp.float32)
+    saved_share = lax.dynamic_slice_in_dim(recv_saved[:, 0], side * share, share, 1)
+    grad_share = lax.dynamic_slice_in_dim(recv_grad[:, 0], side * share, share, 1)
+    other_gate = jnp.einsum("smd,df->smf", saved_share, gate_other, preferred_element_type=jnp.float32)
+    other_up = jnp.einsum("smd,df->smf", saved_share, up_other, preferred_element_type=jnp.float32)
+    _, other_gate_grad, other_up_grad = local_backward(
+        other_gate[:, None], other_up[:, None], grad_share[:, None], down_other[None]
+    )
+    gate_share = jnp.concatenate(
+        [lax.dynamic_slice_in_dim(gate_grad[:, 0], side * share, share, 1), other_gate_grad[:, 0]], -1
+    )
+    up_share = jnp.concatenate(
+        [lax.dynamic_slice_in_dim(up_grad[:, 0], side * share, share, 1), other_up_grad[:, 0]], -1
+    )
+    grad_rows = (
+        jnp.einsum("smf,df->smd", gate_share, gate_full, preferred_element_type=jnp.float32)
+        + jnp.einsum("smf,df->smd", up_share, up_full, preferred_element_type=jnp.float32)
     ).astype(jnp.bfloat16)
 
     back_out = lax.all_to_all(out_rows, "expert", split_axis=0, concat_axis=0, tiled=True)
     picked = back_out.reshape(-1, model_width)[jnp.maximum(fwd_local, 0)].reshape(-1, choices_per, model_width)
     weights = jnp.where(fwd_mine, mixing.reshape(-1), 0.0).reshape(-1, choices_per)
     partial = jnp.sum(weights[:, :, None] * picked.astype(jnp.float32), 1)
-    partial_other = swapped(partial)
+
+    back_grad = lax.all_to_all(grad_rows, "expert", split_axis=0, concat_axis=0, tiled=True)
+    back_mine = (back_rank >= share).astype(jnp.int32) == side
+    back_local = jnp.where(back_mine, back_flat * share + back_rank - side * share, 0)
+    picked_grad = back_grad.reshape(-1, model_width)[back_local].reshape(-1, choices_per, model_width)
+    grad_partial = jnp.sum(
+        jnp.where(back_mine.reshape(-1, choices_per)[:, :, None], picked_grad.astype(jnp.float32), 0.0), 1
+    )
+    partial_other, grad_partial_other = swapped((partial, grad_partial))
     first = side == 0
     layer_out = (
         (inputs.astype(jnp.float32) + jnp.where(first, partial, partial_other))
         + jnp.where(first, partial_other, partial)
     ).astype(jnp.bfloat16)
+    input_grad = (
+        (grad_in.astype(jnp.float32) + jnp.where(first, grad_partial, grad_partial_other))
+        + jnp.where(first, grad_partial_other, grad_partial)
+    ).astype(jnp.bfloat16)
     next_fwd = passed_along(layer_out, "section", 1)[None]
-
-    back_grad = lax.all_to_all(grad_part, "expert", split_axis=0, concat_axis=0, tiled=True)
-    grad_in_part = lax.dynamic_slice_in_dim(grad_in, mine, half, 1)
-    input_grad = mix_rows(grad_in_part, back_grad, back_positions, unit_weights, choices_per)
-    next_bwd = handoff(input_grad, -1)[None]
+    next_bwd = passed_along(input_grad, "section", -1)[None]
     gate_sum = gate_term.astype(jnp.bfloat16)
     up_sum = up_term.astype(jnp.bfloat16)
     down_sum = down_term.astype(jnp.bfloat16)

time: 447 us -> 462 us (1.034)
  waiting for transfers between devices: 66.8 us -> 76.7 us
  matrix products: 51 us -> 60.8 us
    ppermute x3 -> x2, waiting for transfers between devices: 0.01 us -> 9 us  [swapped(): return lax.ppermute(block, 'dp', [(0, 1), (1, 0)])]
    all_to_all x1, starting transfers between devices: 5.08 us -> 12.7 us  [local(): lax.all_to_all(grad_rows, 'expert', split_axis=0, concat_axis=0, tiled=True)]
    all_to_all x1, waiting for transfers between devices: 24.2 us -> 31.7 us  [local(): lax.all_to_all(grad_rows, 'expert', split_axis=0, concat_axis=0, tiled=True)]
    all_to_all x1, starting transfers between devices: 12.3 us -> 5.31 us  [local(): lax.all_to_all(out_rows, 'expert', split_axis=0, concat_axis=0, tiled=True)]
    ppermute x1 -> x0, waiting for transfers between devices: 5.06 us -> none  [handoff(): crossed = lax.ppermute(value, ('section', 'dp'), route)]
    dot_general x1 -> x2, matrix products: 2.8 us -> 7.83 us  [local_backward(): jnp.einsum('semd,efd->semf', grad_rows, down_weight, preferred_element_ty...]
  transfers between devices with their start and end apart: 9 -> 7, of which waited for: 4 -> 4; matrix products, arithmetic and copies ran while one was open for 21% -> 23% of each run, Pallas kernels for 51% -> 49%
where the time goes in v7:
time: 462 us; the launch traced here: 454 us
  Pallas kernels  224 us (48%)
  waiting for transfers between devices  76.7 us (17%)
  matrix products  60.8 us (13%)
  starting transfers between devices  36.3 us (8%)
  local copies, waits for them, and re-layouts  35.9 us (8%)
  other arithmetic  18.7 us (4%)
    pallas_call x1, Pallas kernels, exchange(): pl.pallas_call(functools.partial(exchange_kernel, n, len(sends), len(swap...  224 us
    all_to_all x1, waiting for transfers between devices, local(): lax.all_to_all(grad_rows, 'expert', split_axis=0, concat_axis=0, tiled=True)  31.7 us
    all_to_all x1, waiting for transfers between devices, local(): lax.all_to_all(out_rows, 'expert', split_axis=0, concat_axis=0, tiled=True)  30.5 us
    all_to_all x1, starting transfers between devices, local(): lax.all_to_all(grad_rows, 'expert', split_axis=0, concat_axis=0, tiled=True)  12.7 us
    all_to_all x1, starting transfers between devices, local(): lax.all_to_all(send_inputs, 'expert', split_axis=0, concat_axis=0, tiled=...  10.2 us
  transfers between devices with their start and end apart: 7, of which 4 were waited for; matrix products, arithmetic and copies ran while one was open for 23% of the time, Pallas kernels for 49%

profile of v7, /device:TPU:8, one launch (start us, length us, event | category | flops | bytes accessed | tf_op | source)
XLA Modules:
  0.0 453.9 jit_solution(18101399755989549582)
XLA Ops:
  0.7 0.8 copy.141
  1.7 1.7 reduce-window.14
  4.7 1.6 convolution_convert_fusion.1
  6.3 2.3 copy.148
  8.6 10.2 %all-to-all-start = ((bf16[32,13,2048]{2,1,0:T(8,128)(2,1)}), bf16[32,13,2048]{2,1,0:T(8,128)(2,1)S(1)}, u32[]{:S(2)}, u32[]{:S(2)}) async-start(bf16[32,13,2048]{2,1,0:T(8,128)(2,1)} %copy.148), calls=%async_computation | async-start | bytes 4194304 | tf_op jit(solution)/shard_map/all_to_all | solution.py:232
  19.2 1.7 reduce-window.16
  21.6 0.9 fusion.6
  22.8 1.0 convolution_convert_fusion
  23.9 3.9 copy.159.refs_0_
  28.5 3.2 multiply_convert_fusion.refs_1_
  31.7 224.1 %shard_map.137 = (bf16[32,26,2048]{2,1,0:T(8,128)(2,1)}, bf16[32,26,2048]{2,1,0:T(8,128)(2,1)}, bf16[2048,384]{1,0:T(8,128)(2,1)}, bf16[2048,384]{1,0:T(8,128)(2,1)}, bf16[384,2048]{1,0:T(8,128)(2,1)}) custom-call(bf16[32,26,2048]{2,1,0:T(8,128)(2,1)} %copy.159.refs_0_, bf16[32,26,2048]{2,1,0:T(8,128)(2,1)} %multiply_convert_fusion.refs_1_, ...), custom_call_target="tpu_custom_call" | custom-call | bytes 23068672 | tf_op jit(solution)/shard_map/pallas_call | solution.py:98
  255.8 6.3 %fusion.15 = f32[32,26,384]{2,1,0:T(8,128)} fusion(bf16[32,26,2048]{2,1,0:T(8,128)(2,1)} %get-tuple-element.14, bf16[1,1,2048,384]{3,2,1,0:T(8,128)(2,1)} %param.17), kind=kOutput, calls=%fused_computation.31 | convolution fusion | flops 1308622848 | bytes 6258688 | tf_op jit(solution)/shard_map/semd,edf->semf/dot_general | solution.py:153
  262.1 3.5 fusion.17
  265.5 6.5 %fusion.25 = (bf16[32,1,26,384]{3,2,0,1:T(8,128)(2,1)S(1)}, bf16[32,1,26,384]{3,2,0,1:T(8,128)(2,1)S(1)}) fusion(f32[32,26,384]{2,1,0:T(8,128)} %fusion.15, f32[32,26,384]{2,1,0:T(8,128)} %fusion.17, bf16[32,26,2048]{2,1,0:T(8,128)(2,1)} %get-tuple-element.13, bf16[1,1,384,2048]{3,2,1,0:T(8,128)(2,1)} %param.19), kind=kOutput, calls=%fused_computation.44 | convolution fusion | flops 1312776192 | bytes 8814592 | tf_op jit(solution)/shard_map/semd,efd->semf/dot_general | solution.py:162
  273.3 2.4 constant_dynamic-slice_fusion.1
  275.7 1.3 fusion.47
  277.1 1.3 fusion.26
  278.6 1.5 fusion.72
  280.0 1.7 fusion.11
  282.0 1.5 add_convert_fusion
  283.5 2.3 copy.168
  285.8 1.4 copy-done.3
  287.2 12.7 %all-to-all-start.2 = ((bf16[32,13,2048]{2,1,0:T(8,128)(2,1)}), bf16[32,13,2048]{2,1,0:T(8,128)(2,1)S(1)}, u32[]{:S(2)}, u32[]{:S(2)}) async-start(bf16[32,13,2048]{2,1,0:T(8,128)(2,1)} %copy.168), calls=%async_computation.2 | async-start | bytes 4194304 | tf_op jit(solution)/shard_map/all_to_all | solution.py:268
  300.0 5.9 %fusion.12 = f32[32,13,768]{2,0,1:T(8,128)} fusion(bf16[2048,384]{1,0:T(8,128)(2,1)} %get-tuple-element.10, bf16[2048,384]{1,0:T(8,128)(2,1)} %bitcast.256, bf16[32,13,2048]{2,1,0:T(8,128)(2,1)} %copy-done.3), kind=kOutput, calls=%fused_computation.28 | convolution fusion | flops 1314914304 | bytes 6127616 | tf_op jit(solution)/shard_map/smd,df->smf/dot_general | solution.py:233
  305.9 8.8 %fusion.5 = bf16[32,13,2048]{2,0,1:T(8,128)(2,1)} fusion(bf16[384,2048]{1,0:T(8,128)(2,1)} %get-tuple-element.12, bf16[384,2048]{1,0:T(8,128)(2,1)} %bitcast.262, bf16[2048,384]{1,0:T(8,128)(2,1)} %get-tuple-element.11, bf16[2048,384]{1,0:T(8,128)(2,1)} %bitcast.259, bf16[32,13,2048]{2,1,0:T(8,128)(2,1)} %copy-done.3, f32[32,13,768]{2,0,1:T(8,128)} %fusion.12), kind=kOutput, calls=%fused_computation.18 | convolution fusion | flops 2632597504 | bytes 10977280 | tf_op jit(solution)/shard_map/smf,fd->smd/dot_general | solution.py:236
  314.7 3.8 copy.162
  318.5 31.7 %all-to-all-done.2 = bf16[32,13,2048]{2,1,0:T(8,128)(2,1)S(1)} async-done(((bf16[32,13,2048]{2,1,0:T(8,128)(2,1)}), bf16[32,13,2048]{2,1,0:T(8,128)(2,1)S(1)}, u32[]{:S(2)}, u32[]{:S(2)}) %all-to-all-start.2) | async-done | bytes 1703968 | tf_op jit(solution)/shard_map/all_to_all | solution.py:268
  350.2 1.4 copy-done.2
  351.5 5.3 %all-to-all-start.1 = ((bf16[32,13,2048]{2,1,0:T(8,128)(2,1)}), bf16[32,13,2048]{2,1,0:T(8,128)(2,1)}, u32[]{:S(2)}, u32[]{:S(2)}) async-start(bf16[32,13,2048]{2,1,0:T(8,128)(2,1)} %copy.162), calls=%async_computation.1 | async-start | bytes 4194304 | tf_op jit(solution)/shard_map/all_to_all | solution.py:263
  357.6 6.2 %fusion.9 = bf16[1,1,384,2048]{3,2,1,0:T(8,128)(2,1)} fusion(bf16[32,26,2048]{2,1,0:T(8,128)(2,1)} %get-tuple-element.13, f32[32,26,384]{2,1,0:T(8,128)} %fusion.17, f32[32,26,384]{2,1,0:T(8,128)} %fusion.15), kind=kOutput, calls=%fused_computation.25 | convolution fusion | flops 1311326208 | bytes 7536640 | tf_op jit(solution)/shard_map/semf,semd->efd/dot_general | solution.py:177
  363.8 1.8 reshape.279
  365.7 4.3 gather_fusion.1
  369.9 4.9 %fusion = f32[96,2048]{1,0:T(8,128)S(1)} fusion(bf16[768,2048]{1,0:T(8,128)(2,1)} %gather_fusion.1, pred[96,8]{1,0:T(8,128)(4,1)S(1)} %eq.171), kind=kLoop, calls=%fused_computation.4 | loop fusion | flops 4521984 | bytes 3932928 | tf_op jit(solution)/shard_map/reduce_sum | solution.py:272
  374.9 1.6 collective-permute-start.2
  376.5 30.5 %all-to-all-done.1 = bf16[32,13,2048]{2,1,0:T(8,128)(2,1)} async-done(((bf16[32,13,2048]{2,1,0:T(8,128)(2,1)}), bf16[32,13,2048]{2,1,0:T(8,128)(2,1)}, u32[]{:S(2)}, u32[]{:S(2)}) %all-to-all-start.1) | async-done | bytes 1703968 | tf_op jit(solution)/shard_map/all_to_all | solution.py:263
  407.0 1.8 reshape.278
  408.8 4.3 gather_fusion
  413.1 4.9 %fusion.1 = f32[96,2048]{1,0:T(8,128)S(1)} fusion(bf16[768,2048]{1,0:T(8,128)(2,1)} %gather_fusion, f32[96,8]{1,0:T(8,128)S(1)} %fusion.105), kind=kLoop, calls=%fused_computation.6 | loop fusion | flops 4521984 | bytes 3935232 | tf_op jit(solution)/shard_map/reduce_sum | solution.py:266
  418.0 1.8 collective-permute-start
  419.8 5.7 %fusion.7 = bf16[1,1,2048,384]{3,2,1,0:T(8,128)(2,1)} fusion(bf16[32,26,2048]{2,1,0:T(8,128)(2,1)} %get-tuple-element.14, bf16[32,1,26,384]{3,2,0,1:T(8,128)(2,1)S(1)} %copy-done.15), kind=kOutput, calls=%fused_computation.23 | convolution fusion | flops 1309409280 | bytes 5619712 | tf_op jit(solution)/shard_map/semd,semf->edf/dot_general | solution.py:173
  425.5 1.4 add_convert_fusion.1
  426.9 3.5 collective-permute-start.3
  430.4 9.0 %collective-permute-done = f32[96,2048]{1,0:T(8,128)} collective-permute-done((f32[96,2048]{1,0:T(8,128)S(1)}, f32[96,2048]{1,0:T(8,128)}, u32[]{:S(2)}, u32[]{:S(2)}) %collective-permute-start) | collective-permute-done | bytes 786464 | tf_op jit(solution)/shard_map/ppermute | solution.py:23
  439.4 1.3 add_convert_fusion.2
  440.7 1.2 collective-permute-start.1
  441.9 4.8 %fusion.8 = bf16[1,1,2048,384]{3,2,1,0:T(8,128)(2,1)} fusion(bf16[32,26,2048]{2,1,0:T(8,128)(2,1)S(1)} %copy-done.11, bf16[32,1,26,384]{3,2,0,1:T(8,128)(2,1)} %copy-done.13), kind=kOutput, calls=%fused_computation.24 | convolution fusion | flops 1309409280 | bytes 5619712 | tf_op jit(solution)/shard_map/semd,semf->edf/dot_general | solution.py:176
  446.7 5.5 %collective-permute-done.1 = bf16[96,2048]{1,0:T(8,128)(2,1)S(1)} collective-permute-done((bf16[96,2048]{1,0:T(8,128)(2,1)S(1)}, bf16[96,2048]{1,0:T(8,128)(2,1)S(1)}, u32[]{:S(2)}, u32[]{:S(2)}) %collective-permute-start.1) | collective-permute-done | bytes 393248 | tf_op jit(solution)/shard_map/ppermute | solution.py:19
  452.2 0.7 copy.212
  (93 shorter events, 6.4 us)
Async XLA Ops:
  0.6 22.2 %copy-start = (bf16[1,96,2048]{2,1,0:T(8,128)(2,1)S(1)}, bf16[1,96,2048]{2,1,0:T(8,128)(2,1)}, u32[]{:S(2)}) copy-start(bf16[1,96,2048]{2,1,0:T(8,128)(2,1)} %param.13) | copy-start | bytes 1179652
  8.6 10.2 %copy-start.17 = (s32[1,96,8]{1,2,0:T(8,128)S(1)}, s32[1,96,8]{1,2,0:T(8,128)}, u32[]{:S(2)}) copy-start(s32[1,96,8]{1,2,0:T(8,128)} %param.14) | copy-start | bytes 9220
  8.6 277.1 %all-to-all-start = ((bf16[32,13,2048]{2,1,0:T(8,128)(2,1)}), bf16[32,13,2048]{2,1,0:T(8,128)(2,1)S(1)}, u32[]{:S(2)}, u32[]{:S(2)}) async-start(bf16[32,13,2048]{2,1,0:T(8,128)(2,1)} %copy.148), calls=%async_computation | async-start | bytes 4194304 | tf_op jit(solution)/shard_map/all_to_all | solution.py:232
  23.9 3.9 copy-start.16
  23.9 4.6 %copy-start.7 = (bf16[1,96,2048]{2,1,0:T(8,128)(2,1)S(1)}, bf16[1,96,2048]{2,1,0:T(8,128)(2,1)}, u32[]{:S(2)}) copy-start(bf16[1,96,2048]{2,1,0:T(8,128)(2,1)} %param.16) | copy-start | bytes 1179652
  255.7 6.3 %copy-start.5 = (bf16[1,1,2048,384]{3,2,1,0:T(8,128)(2,1)S(1)}, bf16[1,1,2048,384]{3,2,1,0:T(8,128)(2,1)}, u32[]{:S(2)}) copy-start(bf16[1,1,2048,384]{3,2,1,0:T(8,128)(2,1)} %param.18) | copy-start | bytes 4718596
  255.8 6.3 %copy-start.9 = (bf16[32,26,2048]{2,1,0:T(8,128)(2,1)S(1)}, bf16[32,26,2048]{2,1,0:T(8,128)(2,1)}, u32[]{:S(2)}) copy-start(bf16[32,26,2048]{2,1,0:T(8,128)(2,1)} %get-tuple-element.14) | copy-start | bytes 10223620
  265.5 7.8 %copy-start.10 = (bf16[32,26,2048]{2,1,0:T(8,128)(2,1)S(1)}, bf16[32,26,2048]{2,1,0:T(8,128)(2,1)}, u32[]{:S(2)}) copy-start(bf16[32,26,2048]{2,1,0:T(8,128)(2,1)} %get-tuple-element.14) | copy-start | bytes 10223620
  265.5 7.8 %copy-start.12 = (bf16[32,26,2048]{2,1,0:T(8,128)(2,1)S(1)}, bf16[32,26,2048]{2,1,0:T(8,128)(2,1)}, u32[]{:S(2)}) copy-start(bf16[32,26,2048]{2,1,0:T(8,128)(2,1)} %get-tuple-element.13) | copy-start | bytes 10223620
  272.1 0.9 copy-start.13
  272.1 1.2 copy-start.14
  273.3 2.4 copy-start.20
  275.7 1.4 copy-start.21
  277.1 1.4 copy-start.19
  278.5 1.5 copy-start.4
  280.0 1.9 copy-start.6
  285.8 1.4 copy-start.3
  287.2 63.0 %all-to-all-start.2 = ((bf16[32,13,2048]{2,1,0:T(8,128)(2,1)}), bf16[32,13,2048]{2,1,0:T(8,128)(2,1)S(1)}, u32[]{:S(2)}, u32[]{:S(2)}) async-start(bf16[32,13,2048]{2,1,0:T(8,128)(2,1)} %copy.168), calls=%async_computation.2 | async-start | bytes 4194304 | tf_op jit(solution)/shard_map/all_to_all | solution.py:268
  318.5 38.5 %copy-start.18 = (s32[1,96,8]{1,2,0:T(8,128)S(1)}, s32[1,96,8]{1,2,0:T(8,128)}, u32[]{:S(2)}) copy-start(s32[1,96,8]{1,2,0:T(8,128)} %param.12) | copy-start | bytes 9220
  350.2 1.4 copy-start.2
  351.5 55.4 %all-to-all-start.1 = ((bf16[32,13,2048]{2,1,0:T(8,128)(2,1)}), bf16[32,13,2048]{2,1,0:T(8,128)(2,1)}, u32[]{:S(2)}, u32[]{:S(2)}) async-start(bf16[32,13,2048]{2,1,0:T(8,128)(2,1)} %copy.162), calls=%async_computation.1 | async-start | bytes 4194304 | tf_op jit(solution)/shard_map/all_to_all | solution.py:263
  374.9 50.6 %collective-permute-start.2 = (f32[96,2048]{1,0:T(8,128)S(1)}, f32[96,2048]{1,0:T(8,128)}, u32[]{:S(2)}, u32[]{:S(2)}) collective-permute-start(f32[96,2048]{1,0:T(8,128)S(1)} %fusion), channel_id=1, source_target_pairs={{0,1},{1,0},{2,3},{3,2},{4,5},{5,4},{6,7},{7,6},{8,9},{9,8},{10,11... | collective-permute-start | bytes 2359304 | tf_op jit(solution)/shard_map/ppermute | solution.py:23
  413.1 6.7 %copy-start.15 = (bf16[32,1,26,384]{3,2,0,1:T(8,128)(2,1)S(1)}, bf16[32,1,26,384]{3,2,0,1:T(8,128)(2,1)}, u32[]{:S(2)}) copy-start(bf16[32,1,26,384]{3,2,0,1:T(8,128)(2,1)} %copy-done.14) | copy-start | bytes 1916932
  418.0 21.4 %collective-permute-start = (f32[96,2048]{1,0:T(8,128)S(1)}, f32[96,2048]{1,0:T(8,128)}, u32[]{:S(2)}, u32[]{:S(2)}) collective-permute-start(f32[96,2048]{1,0:T(8,128)S(1)} %fusion.1), channel_id=1, source_target_pairs={{0,1},{1,0},{2,3},{3,2},{4,5},{5,4},{6,7},{7,6},{8,9},{9,8},{10,11... | collective-permute-start | bytes 2359304 | tf_op jit(solution)/shard_map/ppermute | solution.py:23
  425.5 13.9 %copy-start.8 = (bf16[1,96,2048]{2,1,0:T(8,128)(2,1)S(1)}, bf16[1,96,2048]{2,1,0:T(8,128)(2,1)}, u32[]{:S(2)}) copy-start(bf16[1,96,2048]{2,1,0:T(8,128)(2,1)} %param.10) | copy-start | bytes 1179652
  425.5 16.4 %copy-start.11 = (bf16[32,26,2048]{2,1,0:T(8,128)(2,1)S(1)}, bf16[32,26,2048]{2,1,0:T(8,128)(2,1)}, u32[]{:S(2)}) copy-start(bf16[32,26,2048]{2,1,0:T(8,128)(2,1)} %get-tuple-element.14) | copy-start | bytes 10223620
  426.9 19.7 %collective-permute-start.3 = (bf16[96,2048]{1,0:T(8,128)(2,1)S(1)}, bf16[96,2048]{1,0:T(8,128)(2,1)S(1)}, u32[]{:S(2)}, u32[]{:S(2)}) collective-permute-start(bf16[96,2048]{1,0:T(8,128)(2,1)S(1)} %add_convert_fusion.1), channel_id=1, source_target_pairs={{64,0},{128,64},{192,128},{0,192},{65,1},{129,65},{193,129},{1,193... | collective-permute-start | bytes 1179656 | tf_op jit(solution)/shard_map/ppermute | solution.py:19
  440.7 11.5 %collective-permute-start.1 = (bf16[96,2048]{1,0:T(8,128)(2,1)S(1)}, bf16[96,2048]{1,0:T(8,128)(2,1)S(1)}, u32[]{:S(2)}, u32[]{:S(2)}) collective-permute-start(bf16[96,2048]{1,0:T(8,128)(2,1)S(1)} %add_convert_fusion.2), channel_id=1, source_target_pairs={{192,0},{0,64},{64,128},{128,192},{193,1},{1,65},{65,129},{129,193... | collective-permute-start | bytes 1179656 | tf_op jit(solution)/shard_map/ppermute | solution.py:19
  441.9 11.8 %copy-start.1 = (bf16[1,96,2048]{2,1,0:T(8,128)(2,1)S(1)}, bf16[1,96,2048]{2,1,0:T(8,128)(2,1)}, u32[]{:S(2)}) copy-start(bf16[1,96,2048]{2,1,0:T(8,128)(2,1)} %param.13) | copy-start | bytes 1179652

commit v8 on v7

--- a/solution.py
+++ b/solution.py
@@ -237,6 +237,8 @@
         "smf,fd->smd", hidden, down_full, preferred_element_type=jnp.float32
     ).astype(jnp.bfloat16)
 
+    out_rows, recv_saved, recv_grad = lax.optimization_barrier((out_rows, recv_saved, recv_grad))
+    back_out = lax.all_to_all(out_rows, "expert", split_axis=0, concat_axis=0, tiled=True)
     back_gate, back_up = project(recv_saved, gate_half, up_half)
     back_hidden, gate_grad, up_grad = local_backward(back_gate, back_up, recv_grad, down_half)
     gate_term, up_term, down_term = weight_terms(
@@ -260,7 +262,6 @@
         + jnp.einsum("smf,df->smd", up_share, up_full, preferred_element_type=jnp.float32)
     ).astype(jnp.bfloat16)
 
-    back_out = lax.all_to_all(out_rows, "expert", split_axis=0, concat_axis=0, tiled=True)
     picked = back_out.reshape(-1, model_width)[jnp.maximum(fwd_local, 0)].reshape(-1, choices_per, model_width)
     weights = jnp.where(fwd_mine, mixing.reshape(-1), 0.0).reshape(-1, choices_per)
     partial = jnp.sum(weights[:, :, None] * picked.astype(jnp.float32), 1)

time: 462 us -> 454 us (0.983)
    all_to_all x1, starting transfers between devices: 5.31 us -> 13 us  [local(): lax.all_to_all(out_rows, 'expert', split_axis=0, concat_axis=0, tiled=True)]
    all_to_all x1, starting transfers between devices: 12.7 us -> 5.13 us  [local(): lax.all_to_all(grad_rows, 'expert', split_axis=0, concat_axis=0, tiled=True)]
  transfers between devices with their start and end apart: 7 -> 7, of which waited for: 4 -> 4; matrix products, arithmetic and copies ran while one was open for 23% -> 16% of each run, Pallas kernels for 49% -> 50%
where the time goes in v8:
time: 454 us; the launch traced here: 446 us
  Pallas kernels  224 us (49%)
  waiting for transfers between devices  74.3 us (16%)
  matrix products  58.5 us (13%)
  starting transfers between devices  37.1 us (8%)
  local copies, waits for them, and re-layouts  33.1 us (7%)
  other arithmetic  17.6 us (4%)
    pallas_call x1, Pallas kernels, exchange(): pl.pallas_call(functools.partial(exchange_kernel, n, len(sends), len(swap...  224 us
    all_to_all x1, waiting for transfers between devices, local(): lax.all_to_all(grad_rows, 'expert', split_axis=0, concat_axis=0, tiled=True)  30 us
    all_to_all x1, waiting for transfers between devices, local(): lax.all_to_all(out_rows, 'expert', split_axis=0, concat_axis=0, tiled=True)  29.9 us
    all_to_all x1, starting transfers between devices, local(): lax.all_to_all(out_rows, 'expert', split_axis=0, concat_axis=0, tiled=True)  13 us
    all_to_all x1, starting transfers between devices, local(): lax.all_to_all(send_inputs, 'expert', split_axis=0, concat_axis=0, tiled=...  10.2 us
    ppermute x2, waiting for transfers between devices, swapped(): return lax.ppermute(block, 'dp', [(0, 1), (1, 0)])  10.2 us
  transfers between devices with their start and end apart: 7, of which 4 were waited for; matrix products, arithmetic and copies ran while one was open for 16% of the time, Pallas kernels for 50%

profile of v8, /device:TPU:8, one launch (start us, length us, event | category | flops | bytes accessed | tf_op | source)
XLA Modules:
  0.0 445.7 jit_solution(16351237670602902493)
XLA Ops:
  0.7 0.8 copy.134
  1.7 1.7 reduce-window.14
  4.0 0.6 fusion.59
  4.7 1.6 convolution_convert_fusion.1
  6.3 2.3 copy.141
  8.6 10.2 %all-to-all-start = ((bf16[32,13,2048]{2,1,0:T(8,128)(2,1)}), bf16[32,13,2048]{2,1,0:T(8,128)(2,1)S(1)}, u32[]{:S(2)}, u32[]{:S(2)}) async-start(bf16[32,13,2048]{2,1,0:T(8,128)(2,1)} %copy.141), calls=%async_computation | async-start | bytes 4194304 | tf_op jit(solution)/shard_map/all_to_all | solution.py:232
  19.2 1.7 reduce-window.16
  21.6 0.9 fusion.24
  22.8 1.0 convolution_convert_fusion
  23.9 3.9 copy.152.refs_0_
  28.6 3.2 multiply_convert_fusion.refs_1_
  31.8 223.7 %shard_map.137 = (bf16[32,26,2048]{2,1,0:T(8,128)(2,1)}, bf16[32,26,2048]{2,1,0:T(8,128)(2,1)}, bf16[2048,384]{1,0:T(8,128)(2,1)}, bf16[2048,384]{1,0:T(8,128)(2,1)}, bf16[384,2048]{1,0:T(8,128)(2,1)}) custom-call(bf16[32,26,2048]{2,1,0:T(8,128)(2,1)} %copy.152.refs_0_, bf16[32,26,2048]{2,1,0:T(8,128)(2,1)} %multiply_convert_fusion.refs_1_, ...), custom_call_target="tpu_custom_call" | custom-call | bytes 23068672 | tf_op jit(solution)/shard_map/pallas_call | solution.py:98
  255.5 5.5 %fusion.36 = f32[32,13,768]{2,0,1:T(8,128)} fusion(bf16[2048,384]{1,0:T(8,128)(2,1)} %get-tuple-element.13, bf16[2048,384]{1,0:T(8,128)(2,1)} %bitcast.304, bf16[32,13,2048]{2,1,0:T(8,128)(2,1)S(1)} %all-to-all-done), kind=kOutput, calls=%fused_computation.40 | convolution fusion | flops 1314914304 | bytes 6127616 | tf_op jit(solution)/shard_map/smd,df->smf/dot_general | solution.py:233
  260.9 8.2 %fusion.23 = bf16[32,13,2048]{2,0,1:T(8,128)(2,1)} fusion(bf16[384,2048]{1,0:T(8,128)(2,1)} %get-tuple-element.15, bf16[384,2048]{1,0:T(8,128)(2,1)} %bitcast.302, bf16[2048,384]{1,0:T(8,128)(2,1)} %get-tuple-element.14, bf16[2048,384]{1,0:T(8,128)(2,1)} %bitcast.307, bf16[32,13,2048]{2,1,0:T(8,128)(2,1)S(1)} %all-to-all-done, f32[32,13,768]{2,0,1:T(8,128)} %fusion.36), kind=kOutput, calls=%fused_computation.30 | convolution fusion | flops 2632597504 | bytes 10977280 | tf_op jit(solution)/shard_map/smf,fd->smd/dot_general | solution.py:236
  269.1 6.3 %fusion.6 = f32[32,26,384]{2,1,0:T(8,128)} fusion(bf16[32,1,26,2048]{3,2,0,1:T(8,128)(2,1)} %bitcast.309, bf16[1,1,2048,384]{3,2,1,0:T(8,128)(2,1)} %param.17), kind=kOutput, calls=%fused_computation.11 | convolution fusion | flops 1308622848 | bytes 6258688 | tf_op jit(solution)/shard_map/semd,edf->semf/dot_general | solution.py:153
  275.4 3.5 fusion.8
  278.9 2.2 copy.155
  281.2 13.0 %all-to-all-start.1 = ((bf16[32,13,2048]{2,1,0:T(8,128)(2,1)}), bf16[32,13,2048]{2,1,0:T(8,128)(2,1)S(1)}, u32[]{:S(2)}, u32[]{:S(2)}) async-start(bf16[32,13,2048]{2,1,0:T(8,128)(2,1)} %copy.155), calls=%async_computation.1 | async-start | bytes 4194304 | tf_op jit(solution)/shard_map/all_to_all | solution.py:241
  294.2 6.5 %fusion.51 = (bf16[32,1,26,384]{3,2,0,1:T(8,128)(2,1)S(1)}, bf16[32,1,26,384]{3,2,0,1:T(8,128)(2,1)S(1)}) fusion(f32[32,26,384]{2,1,0:T(8,128)} %fusion.6, f32[32,26,384]{2,1,0:T(8,128)} %fusion.8, bf16[1,1,384,2048]{3,2,1,0:T(8,128)(2,1)} %param.19, bf16[32,1,26,2048]{3,2,0,1:T(8,128)(2,1)} %bitcast.314), kind=kOutput, calls=%fused_computation.58 | convolution fusion | flops 1312776192 | bytes 8814592 | tf_op jit(solution)/shard_map/semd,efd->semf/dot_general | solution.py:162
  302.0 2.4 constant_dynamic-slice_fusion.1
  304.4 1.3 fusion.66
  305.8 1.3 fusion.37
  307.2 1.5 fusion.96
  308.7 1.5 fusion.35
  310.4 1.6 add_convert_fusion
  312.0 2.3 copy.160
  314.3 29.9 %all-to-all-done.1 = bf16[32,13,2048]{2,1,0:T(8,128)(2,1)S(1)} async-done(((bf16[32,13,2048]{2,1,0:T(8,128)(2,1)}), bf16[32,13,2048]{2,1,0:T(8,128)(2,1)S(1)}, u32[]{:S(2)}, u32[]{:S(2)}) %all-to-all-start.1) | async-done | bytes 1703968 | tf_op jit(solution)/shard_map/all_to_all | solution.py:241
  344.3 1.4 copy-done.2
  345.6 5.1 %all-to-all-start.2 = ((bf16[32,13,2048]{2,1,0:T(8,128)(2,1)}), bf16[32,13,2048]{2,1,0:T(8,128)(2,1)}, u32[]{:S(2)}, u32[]{:S(2)}) async-start(bf16[32,13,2048]{2,1,0:T(8,128)(2,1)} %copy.160), calls=%async_computation.2 | async-start | bytes 4194304 | tf_op jit(solution)/shard_map/all_to_all | solution.py:269
  351.5 6.2 %fusion.31 = bf16[1,1,384,2048]{3,2,1,0:T(8,128)(2,1)} fusion(bf16[32,1,26,2048]{3,2,0,1:T(8,128)(2,1)} %bitcast.315, f32[32,26,384]{2,1,0:T(8,128)} %fusion.8, f32[32,26,384]{2,1,0:T(8,128)} %fusion.6), kind=kOutput, calls=%fused_computation.37 | convolution fusion | flops 1311326208 | bytes 7536640 | tf_op jit(solution)/shard_map/semf,semd->efd/dot_general | solution.py:177
  357.7 1.8 reshape.286
  359.6 4.3 gather_fusion
  363.8 4.8 %fusion.1 = f32[96,2048]{1,0:T(8,128)S(1)} fusion(bf16[768,2048]{1,0:T(8,128)(2,1)} %gather_fusion, f32[96,8]{1,0:T(8,128)S(1)} %fusion.129), kind=kLoop, calls=%fused_computation.6 | loop fusion | flops 4521984 | bytes 3935232 | tf_op jit(solution)/shard_map/reduce_sum | solution.py:267
  368.7 2.4 collective-permute-start
  371.1 30.0 %all-to-all-done.2 = bf16[32,13,2048]{2,1,0:T(8,128)(2,1)} async-done(((bf16[32,13,2048]{2,1,0:T(8,128)(2,1)}), bf16[32,13,2048]{2,1,0:T(8,128)(2,1)}, u32[]{:S(2)}, u32[]{:S(2)}) %all-to-all-start.2) | async-done | bytes 1703968 | tf_op jit(solution)/shard_map/all_to_all | solution.py:269
  401.1 1.8 reshape.290
  402.9 4.3 gather_fusion.1
  407.2 5.0 %fusion = f32[96,2048]{1,0:T(8,128)S(1)} fusion(bf16[768,2048]{1,0:T(8,128)(2,1)} %gather_fusion.1, pred[96,8]{1,0:T(8,128)(4,1)S(1)} %eq.171), kind=kLoop, calls=%fused_computation.4 | loop fusion | flops 4521984 | bytes 3932928 | tf_op jit(solution)/shard_map/reduce_sum | solution.py:273
  412.2 2.6 collective-permute-start.2
  414.8 5.8 %fusion.25 = bf16[1,1,2048,384]{3,2,1,0:T(8,128)(2,1)} fusion(bf16[32,1,26,2048]{3,2,0,1:T(8,128)(2,1)} %bitcast.310, bf16[32,1,26,384]{3,2,0,1:T(8,128)(2,1)S(1)} %copy-done.16), kind=kOutput, calls=%fused_computation.35 | convolution fusion | flops 1309409280 | bytes 5619712 | tf_op jit(solution)/shard_map/semd,semf->edf/dot_general | solution.py:173
  420.6 1.4 add_convert_fusion.2
  422.1 1.3 collective-permute-start.1
  423.4 10.1 %collective-permute-done.2 = f32[96,2048]{1,0:T(8,128)S(1)} collective-permute-done((f32[96,2048]{1,0:T(8,128)S(1)}, f32[96,2048]{1,0:T(8,128)S(1)}, u32[]{:S(2)}, u32[]{:S(2)}) %collective-permute-start.2) | collective-permute-done | bytes 786464 | tf_op jit(solution)/shard_map/ppermute | solution.py:23
  433.7 2.5 collective-permute-start.3
  436.2 3.6 fusion.28
  439.8 4.2 collective-permute-done.3
  444.0 0.7 copy.210
  444.7 0.7 copy.211
  (95 shorter events, 5.3 us)
Async XLA Ops:
  0.6 22.2 %copy-start = (bf16[1,96,2048]{2,1,0:T(8,128)(2,1)S(1)}, bf16[1,96,2048]{2,1,0:T(8,128)(2,1)}, u32[]{:S(2)}) copy-start(bf16[1,96,2048]{2,1,0:T(8,128)(2,1)} %param.13) | copy-start | bytes 1179652
  8.6 10.2 %copy-start.18 = (s32[1,96,8]{1,2,0:T(8,128)S(1)}, s32[1,96,8]{1,2,0:T(8,128)}, u32[]{:S(2)}) copy-start(s32[1,96,8]{1,2,0:T(8,128)} %param.14) | copy-start | bytes 9220
  8.6 246.8 %all-to-all-start = ((bf16[32,13,2048]{2,1,0:T(8,128)(2,1)}), bf16[32,13,2048]{2,1,0:T(8,128)(2,1)S(1)}, u32[]{:S(2)}, u32[]{:S(2)}) async-start(bf16[32,13,2048]{2,1,0:T(8,128)(2,1)} %copy.141), calls=%async_computation | async-start | bytes 4194304 | tf_op jit(solution)/shard_map/all_to_all | solution.py:232
  23.9 3.9 copy-start.17
  23.9 4.7 %copy-start.8 = (bf16[1,96,2048]{2,1,0:T(8,128)(2,1)S(1)}, bf16[1,96,2048]{2,1,0:T(8,128)(2,1)}, u32[]{:S(2)}) copy-start(bf16[1,96,2048]{2,1,0:T(8,128)(2,1)} %param.16) | copy-start | bytes 1179652
  269.1 6.3 %copy-start.5 = (bf16[1,1,2048,384]{3,2,1,0:T(8,128)(2,1)S(1)}, bf16[1,1,2048,384]{3,2,1,0:T(8,128)(2,1)}, u32[]{:S(2)}) copy-start(bf16[1,1,2048,384]{3,2,1,0:T(8,128)(2,1)} %param.18) | copy-start | bytes 4718596
  269.1 6.3 %copy-start.9 = (bf16[32,26,2048]{2,1,0:T(8,128)(2,1)S(1)}, bf16[32,26,2048]{2,1,0:T(8,128)(2,1)}, u32[]{:S(2)}) copy-start(bf16[32,26,2048]{2,1,0:T(8,128)(2,1)} %get-tuple-element.16) | copy-start | bytes 10223620
  275.4 3.5 copy-start.3
  281.2 63.1 %all-to-all-start.1 = ((bf16[32,13,2048]{2,1,0:T(8,128)(2,1)}), bf16[32,13,2048]{2,1,0:T(8,128)(2,1)S(1)}, u32[]{:S(2)}, u32[]{:S(2)}) async-start(bf16[32,13,2048]{2,1,0:T(8,128)(2,1)} %copy.155), calls=%async_computation.1 | async-start | bytes 4194304 | tf_op jit(solution)/shard_map/all_to_all | solution.py:241
  294.1 7.8 %copy-start.10 = (bf16[32,26,2048]{2,1,0:T(8,128)(2,1)S(1)}, bf16[32,26,2048]{2,1,0:T(8,128)(2,1)}, u32[]{:S(2)}) copy-start(bf16[32,26,2048]{2,1,0:T(8,128)(2,1)} %get-tuple-element.16) | copy-start | bytes 10223620
  294.1 7.8 %copy-start.12 = (bf16[32,26,2048]{2,1,0:T(8,128)(2,1)S(1)}, bf16[32,26,2048]{2,1,0:T(8,128)(2,1)}, u32[]{:S(2)}) copy-start(bf16[32,26,2048]{2,1,0:T(8,128)(2,1)} %get-tuple-element.17) | copy-start | bytes 10223620
  300.7 0.9 copy-start.13
  300.7 1.2 copy-start.15
  302.0 2.4 copy-start.22
  304.4 1.4 copy-start.21
  305.8 1.4 copy-start.20
  307.2 1.5 copy-start.4
  308.7 1.7 copy-start.6
  314.3 36.6 %copy-start.19 = (s32[1,96,8]{1,2,0:T(8,128)S(1)}, s32[1,96,8]{1,2,0:T(8,128)}, u32[]{:S(2)}) copy-start(s32[1,96,8]{1,2,0:T(8,128)} %param.12) | copy-start | bytes 9220
  344.3 1.4 copy-start.2
  345.6 55.4 %all-to-all-start.2 = ((bf16[32,13,2048]{2,1,0:T(8,128)(2,1)}), bf16[32,13,2048]{2,1,0:T(8,128)(2,1)}, u32[]{:S(2)}, u32[]{:S(2)}) async-start(bf16[32,13,2048]{2,1,0:T(8,128)(2,1)} %copy.160), calls=%async_computation.2 | async-start | bytes 4194304 | tf_op jit(solution)/shard_map/all_to_all | solution.py:269
  368.7 51.9 %collective-permute-start = (f32[96,2048]{1,0:T(8,128)S(1)}, f32[96,2048]{1,0:T(8,128)}, u32[]{:S(2)}, u32[]{:S(2)}) collective-permute-start(f32[96,2048]{1,0:T(8,128)S(1)} %fusion.1), channel_id=1, source_target_pairs={{0,1},{1,0},{2,3},{3,2},{4,5},{5,4},{6,7},{7,6},{8,9},{9,8},{10,11... | collective-permute-start | bytes 2359304 | tf_op jit(solution)/shard_map/ppermute | solution.py:23
  407.2 7.6 %copy-start.16 = (bf16[32,1,26,384]{3,2,0,1:T(8,128)(2,1)S(1)}, bf16[32,1,26,384]{3,2,0,1:T(8,128)(2,1)}, u32[]{:S(2)}) copy-start(bf16[32,1,26,384]{3,2,0,1:T(8,128)(2,1)} %copy-done.15) | copy-start | bytes 1916932
  412.2 8.4 %copy-start.7 = (bf16[1,96,2048]{2,1,0:T(8,128)(2,1)S(1)}, bf16[1,96,2048]{2,1,0:T(8,128)(2,1)}, u32[]{:S(2)}) copy-start(bf16[1,96,2048]{2,1,0:T(8,128)(2,1)} %param.10) | copy-start | bytes 1179652
  412.2 21.3 %collective-permute-start.2 = (f32[96,2048]{1,0:T(8,128)S(1)}, f32[96,2048]{1,0:T(8,128)S(1)}, u32[]{:S(2)}, u32[]{:S(2)}) collective-permute-start(f32[96,2048]{1,0:T(8,128)S(1)} %fusion), channel_id=1, source_target_pairs={{0,1},{1,0},{2,3},{3,2},{4,5},{5,4},{6,7},{7,6},{8,9},{9,8},{10,11... | collective-permute-start | bytes 2359304 | tf_op jit(solution)/shard_map/ppermute | solution.py:23
  414.8 21.4 %copy-start.14 = (bf16[32,1,26,384]{3,2,0,1:T(8,128)(2,1)S(1)}, bf16[32,1,26,384]{3,2,0,1:T(8,128)(2,1)}, u32[]{:S(2)}) copy-start(bf16[32,1,26,384]{3,2,0,1:T(8,128)(2,1)} %copy-done.13) | copy-start | bytes 1916932
  420.6 15.6 %copy-start.11 = (bf16[32,26,2048]{2,1,0:T(8,128)(2,1)S(1)}, bf16[32,26,2048]{2,1,0:T(8,128)(2,1)}, u32[]{:S(2)}) copy-start(bf16[32,26,2048]{2,1,0:T(8,128)(2,1)} %get-tuple-element.16) | copy-start | bytes 10223620
  422.1 17.7 %collective-permute-start.1 = (bf16[96,2048]{1,0:T(8,128)(2,1)S(1)}, bf16[96,2048]{1,0:T(8,128)(2,1)S(1)}, u32[]{:S(2)}, u32[]{:S(2)}) collective-permute-start(bf16[96,2048]{1,0:T(8,128)(2,1)S(1)} %add_convert_fusion.2), channel_id=1, source_target_pairs={{192,0},{0,64},{64,128},{128,192},{193,1},{1,65},{65,129},{129,193... | collective-permute-start | bytes 1179656 | tf_op jit(solution)/shard_map/ppermute | solution.py:19
  433.7 10.3 %collective-permute-start.3 = (bf16[96,2048]{1,0:T(8,128)(2,1)S(1)}, bf16[96,2048]{1,0:T(8,128)(2,1)S(1)}, u32[]{:S(2)}, u32[]{:S(2)}) collective-permute-start(bf16[96,2048]{1,0:T(8,128)(2,1)S(1)} %add_convert_fusion.1), channel_id=1, source_target_pairs={{64,0},{128,64},{192,128},{0,192},{65,1},{129,65},{193,129},{1,193... | collective-permute-start | bytes 1179656 | tf_op jit(solution)/shard_map/ppermute | solution.py:19
  436.2 9.3 %copy-start.1 = (bf16[1,96,2048]{2,1,0:T(8,128)(2,1)S(1)}, bf16[1,96,2048]{2,1,0:T(8,128)(2,1)}, u32[]{:S(2)}) copy-start(bf16[1,96,2048]{2,1,0:T(8,128)(2,1)} %param.13) | copy-start | bytes 1179652

commit v9 on v8

--- a/solution.py
+++ b/solution.py
@@ -265,6 +265,13 @@
     picked = back_out.reshape(-1, model_width)[jnp.maximum(fwd_local, 0)].reshape(-1, choices_per, model_width)
     weights = jnp.where(fwd_mine, mixing.reshape(-1), 0.0).reshape(-1, choices_per)
     partial = jnp.sum(weights[:, :, None] * picked.astype(jnp.float32), 1)
+    partial_other = swapped(partial)
+    first = side == 0
+    layer_out = (
+        (inputs.astype(jnp.float32) + jnp.where(first, partial, partial_other))
+        + jnp.where(first, partial_other, partial)
+    ).astype(jnp.bfloat16)
+    next_fwd = passed_along(layer_out, "section", 1)[None]
 
     back_grad = lax.all_to_all(grad_rows, "expert", split_axis=0, concat_axis=0, tiled=True)
     back_mine = (back_rank >= share).astype(jnp.int32) == side
@@ -273,17 +280,11 @@
     grad_partial = jnp.sum(
         jnp.where(back_mine.reshape(-1, choices_per)[:, :, None], picked_grad.astype(jnp.float32), 0.0), 1
     )
-    partial_other, grad_partial_other = swapped((partial, grad_partial))
-    first = side == 0
-    layer_out = (
-        (inputs.astype(jnp.float32) + jnp.where(first, partial, partial_other))
-        + jnp.where(first, partial_other, partial)
-    ).astype(jnp.bfloat16)
+    grad_partial_other = swapped(grad_partial)
     input_grad = (
         (grad_in.astype(jnp.float32) + jnp.where(first, grad_partial, grad_partial_other))
         + jnp.where(first, grad_partial_other, grad_partial)
     ).astype(jnp.bfloat16)
-    next_fwd = passed_along(layer_out, "section", 1)[None]
     next_bwd = passed_along(input_grad, "section", -1)[None]
     gate_sum = gate_term.astype(jnp.bfloat16)
     up_sum = up_term.astype(jnp.bfloat16)

time: 454 us -> 454 us (level)
  no operation moved by 1% of the time
where the time goes in v9:
time: 454 us; the launch traced here: 446 us
  Pallas kernels  224 us (49%)
  waiting for transfers between devices  74.3 us (16%)
  matrix products  58.5 us (13%)
  starting transfers between devices  37.1 us (8%)
  local copies, waits for them, and re-layouts  33.1 us (7%)
  other arithmetic  17.6 us (4%)
    pallas_call x1, Pallas kernels, exchange(): pl.pallas_call(functools.partial(exchange_kernel, n, len(sends), len(swap...  224 us
    all_to_all x1, waiting for transfers between devices, local(): lax.all_to_all(grad_rows, 'expert', split_axis=0, concat_axis=0, tiled=True)  30 us
    all_to_all x1, waiting for transfers between devices, local(): lax.all_to_all(out_rows, 'expert', split_axis=0, concat_axis=0, tiled=True)  29.9 us
    all_to_all x1, starting transfers between devices, local(): lax.all_to_all(out_rows, 'expert', split_axis=0, concat_axis=0, tiled=True)  13 us
    all_to_all x1, starting transfers between devices, local(): lax.all_to_all(send_inputs, 'expert', split_axis=0, concat_axis=0, tiled=...  10.2 us
    ppermute x2, waiting for transfers between devices, swapped(): return lax.ppermute(block, 'dp', [(0, 1), (1, 0)])  10.2 us
  transfers between devices with their start and end apart: 7, of which 4 were waited for; matrix products, arithmetic and copies ran while one was open for 16% of the time, Pallas kernels for 50%

profile of v9, /device:TPU:8, one launch (start us, length us, event | category | flops | bytes accessed | tf_op | source)
XLA Modules:
  0.0 445.7 jit_solution(16351237670602902493)
XLA Ops:
  0.7 0.8 copy.134
  1.7 1.7 reduce-window.14
  4.0 0.6 fusion.59
  4.7 1.6 convolution_convert_fusion.1
  6.3 2.3 copy.141
  8.6 10.2 %all-to-all-start = ((bf16[32,13,2048]{2,1,0:T(8,128)(2,1)}), bf16[32,13,2048]{2,1,0:T(8,128)(2,1)S(1)}, u32[]{:S(2)}, u32[]{:S(2)}) async-start(bf16[32,13,2048]{2,1,0:T(8,128)(2,1)} %copy.141), calls=%async_computation | async-start | bytes 4194304 | tf_op jit(solution)/shard_map/all_to_all | solution.py:232
  19.2 1.7 reduce-window.16
  21.6 0.9 fusion.24
  22.8 1.0 convolution_convert_fusion
  23.9 3.9 copy.152.refs_0_
  28.6 3.2 multiply_convert_fusion.refs_1_
  31.8 223.7 %shard_map.137 = (bf16[32,26,2048]{2,1,0:T(8,128)(2,1)}, bf16[32,26,2048]{2,1,0:T(8,128)(2,1)}, bf16[2048,384]{1,0:T(8,128)(2,1)}, bf16[2048,384]{1,0:T(8,128)(2,1)}, bf16[384,2048]{1,0:T(8,128)(2,1)}) custom-call(bf16[32,26,2048]{2,1,0:T(8,128)(2,1)} %copy.152.refs_0_, bf16[32,26,2048]{2,1,0:T(8,128)(2,1)} %multiply_convert_fusion.refs_1_, ...), custom_call_target="tpu_custom_call" | custom-call | bytes 23068672 | tf_op jit(solution)/shard_map/pallas_call | solution.py:98
  255.5 5.5 %fusion.36 = f32[32,13,768]{2,0,1:T(8,128)} fusion(bf16[2048,384]{1,0:T(8,128)(2,1)} %get-tuple-element.13, bf16[2048,384]{1,0:T(8,128)(2,1)} %bitcast.304, bf16[32,13,2048]{2,1,0:T(8,128)(2,1)S(1)} %all-to-all-done), kind=kOutput, calls=%fused_computation.40 | convolution fusion | flops 1314914304 | bytes 6127616 | tf_op jit(solution)/shard_map/smd,df->smf/dot_general | solution.py:233
  260.9 8.2 %fusion.23 = bf16[32,13,2048]{2,0,1:T(8,128)(2,1)} fusion(bf16[384,2048]{1,0:T(8,128)(2,1)} %get-tuple-element.15, bf16[384,2048]{1,0:T(8,128)(2,1)} %bitcast.302, bf16[2048,384]{1,0:T(8,128)(2,1)} %get-tuple-element.14, bf16[2048,384]{1,0:T(8,128)(2,1)} %bitcast.307, bf16[32,13,2048]{2,1,0:T(8,128)(2,1)S(1)} %all-to-all-done, f32[32,13,768]{2,0,1:T(8,128)} %fusion.36), kind=kOutput, calls=%fused_computation.30 | convolution fusion | flops 2632597504 | bytes 10977280 | tf_op jit(solution)/shard_map/smf,fd->smd/dot_general | solution.py:236
  269.1 6.3 %fusion.6 = f32[32,26,384]{2,1,0:T(8,128)} fusion(bf16[32,1,26,2048]{3,2,0,1:T(8,128)(2,1)} %bitcast.309, bf16[1,1,2048,384]{3,2,1,0:T(8,128)(2,1)} %param.17), kind=kOutput, calls=%fused_computation.11 | convolution fusion | flops 1308622848 | bytes 6258688 | tf_op jit(solution)/shard_map/semd,edf->semf/dot_general | solution.py:153
  275.4 3.5 fusion.8
  278.9 2.2 copy.155
  281.2 13.0 %all-to-all-start.1 = ((bf16[32,13,2048]{2,1,0:T(8,128)(2,1)}), bf16[32,13,2048]{2,1,0:T(8,128)(2,1)S(1)}, u32[]{:S(2)}, u32[]{:S(2)}) async-start(bf16[32,13,2048]{2,1,0:T(8,128)(2,1)} %copy.155), calls=%async_computation.1 | async-start | bytes 4194304 | tf_op jit(solution)/shard_map/all_to_all | solution.py:241
  294.2 6.5 %fusion.51 = (bf16[32,1,26,384]{3,2,0,1:T(8,128)(2,1)S(1)}, bf16[32,1,26,384]{3,2,0,1:T(8,128)(2,1)S(1)}) fusion(f32[32,26,384]{2,1,0:T(8,128)} %fusion.6, f32[32,26,384]{2,1,0:T(8,128)} %fusion.8, bf16[1,1,384,2048]{3,2,1,0:T(8,128)(2,1)} %param.19, bf16[32,1,26,2048]{3,2,0,1:T(8,128)(2,1)} %bitcast.314), kind=kOutput, calls=%fused_computation.58 | convolution fusion | flops 1312776192 | bytes 8814592 | tf_op jit(solution)/shard_map/semd,efd->semf/dot_general | solution.py:162
  302.0 2.4 constant_dynamic-slice_fusion.1
  304.4 1.3 fusion.66
  305.8 1.3 fusion.37
  307.2 1.5 fusion.96
  308.7 1.5 fusion.35
  310.4 1.6 add_convert_fusion
  312.0 2.3 copy.160
  314.3 29.9 %all-to-all-done.1 = bf16[32,13,2048]{2,1,0:T(8,128)(2,1)S(1)} async-done(((bf16[32,13,2048]{2,1,0:T(8,128)(2,1)}), bf16[32,13,2048]{2,1,0:T(8,128)(2,1)S(1)}, u32[]{:S(2)}, u32[]{:S(2)}) %all-to-all-start.1) | async-done | bytes 1703968 | tf_op jit(solution)/shard_map/all_to_all | solution.py:241
  344.3 1.4 copy-done.2
  345.6 5.1 %all-to-all-start.2 = ((bf16[32,13,2048]{2,1,0:T(8,128)(2,1)}), bf16[32,13,2048]{2,1,0:T(8,128)(2,1)}, u32[]{:S(2)}, u32[]{:S(2)}) async-start(bf16[32,13,2048]{2,1,0:T(8,128)(2,1)} %copy.160), calls=%async_computation.2 | async-start | bytes 4194304 | tf_op jit(solution)/shard_map/all_to_all | solution.py:276
  351.5 6.2 %fusion.31 = bf16[1,1,384,2048]{3,2,1,0:T(8,128)(2,1)} fusion(bf16[32,1,26,2048]{3,2,0,1:T(8,128)(2,1)} %bitcast.315, f32[32,26,384]{2,1,0:T(8,128)} %fusion.8, f32[32,26,384]{2,1,0:T(8,128)} %fusion.6), kind=kOutput, calls=%fused_computation.37 | convolution fusion | flops 1311326208 | bytes 7536640 | tf_op jit(solution)/shard_map/semf,semd->efd/dot_general | solution.py:177
  357.7 1.8 reshape.286
  359.6 4.3 gather_fusion
  363.8 4.8 %fusion.1 = f32[96,2048]{1,0:T(8,128)S(1)} fusion(bf16[768,2048]{1,0:T(8,128)(2,1)} %gather_fusion, f32[96,8]{1,0:T(8,128)S(1)} %fusion.129), kind=kLoop, calls=%fused_computation.6 | loop fusion | flops 4521984 | bytes 3935232 | tf_op jit(solution)/shard_map/reduce_sum | solution.py:267
  368.7 2.4 collective-permute-start
  371.1 30.0 %all-to-all-done.2 = bf16[32,13,2048]{2,1,0:T(8,128)(2,1)} async-done(((bf16[32,13,2048]{2,1,0:T(8,128)(2,1)}), bf16[32,13,2048]{2,1,0:T(8,128)(2,1)}, u32[]{:S(2)}, u32[]{:S(2)}) %all-to-all-start.2) | async-done | bytes 1703968 | tf_op jit(solution)/shard_map/all_to_all | solution.py:276
  401.1 1.8 reshape.290
  402.9 4.3 gather_fusion.1
  407.2 5.0 %fusion = f32[96,2048]{1,0:T(8,128)S(1)} fusion(bf16[768,2048]{1,0:T(8,128)(2,1)} %gather_fusion.1, pred[96,8]{1,0:T(8,128)(4,1)S(1)} %eq.171), kind=kLoop, calls=%fused_computation.4 | loop fusion | flops 4521984 | bytes 3932928 | tf_op jit(solution)/shard_map/reduce_sum | solution.py:280
  412.2 2.6 collective-permute-start.2
  414.8 5.8 %fusion.25 = bf16[1,1,2048,384]{3,2,1,0:T(8,128)(2,1)} fusion(bf16[32,1,26,2048]{3,2,0,1:T(8,128)(2,1)} %bitcast.310, bf16[32,1,26,384]{3,2,0,1:T(8,128)(2,1)S(1)} %copy-done.16), kind=kOutput, calls=%fused_computation.35 | convolution fusion | flops 1309409280 | bytes 5619712 | tf_op jit(solution)/shard_map/semd,semf->edf/dot_general | solution.py:173
  420.6 1.4 add_convert_fusion.2
  422.1 1.3 collective-permute-start.1
  423.4 10.1 %collective-permute-done.2 = f32[96,2048]{1,0:T(8,128)S(1)} collective-permute-done((f32[96,2048]{1,0:T(8,128)S(1)}, f32[96,2048]{1,0:T(8,128)S(1)}, u32[]{:S(2)}, u32[]{:S(2)}) %collective-permute-start.2) | collective-permute-done | bytes 786464 | tf_op jit(solution)/shard_map/ppermute | solution.py:23
  433.7 2.5 collective-permute-start.3
  436.2 3.6 fusion.28
  439.8 4.2 collective-permute-done.3
  444.0 0.7 copy.210
  444.7 0.7 copy.211
  (95 shorter events, 5.3 us)
Async XLA Ops:
  0.6 22.2 %copy-start = (bf16[1,96,2048]{2,1,0:T(8,128)(2,1)S(1)}, bf16[1,96,2048]{2,1,0:T(8,128)(2,1)}, u32[]{:S(2)}) copy-start(bf16[1,96,2048]{2,1,0:T(8,128)(2,1)} %param.13) | copy-start | bytes 1179652
  8.6 10.2 %copy-start.18 = (s32[1,96,8]{1,2,0:T(8,128)S(1)}, s32[1,96,8]{1,2,0:T(8,128)}, u32[]{:S(2)}) copy-start(s32[1,96,8]{1,2,0:T(8,128)} %param.14) | copy-start | bytes 9220
  8.6 246.8 %all-to-all-start = ((bf16[32,13,2048]{2,1,0:T(8,128)(2,1)}), bf16[32,13,2048]{2,1,0:T(8,128)(2,1)S(1)}, u32[]{:S(2)}, u32[]{:S(2)}) async-start(bf16[32,13,2048]{2,1,0:T(8,128)(2,1)} %copy.141), calls=%async_computation | async-start | bytes 4194304 | tf_op jit(solution)/shard_map/all_to_all | solution.py:232
  23.9 3.9 copy-start.17
  23.9 4.7 %copy-start.8 = (bf16[1,96,2048]{2,1,0:T(8,128)(2,1)S(1)}, bf16[1,96,2048]{2,1,0:T(8,128)(2,1)}, u32[]{:S(2)}) copy-start(bf16[1,96,2048]{2,1,0:T(8,128)(2,1)} %param.16) | copy-start | bytes 1179652
  269.1 6.3 %copy-start.5 = (bf16[1,1,2048,384]{3,2,1,0:T(8,128)(2,1)S(1)}, bf16[1,1,2048,384]{3,2,1,0:T(8,128)(2,1)}, u32[]{:S(2)}) copy-start(bf16[1,1,2048,384]{3,2,1,0:T(8,128)(2,1)} %param.18) | copy-start | bytes 4718596
  269.1 6.3 %copy-start.9 = (bf16[32,26,2048]{2,1,0:T(8,128)(2,1)S(1)}, bf16[32,26,2048]{2,1,0:T(8,128)(2,1)}, u32[]{:S(2)}) copy-start(bf16[32,26,2048]{2,1,0:T(8,128)(2,1)} %get-tuple-element.16) | copy-start | bytes 10223620
  275.4 3.5 copy-start.3
  281.2 63.1 %all-to-all-start.1 = ((bf16[32,13,2048]{2,1,0:T(8,128)(2,1)}), bf16[32,13,2048]{2,1,0:T(8,128)(2,1)S(1)}, u32[]{:S(2)}, u32[]{:S(2)}) async-start(bf16[32,13,2048]{2,1,0:T(8,128)(2,1)} %copy.155), calls=%async_computation.1 | async-start | bytes 4194304 | tf_op jit(solution)/shard_map/all_to_all | solution.py:241
  294.1 7.8 %copy-start.10 = (bf16[32,26,2048]{2,1,0:T(8,128)(2,1)S(1)}, bf16[32,26,2048]{2,1,0:T(8,128)(2,1)}, u32[]{:S(2)}) copy-start(bf16[32,26,2048]{2,1,0:T(8,128)(2,1)} %get-tuple-element.16) | copy-start | bytes 10223620
  294.1 7.8 %copy-start.12 = (bf16[32,26,2048]{2,1,0:T(8,128)(2,1)S(1)}, bf16[32,26,2048]{2,1,0:T(8,128)(2,1)}, u32[]{:S(2)}) copy-start(bf16[32,26,2048]{2,1,0:T(8,128)(2,1)} %get-tuple-element.17) | copy-start | bytes 10223620
  300.7 0.9 copy-start.13
  300.7 1.2 copy-start.15
  302.0 2.4 copy-start.22
  304.4 1.4 copy-start.21
  305.8 1.4 copy-start.20
  307.2 1.5 copy-start.4
  308.7 1.7 copy-start.6
  314.3 36.6 %copy-start.19 = (s32[1,96,8]{1,2,0:T(8,128)S(1)}, s32[1,96,8]{1,2,0:T(8,128)}, u32[]{:S(2)}) copy-start(s32[1,96,8]{1,2,0:T(8,128)} %param.12) | copy-start | bytes 9220
  344.3 1.4 copy-start.2
  345.6 55.4 %all-to-all-start.2 = ((bf16[32,13,2048]{2,1,0:T(8,128)(2,1)}), bf16[32,13,2048]{2,1,0:T(8,128)(2,1)}, u32[]{:S(2)}, u32[]{:S(2)}) async-start(bf16[32,13,2048]{2,1,0:T(8,128)(2,1)} %copy.160), calls=%async_computation.2 | async-start | bytes 4194304 | tf_op jit(solution)/shard_map/all_to_all | solution.py:276
  368.7 51.9 %collective-permute-start = (f32[96,2048]{1,0:T(8,128)S(1)}, f32[96,2048]{1,0:T(8,128)}, u32[]{:S(2)}, u32[]{:S(2)}) collective-permute-start(f32[96,2048]{1,0:T(8,128)S(1)} %fusion.1), channel_id=1, source_target_pairs={{0,1},{1,0},{2,3},{3,2},{4,5},{5,4},{6,7},{7,6},{8,9},{9,8},{10,11... | collective-permute-start | bytes 2359304 | tf_op jit(solution)/shard_map/ppermute | solution.py:23
  407.2 7.6 %copy-start.16 = (bf16[32,1,26,384]{3,2,0,1:T(8,128)(2,1)S(1)}, bf16[32,1,26,384]{3,2,0,1:T(8,128)(2,1)}, u32[]{:S(2)}) copy-start(bf16[32,1,26,384]{3,2,0,1:T(8,128)(2,1)} %copy-done.15) | copy-start | bytes 1916932
  412.2 8.4 %copy-start.7 = (bf16[1,96,2048]{2,1,0:T(8,128)(2,1)S(1)}, bf16[1,96,2048]{2,1,0:T(8,128)(2,1)}, u32[]{:S(2)}) copy-start(bf16[1,96,2048]{2,1,0:T(8,128)(2,1)} %param.10) | copy-start | bytes 1179652
  412.2 21.3 %collective-permute-start.2 = (f32[96,2048]{1,0:T(8,128)S(1)}, f32[96,2048]{1,0:T(8,128)S(1)}, u32[]{:S(2)}, u32[]{:S(2)}) collective-permute-start(f32[96,2048]{1,0:T(8,128)S(1)} %fusion), channel_id=1, source_target_pairs={{0,1},{1,0},{2,3},{3,2},{4,5},{5,4},{6,7},{7,6},{8,9},{9,8},{10,11... | collective-permute-start | bytes 2359304 | tf_op jit(solution)/shard_map/ppermute | solution.py:23
  414.8 21.4 %copy-start.14 = (bf16[32,1,26,384]{3,2,0,1:T(8,128)(2,1)S(1)}, bf16[32,1,26,384]{3,2,0,1:T(8,128)(2,1)}, u32[]{:S(2)}) copy-start(bf16[32,1,26,384]{3,2,0,1:T(8,128)(2,1)} %copy-done.13) | copy-start | bytes 1916932
  420.6 15.6 %copy-start.11 = (bf16[32,26,2048]{2,1,0:T(8,128)(2,1)S(1)}, bf16[32,26,2048]{2,1,0:T(8,128)(2,1)}, u32[]{:S(2)}) copy-start(bf16[32,26,2048]{2,1,0:T(8,128)(2,1)} %get-tuple-element.16) | copy-start | bytes 10223620
  422.1 17.7 %collective-permute-start.1 = (bf16[96,2048]{1,0:T(8,128)(2,1)S(1)}, bf16[96,2048]{1,0:T(8,128)(2,1)S(1)}, u32[]{:S(2)}, u32[]{:S(2)}) collective-permute-start(bf16[96,2048]{1,0:T(8,128)(2,1)S(1)} %add_convert_fusion.2), channel_id=1, source_target_pairs={{192,0},{0,64},{64,128},{128,192},{193,1},{1,65},{65,129},{129,193... | collective-permute-start | bytes 1179656 | tf_op jit(solution)/shard_map/ppermute | solution.py:19
  433.7 10.3 %collective-permute-start.3 = (bf16[96,2048]{1,0:T(8,128)(2,1)S(1)}, bf16[96,2048]{1,0:T(8,128)(2,1)S(1)}, u32[]{:S(2)}, u32[]{:S(2)}) collective-permute-start(bf16[96,2048]{1,0:T(8,128)(2,1)S(1)} %add_convert_fusion.1), channel_id=1, source_target_pairs={{64,0},{128,64},{192,128},{0,192},{65,1},{129,65},{193,129},{1,193... | collective-permute-start | bytes 1179656 | tf_op jit(solution)/shard_map/ppermute | solution.py:19
  436.2 9.3 %copy-start.1 = (bf16[1,96,2048]{2,1,0:T(8,128)(2,1)S(1)}, bf16[1,96,2048]{2,1,0:T(8,128)(2,1)}, u32[]{:S(2)}) copy-start(bf16[1,96,2048]{2,1,0:T(8,128)(2,1)} %param.13) | copy-start | bytes 1179652

commit v10 on v6

--- a/solution.py
+++ b/solution.py
@@ -215,8 +215,14 @@
     back_table = slot_table(back_positions, choices_per)
     send_saved = packed_rows(saved, back_table)
     send_grad = packed_rows(grad_in, back_table, back_mixing)
-    (recv_saved, recv_grad), (gate_other, up_other, down_other) = exchange(
-        (send_saved, send_grad), (gate_half[0], up_half[0], down_half[0]), 0
+    share = MOST // 2
+    side = lax.axis_index("dp")
+    fwd_mine = (fwd_rank >= share).astype(jnp.int32) == side
+    fwd_local = jnp.where(fwd_mine, fwd_flat * share + fwd_rank - side * share, -1)
+    fwd_table = slot_table(fwd_local, choices_per, share)
+    send_inputs = packed_rows(inputs, fwd_table, depth=share)
+    (recv_saved, recv_grad, recv_inputs), (gate_other, up_other, down_other) = exchange(
+        (send_saved, send_grad, send_inputs), (gate_half[0], up_half[0], down_half[0]), 0
     )
     recv_saved, recv_grad = (x.reshape(groups, 1, MOST, model_width) for x in (recv_saved, recv_grad))
     gate_full = jnp.concatenate([gate_half[0], gate_other], 1)
@@ -225,13 +231,6 @@
     gate_mine = lax.dynamic_slice_in_dim(gate_full, mine, half, 0)[None]
     up_mine = lax.dynamic_slice_in_dim(up_full, mine, half, 0)[None]
 
-    share = MOST // 2
-    side = lax.axis_index("dp")
-    fwd_mine = (fwd_rank >= share).astype(jnp.int32) == side
-    fwd_local = jnp.where(fwd_mine, fwd_flat * share + fwd_rank - side * share, -1)
-    fwd_table = slot_table(fwd_local, choices_per, share)
-    send_inputs = packed_rows(inputs, fwd_table, depth=share)
-    recv_inputs = lax.all_to_all(send_inputs, "expert", split_axis=0, concat_axis=0, tiled=True)
     gate_value = jnp.einsum("smd,df->smf", recv_inputs, gate_full, preferred_element_type=jnp.float32)
     up_value = jnp.einsum("smd,df->smf", recv_inputs, up_full, preferred_element_type=jnp.float32)
     hidden = (jax.nn.silu(gate_value) * up_value).astype(jnp.bfloat16)

time: 447 us -> 459 us (1.027)
  Pallas kernels: 224 us -> 250 us
  starting transfers between devices: 40.2 us -> 31.5 us
  matrix products: 51 us -> 46.1 us
    ppermute x3, waiting for transfers between devices: 0.01 us -> 34.6 us  [swapped(): return lax.ppermute(block, 'dp', [(0, 1), (1, 0)])]
    all_to_all x1, waiting for transfers between devices: 32.6 us -> 0.01 us  [local(): lax.all_to_all(out_rows, 'expert', split_axis=0, concat_axis=0, tiled=True)]
    pallas_call x1, Pallas kernels: 224 us -> 250 us  [exchange(): pl.pallas_call(functools.partial(exchange_kernel, n, len(sends), len(swap...]
    all_to_all x1 -> x0, starting transfers between devices: 10.2 us -> none  [local(): lax.all_to_all(send_inputs, 'expert', split_axis=0, concat_axis=0, tiled=...]
  transfers between devices with their start and end apart: 9 -> 8, of which waited for: 4 -> 6; matrix products, arithmetic and copies ran while one was open for 21% -> 13% of each run, Pallas kernels for 51% -> 0%
where the time goes in v10:
time: 459 us; the launch traced here: 451 us
  Pallas kernels  250 us (54%)
  waiting for transfers between devices  68.3 us (15%)
  matrix products  46.1 us (10%)
  local copies, waits for them, and re-layouts  35.9 us (8%)
  starting transfers between devices  31.5 us (7%)
  other arithmetic  18.5 us (4%)
    pallas_call x1, Pallas kernels, exchange(): pl.pallas_call(functools.partial(exchange_kernel, n, len(sends), len(swap...  250 us
    ppermute x3, waiting for transfers between devices, swapped(): return lax.ppermute(block, 'dp', [(0, 1), (1, 0)])  34.6 us
    all_to_all x1, waiting for transfers between devices, local(): lax.all_to_all(grad_part, 'expert', split_axis=0, concat_axis=0, tiled=True)  23.9 us
  transfers between devices with their start and end apart: 8, of which 6 were waited for; matrix products, arithmetic and copies ran while one was open for 13% of the time, Pallas kernels for 0%

profile of v10, /device:TPU:8, one launch (start us, length us, event | category | flops | bytes accessed | tf_op | source)
XLA Modules:
  0.0 451.4 jit_solution(539237628532321728)
XLA Ops:
  0.7 0.8 copy.132
  1.7 0.8 copy.136
  4.2 1.7 reduce-window.16
  6.4 0.9 fusion.11
  8.2 1.7 reduce-window.14
  11.9 2.3 copy.149.refs_2_
  14.2 1.0 convolution_convert_fusion
  15.2 3.9 copy.148.refs_0_
  19.1 3.2 multiply_convert_fusion.refs_1_
  22.3 249.6 %shard_map.137 = (bf16[32,26,2048]{2,1,0:T(8,128)(2,1)}, bf16[32,26,2048]{2,1,0:T(8,128)(2,1)}, bf16[32,13,2048]{2,1,0:T(8,128)(2,1)}, bf16[2048,384]{1,0:T(8,12...) custom-call(bf16[32,26,2048]{2,1,0:T(8,128)(2,1)} %copy.148.refs_0_, ...), custom_call_target="tpu_custom_call" | custom-call | bytes 26476544 | tf_op jit(solution)/shard_map/pallas_call | solution.py:98
  271.9 5.4 %fusion.5 = f32[32,13,768]{2,0,1:T(8,128)} fusion(bf16[2048,384]{1,0:T(8,128)(2,1)} %get-tuple-element.12, bf16[2048,384]{1,0:T(8,128)(2,1)S(1)} %bitcast.216, bf16[32,13,2048]{2,1,0:T(8,128)(2,1)} %get-tuple-element.11), kind=kOutput, calls=%fused_computation.16 | convolution fusion | flops 1314914304 | bytes 6127616 | tf_op jit(solution)/shard_map/smd,df->smf/dot_general | solution.py:234
  277.4 7.5 %fusion.10 = bf16[32,13,2048]{2,0,1:T(8,128)(2,1)S(1)} fusion(bf16[384,2048]{1,0:T(8,128)(2,1)} %get-tuple-element.14, bf16[384,2048]{1,0:T(8,128)(2,1)} %bitcast.214, bf16[2048,384]{1,0:T(8,128)(2,1)} %get-tuple-element.13, bf16[2048,384]{1,0:T(8,128)(2,1)} %bitcast.219, bf16[32,13,2048]{2,1,0:T(8,128)(2,1)} %get-tuple-element.11, f32[32,13,768]{2,0,1:T(8,128)} %fusion.5), kind=kOutput, calls=%fused_computation.25 | convolution fusion | flops 2632597504 | bytes 10977280 | tf_op jit(solution)/shard_map/smf,fd->smd/dot_general | solution.py:237
  284.9 2.3 copy.152
  287.2 9.0 %all-to-all-start = ((bf16[32,13,2048]{2,1,0:T(8,128)(2,1)}), bf16[32,13,2048]{2,1,0:T(8,128)(2,1)S(1)}, u32[]{:S(2)}, u32[]{:S(2)}) async-start(bf16[32,13,2048]{2,1,0:T(8,128)(2,1)} %copy.152), calls=%async_computation | async-start | bytes 4194304 | tf_op jit(solution)/shard_map/all_to_all | solution.py:254
  296.2 5.1 %fusion.22 = f32[32,26,384]{2,1,0:T(8,128)S(1)} fusion(bf16[32,26,2048]{2,1,0:T(8,128)(2,1)} %get-tuple-element.16, bf16[1,1,2048,384]{3,2,1,0:T(8,128)(2,1)} %param.17), kind=kOutput, calls=%fused_computation.40 | convolution fusion | flops 1308622848 | bytes 6258688 | tf_op jit(solution)/shard_map/semd,edf->semf/dot_general | solution.py:153
  301.4 2.3 fusion.24
  304.1 2.8 fusion.32
  306.9 1.1 copy.153
  308.0 1.0 copy.156
  309.0 3.7 collective-permute-start.3
  312.7 3.0 fusion.14
  316.4 21.3 %collective-permute-done.2 = bf16[32,1,26,384]{3,0,2,1:T(8,128)(2,1)} collective-permute-done((bf16[32,1,26,384]{3,0,2,1:T(8,128)(2,1)}, bf16[32,1,26,384]{3,0,2,1:T(8,128)(2,1)}, u32[]{:S(2)}, u32[]{:S(2)}) %collective-permute-start.2) | collective-permute-done | bytes 639008 | tf_op jit(solution)/shard_map/ppermute | solution.py:23
  337.7 1.3 copy.154
  339.0 13.3 %collective-permute-done.3 = bf16[32,1,26,384]{3,0,2,1:T(8,128)(2,1)} collective-permute-done((bf16[32,1,26,384]{3,0,2,1:T(8,128)(2,1)}, bf16[32,1,26,384]{3,0,2,1:T(8,128)(2,1)}, u32[]{:S(2)}, u32[]{:S(2)}) %collective-permute-start.3) | collective-permute-done | bytes 639008 | tf_op jit(solution)/shard_map/ppermute | solution.py:23
  352.2 1.3 copy.157
  354.0 1.2 copy-done.7
  355.6 1.7 fusion.20
  357.5 1.7 fusion.38
  359.3 2.3 copy.159
  361.5 1.3 copy-done.2
  362.9 8.2 %all-to-all-start.1 = ((bf16[32,1,26,1024]{3,2,1,0:T(8,128)(2,1)}), bf16[32,1,26,1024]{3,2,1,0:T(8,128)(2,1)}, u32[]{:S(2)}, u32[]{:S(2)}) async-start(bf16[32,1,26,1024]{3,2,1,0:T(8,128)(2,1)} %copy.159), calls=%async_computation.1 | async-start | bytes 4194304 | tf_op jit(solution)/shard_map/all_to_all | solution.py:266
  371.1 5.9 %fusion.13 = bf16[1,1,2048,384]{3,2,1,0:T(8,128)(2,1)} fusion(bf16[32,26,2048]{2,1,0:T(8,128)(2,1)} %get-tuple-element.16, bf16[32,1,26,384]{3,2,0,1:T(8,128)(2,1)} %copy-done.3), kind=kOutput, calls=%fused_computation.31 | convolution fusion | flops 1309409280 | bytes 5619712 | tf_op jit(solution)/shard_map/semd,semf->edf/dot_general | solution.py:176
  377.0 1.8 reshape.253
  378.9 4.3 gather_fusion
  383.2 5.7 %fusion = f32[96,2048]{1,0:T(8,128)} fusion(bf16[768,2048]{1,0:T(8,128)(2,1)} %gather_fusion, f32[96,8]{1,0:T(8,128)S(1)} %fusion.74), kind=kLoop, calls=%fused_computation.4 | loop fusion | flops 4521984 | bytes 3935232 | tf_op jit(solution)/shard_map/reduce_sum | solution.py:257
  388.9 2.6 collective-permute-start
  391.5 5.7 %fusion.12 = bf16[1,1,2048,384]{3,2,1,0:T(8,128)(2,1)} fusion(bf16[32,26,2048]{2,1,0:T(8,128)(2,1)} %get-tuple-element.16, bf16[32,1,26,384]{3,2,0,1:T(8,128)(2,1)S(1)} %get-tuple-element.18), kind=kOutput, calls=%fused_computation.30 | convolution fusion | flops 1309409280 | bytes 5619712 | tf_op jit(solution)/shard_map/semd,semf->edf/dot_general | solution.py:173
  397.4 23.9 %all-to-all-done.1 = bf16[32,1,26,1024]{3,2,1,0:T(8,128)(2,1)} async-done(((bf16[32,1,26,1024]{3,2,1,0:T(8,128)(2,1)}), bf16[32,1,26,1024]{3,2,1,0:T(8,128)(2,1)}, u32[]{:S(2)}, u32[]{:S(2)}) %all-to-all-start.1) | async-done | bytes 1703968 | tf_op jit(solution)/shard_map/all_to_all | solution.py:266
  421.2 2.5 reshape.256
  423.8 3.6 gather_fusion.1
  427.3 2.5 convert_reduce_fusion
  430.0 5.8 %collective-permute-start.5 = (bf16[96,1024]{1,0:T(8,128)(2,1)S(1)}, bf16[96,1024]{1,0:T(8,128)(2,1)S(1)}, u32[]{:S(2)}, u32[]{:S(2)}) collective-permute-start(bf16[96,1024]{1,0:T(8,128)(2,1)S(1)} %fusion.61), channel_id=1, source_target_pairs={{0,193},{1,192},{64,1},{65,0},{128,65},{129,64},{192,129},{193,128... | collective-permute-start | bytes 589832 | tf_op jit(solution)/shard_map/ppermute | solution.py:147
  435.8 1.0 collective-permute-start.4
  436.8 1.6 add_convert_fusion.1
  438.4 1.1 collective-permute-start.1
  439.5 3.1 collective-permute-done.5
  442.6 3.2 collective-permute-done.4
  446.6 3.6 collective-permute-done.1
  (83 shorter events, 8.8 us)
Async XLA Ops:
  0.6 13.5 %copy-start = (bf16[1,96,2048]{2,1,0:T(8,128)(2,1)S(1)}, bf16[1,96,2048]{2,1,0:T(8,128)(2,1)}, u32[]{:S(2)}) copy-start(bf16[1,96,2048]{2,1,0:T(8,128)(2,1)} %param.13) | copy-start | bytes 1179652
  0.6 10.6 %copy-start.10 = (bf16[1,96,2048]{2,1,0:T(8,128)(2,1)S(1)}, bf16[1,96,2048]{2,1,0:T(8,128)(2,1)}, u32[]{:S(2)}) copy-start(bf16[1,96,2048]{2,1,0:T(8,128)(2,1)} %param.10) | copy-start | bytes 1179652
  15.2 3.9 copy-start.12
  22.3 249.6 %copy-start.6 = (bf16[1,1,2048,384]{3,2,1,0:T(8,128)(2,1)S(1)}, bf16[1,1,2048,384]{3,2,1,0:T(8,128)(2,1)}, u32[]{:S(2)}) copy-start(bf16[1,1,2048,384]{3,2,1,0:T(8,128)(2,1)} %param.17) | copy-start | bytes 4718596
  287.2 74.3 %all-to-all-start = ((bf16[32,13,2048]{2,1,0:T(8,128)(2,1)}), bf16[32,13,2048]{2,1,0:T(8,128)(2,1)S(1)}, u32[]{:S(2)}, u32[]{:S(2)}) async-start(bf16[32,13,2048]{2,1,0:T(8,128)(2,1)} %copy.152), calls=%async_computation | async-start | bytes 4194304 | tf_op jit(solution)/shard_map/all_to_all | solution.py:254
  296.2 5.2 %copy-start.8 = (bf16[1,1,2048,384]{3,2,1,0:T(8,128)(2,1)S(1)}, bf16[1,1,2048,384]{3,2,1,0:T(8,128)(2,1)}, u32[]{:S(2)}) copy-start(bf16[1,1,2048,384]{3,2,1,0:T(8,128)(2,1)} %param.18) | copy-start | bytes 4718596
  296.2 5.2 %copy-start.15 = (bf16[32,26,2048]{2,1,0:T(8,128)(2,1)S(1)}, bf16[32,26,2048]{2,1,0:T(8,128)(2,1)}, u32[]{:S(2)}) copy-start(bf16[32,26,2048]{2,1,0:T(8,128)(2,1)} %get-tuple-element.16) | copy-start | bytes 10223620
  301.4 2.4 copy-start.5
  301.4 2.7 copy-start.16
  306.9 8.9 %copy-start.3 = (bf16[32,1,26,384]{3,2,0,1:T(8,128)(2,1)}, bf16[32,1,26,384]{3,2,0,1:T(8,128)(2,1)S(1)}, u32[]{:S(2)}) copy-start(bf16[32,1,26,384]{3,2,0,1:T(8,128)(2,1)S(1)} %get-tuple-element.17) | copy-start | bytes 1916932
  308.0 29.7 %collective-permute-start.2 = (bf16[32,1,26,384]{3,0,2,1:T(8,128)(2,1)}, bf16[32,1,26,384]{3,0,2,1:T(8,128)(2,1)}, u32[]{:S(2)}, u32[]{:S(2)}) collective-permute-start(bf16[32,1,26,384]{3,0,2,1:T(8,128)(2,1)} %copy.153), channel_id=1, source_target_pairs={{0,1},{1,0},{2,3},{3,2},{4,5},{5,4},{6,7},{7,6},{8,9},{9,8},{10,11... | collective-permute-start | bytes 1916936 | tf_op jit(solution)/shard_map/ppermute | solution.py:23
  309.0 6.8 %copy-start.14 = (s32[1,96,8]{1,2,0:T(8,128)S(1)}, s32[1,96,8]{1,2,0:T(8,128)}, u32[]{:S(2)}) copy-start(s32[1,96,8]{1,2,0:T(8,128)} %param.12) | copy-start | bytes 9220
  309.0 43.2 %collective-permute-start.3 = (bf16[32,1,26,384]{3,0,2,1:T(8,128)(2,1)}, bf16[32,1,26,384]{3,0,2,1:T(8,128)(2,1)}, u32[]{:S(2)}, u32[]{:S(2)}) collective-permute-start(bf16[32,1,26,384]{3,0,2,1:T(8,128)(2,1)} %copy.156), channel_id=1, source_target_pairs={{0,1},{1,0},{2,3},{3,2},{4,5},{5,4},{6,7},{7,6},{8,9},{9,8},{10,11... | collective-permute-start | bytes 1916936 | tf_op jit(solution)/shard_map/ppermute | solution.py:23
  316.1 37.4 %copy-start.4 = (bf16[32,1,26,384]{3,2,0,1:T(8,128)(2,1)S(1)}, bf16[32,1,26,384]{3,2,0,1:T(8,128)(2,1)}, u32[]{:S(2)}) copy-start(bf16[32,1,26,384]{3,2,0,1:T(8,128)(2,1)} %copy-done.3) | copy-start | bytes 1916932
  353.8 1.4 copy-start.7
  353.8 1.9 copy-start.18
  355.6 1.7 copy-start.9
  355.6 1.9 copy-start.17
  361.5 1.3 copy-start.2
  362.9 58.4 %all-to-all-start.1 = ((bf16[32,1,26,1024]{3,2,1,0:T(8,128)(2,1)}), bf16[32,1,26,1024]{3,2,1,0:T(8,128)(2,1)}, u32[]{:S(2)}, u32[]{:S(2)}) async-start(bf16[32,1,26,1024]{3,2,1,0:T(8,128)(2,1)} %copy.159), calls=%async_computation.1 | async-start | bytes 4194304 | tf_op jit(solution)/shard_map/all_to_all | solution.py:266
  388.9 47.9 %collective-permute-start = (f32[96,2048]{1,0:T(8,128)}, f32[96,2048]{1,0:T(8,128)}, u32[]{:S(2)}, u32[]{:S(2)}) collective-permute-start(f32[96,2048]{1,0:T(8,128)} %fusion), channel_id=1, source_target_pairs={{0,1},{1,0},{2,3},{3,2},{4,5},{5,4},{6,7},{7,6},{8,9},{9,8},{10,11... | collective-permute-start | bytes 2359304 | tf_op jit(solution)/shard_map/ppermute | solution.py:23
  427.3 2.5 copy-start.13
  427.3 9.4 %copy-start.11 = (bf16[1,96,2048]{2,1,0:T(8,128)(2,1)S(1)}, bf16[1,96,2048]{2,1,0:T(8,128)(2,1)}, u32[]{:S(2)}) copy-start(bf16[1,96,2048]{2,1,0:T(8,128)(2,1)} %param.10) | copy-start | bytes 1179652
  430.0 12.6 %collective-permute-start.5 = (bf16[96,1024]{1,0:T(8,128)(2,1)S(1)}, bf16[96,1024]{1,0:T(8,128)(2,1)S(1)}, u32[]{:S(2)}, u32[]{:S(2)}) collective-permute-start(bf16[96,1024]{1,0:T(8,128)(2,1)S(1)} %fusion.61), channel_id=1, source_target_pairs={{0,193},{1,192},{64,1},{65,0},{128,65},{129,64},{192,129},{193,128... | collective-permute-start | bytes 589832 | tf_op jit(solution)/shard_map/ppermute | solution.py:147
  435.8 10.0 %collective-permute-start.4 = (bf16[96,1024]{1,0:T(8,128)(2,1)S(1)}, bf16[96,1024]{1,0:T(8,128)(2,1)S(1)}, u32[]{:S(2)}, u32[]{:S(2)}) collective-permute-start(bf16[96,1024]{1,0:T(8,128)(2,1)S(1)} %fusion.61), channel_id=1, source_target_pairs={{64,0},{128,64},{192,128},{0,192},{65,1},{129,65},{193,129},{1,193... | collective-permute-start | bytes 589832 | tf_op jit(solution)/shard_map/ppermute | solution.py:19
  436.8 14.2 %copy-start.1 = (bf16[1,96,2048]{2,1,0:T(8,128)(2,1)S(1)}, bf16[1,96,2048]{2,1,0:T(8,128)(2,1)}, u32[]{:S(2)}) copy-start(bf16[1,96,2048]{2,1,0:T(8,128)(2,1)} %param.13) | copy-start | bytes 1179652
  438.4 11.8 %collective-permute-start.1 = (bf16[96,2048]{1,0:T(8,128)(2,1)S(1)}, bf16[96,2048]{1,0:T(8,128)(2,1)S(1)}, u32[]{:S(2)}, u32[]{:S(2)}) collective-permute-start(bf16[96,2048]{1,0:T(8,128)(2,1)S(1)} %add_convert_fusion.1), channel_id=1, source_target_pairs={{192,0},{0,64},{64,128},{128,192},{193,1},{1,65},{65,129},{129,193... | collective-permute-start | bytes 1179656 | tf_op jit(solution)/shard_map/ppermute | solution.py:19

commit v11 on v6

--- a/solution.py
+++ b/solution.py
@@ -239,6 +239,7 @@
         "smf,fd->smd", hidden, down_full, preferred_element_type=jnp.float32
     ).astype(jnp.bfloat16)
 
+    out_rows, recv_saved, recv_grad = lax.optimization_barrier((out_rows, recv_saved, recv_grad))
     back_gate, back_up = project(recv_saved, gate_half, up_half)
     back_hidden, gate_grad, up_grad = local_backward(back_gate, back_up, recv_grad, down_half)
     gate_term, up_term, down_term = weight_terms(

time: 447 us -> 451 us (level)
  waiting for transfers between devices: 66.8 us -> 75.8 us
  local copies, waits for them, and re-layouts: 38.1 us -> 31.3 us
    ppermute x3, waiting for transfers between devices: 0.01 us -> 44.2 us  [swapped(): return lax.ppermute(block, 'dp', [(0, 1), (1, 0)])]
    all_to_all x1, waiting for transfers between devices: 32.6 us -> 0.01 us  [local(): lax.all_to_all(out_rows, 'expert', split_axis=0, concat_axis=0, tiled=True)]
  transfers between devices with their start and end apart: 9 -> 9, of which waited for: 4 -> 6; matrix products, arithmetic and copies ran while one was open for 21% -> 15% of each run, Pallas kernels for 51% -> 51%
where the time goes in v11:
time: 451 us; the launch traced here: 443 us
  Pallas kernels  225 us (50%)
  waiting for transfers between devices  75.8 us (17%)
  matrix products  52 us (12%)
  starting transfers between devices  40.5 us (9%)
  local copies, waits for them, and re-layouts  31.3 us (7%)
  other arithmetic  17.1 us (4%)
    pallas_call x1, Pallas kernels, exchange(): pl.pallas_call(functools.partial(exchange_kernel, n, len(sends), len(swap...  225 us
    ppermute x3, waiting for transfers between devices, swapped(): return lax.ppermute(block, 'dp', [(0, 1), (1, 0)])  44.2 us
    all_to_all x1, waiting for transfers between devices, local(): lax.all_to_all(grad_part, 'expert', split_axis=0, concat_axis=0, tiled=True)  21.4 us
    all_to_all x1, starting transfers between devices, local(): lax.all_to_all(out_rows, 'expert', split_axis=0, concat_axis=0, tiled=True)  11.5 us
    all_to_all x1, starting transfers between devices, local(): lax.all_to_all(send_inputs, 'expert', split_axis=0, concat_axis=0, tiled=...  10.2 us
  transfers between devices with their start and end apart: 9, of which 6 were waited for; matrix products, arithmetic and copies ran while one was open for 15% of the time, Pallas kernels for 51%

profile of v11, /device:TPU:8, one launch (start us, length us, event | category | flops | bytes accessed | tf_op | source)
XLA Modules:
  0.0 443.0 jit_solution(11156734359974420732)
XLA Ops:
  0.6 0.8 copy.128
  1.7 1.7 reduce-window.14
  3.9 0.6 fusion.58
  4.7 1.6 convolution_convert_fusion.1
  6.3 2.3 copy.135
  8.6 10.2 %all-to-all-start = ((bf16[32,13,2048]{2,1,0:T(8,128)(2,1)}), bf16[32,13,2048]{2,1,0:T(8,128)(2,1)S(1)}, u32[]{:S(2)}, u32[]{:S(2)}) async-start(bf16[32,13,2048]{2,1,0:T(8,128)(2,1)} %copy.135), calls=%async_computation | async-start | bytes 4194304 | tf_op jit(solution)/shard_map/all_to_all | solution.py:234
  19.2 1.7 reduce-window.16
  21.4 0.9 fusion.29
  23.3 1.0 convolution_convert_fusion
  24.4 3.9 copy.145.refs_0_
  28.7 3.2 multiply_convert_fusion.refs_1_
  31.9 224.6 %shard_map.137 = (bf16[32,26,2048]{2,1,0:T(8,128)(2,1)}, bf16[32,26,2048]{2,1,0:T(8,128)(2,1)}, bf16[2048,384]{1,0:T(8,128)(2,1)}, bf16[2048,384]{1,0:T(8,128)(2,1)}, bf16[384,2048]{1,0:T(8,128)(2,1)}) custom-call(bf16[32,26,2048]{2,1,0:T(8,128)(2,1)} %copy.145.refs_0_, bf16[32,26,2048]{2,1,0:T(8,128)(2,1)} %multiply_convert_fusion.refs_1_, ...), custom_call_target="tpu_custom_call" | custom-call | bytes 23068672 | tf_op jit(solution)/shard_map/pallas_call | solution.py:98
  256.6 5.5 %fusion.17 = f32[32,13,768]{2,0,1:T(8,128)} fusion(bf16[2048,384]{1,0:T(8,128)(2,1)} %get-tuple-element.13, bf16[2048,384]{1,0:T(8,128)(2,1)} %bitcast.240, bf16[32,13,2048]{2,1,0:T(8,128)(2,1)S(1)} %all-to-all-done), kind=kOutput, calls=%fused_computation.28 | convolution fusion | flops 1314914304 | bytes 6127616 | tf_op jit(solution)/shard_map/smd,df->smf/dot_general | solution.py:235
  262.0 8.2 %fusion.28 = bf16[32,13,2048]{2,0,1:T(8,128)(2,1)} fusion(bf16[384,2048]{1,0:T(8,128)(2,1)} %get-tuple-element.15, bf16[384,2048]{1,0:T(8,128)(2,1)} %bitcast.238, bf16[2048,384]{1,0:T(8,128)(2,1)} %get-tuple-element.14, bf16[2048,384]{1,0:T(8,128)(2,1)} %bitcast.243, bf16[32,13,2048]{2,1,0:T(8,128)(2,1)S(1)} %all-to-all-done, f32[32,13,768]{2,0,1:T(8,128)} %fusion.17), kind=kOutput, calls=%fused_computation.37 | convolution fusion | flops 2632597504 | bytes 10977280 | tf_op jit(solution)/shard_map/smf,fd->smd/dot_general | solution.py:238
  270.3 6.3 %fusion.5 = f32[32,26,384]{2,1,0:T(8,128)} fusion(bf16[32,1,26,2048]{3,2,0,1:T(8,128)(2,1)} %bitcast.248, bf16[1,1,2048,384]{3,2,1,0:T(8,128)(2,1)} %param.17), kind=kOutput, calls=%fused_computation.9 | convolution fusion | flops 1308622848 | bytes 6258688 | tf_op jit(solution)/shard_map/semd,edf->semf/dot_general | solution.py:153
  276.5 2.2 copy.148
  278.8 11.5 %all-to-all-start.1 = ((bf16[32,13,2048]{2,1,0:T(8,128)(2,1)}), bf16[32,13,2048]{2,1,0:T(8,128)(2,1)S(1)}, u32[]{:S(2)}, u32[]{:S(2)}) async-start(bf16[32,13,2048]{2,1,0:T(8,128)(2,1)} %copy.148), calls=%async_computation.1 | async-start | bytes 4194304 | tf_op jit(solution)/shard_map/all_to_all | solution.py:256
  290.3 5.1 %fusion.7 = f32[32,26,384]{2,1,0:T(8,128)S(1)} fusion(bf16[32,1,26,2048]{3,2,0,1:T(8,128)(2,1)} %bitcast.249, bf16[1,1,2048,384]{3,2,1,0:T(8,128)(2,1)} %param.18), kind=kOutput, calls=%fused_computation.11 | convolution fusion | flops 1308622848 | bytes 6258688 | tf_op jit(solution)/shard_map/semd,edf->semf/dot_general | solution.py:154
  295.5 2.8 fusion.53
  298.5 2.4 collective-permute-start.3
  301.2 1.3 collective-permute-start.2
  302.7 26.9 %collective-permute-done.3 = bf16[32,1,26,384]{3,0,2,1:T(8,128)(2,1)S(1)} collective-permute-done((bf16[32,1,26,384]{3,0,2,1:T(8,128)(2,1)S(1)}, bf16[32,1,26,384]{3,0,2,1:T(8,128)(2,1)S(1)}, u32[]{:S(2)}, u32[]{:S(2)}) %collective-permute-start.3) | collective-permute-done | bytes 639008 | tf_op jit(solution)/shard_map/ppermute | solution.py:23
  329.8 17.3 %collective-permute-done.2 = bf16[32,1,26,384]{3,0,2,1:T(8,128)(2,1)S(1)} collective-permute-done((bf16[32,1,26,384]{3,0,2,1:T(8,128)(2,1)S(1)}, bf16[32,1,26,384]{3,0,2,1:T(8,128)(2,1)S(1)}, u32[]{:S(2)}, u32[]{:S(2)}) %collective-permute-start.2) | collective-permute-done | bytes 639008 | tf_op jit(solution)/shard_map/ppermute | solution.py:23
  347.9 1.2 copy-done.6
  349.5 1.7 fusion.44
  351.4 1.7 fusion.59
  353.1 2.4 copy.155
  355.5 1.4 copy-done.2
  356.9 6.9 %all-to-all-start.2 = ((bf16[32,1,26,1024]{3,2,1,0:T(8,128)(2,1)}), bf16[32,1,26,1024]{3,2,1,0:T(8,128)(2,1)}, u32[]{:S(2)}, u32[]{:S(2)}) async-start(bf16[32,1,26,1024]{3,2,1,0:T(8,128)(2,1)} %copy.155), calls=%async_computation.2 | async-start | bytes 4194304 | tf_op jit(solution)/shard_map/all_to_all | solution.py:268
  363.8 6.1 %fusion.33 = bf16[1,1,2048,384]{3,2,1,0:T(8,128)(2,1)} fusion(bf16[32,1,26,2048]{3,2,0,1:T(8,128)(2,1)} %bitcast.250, bf16[32,1,26,384]{3,2,0,1:T(8,128)(2,1)} %copy-done.3), kind=kOutput, calls=%fused_computation.43 | convolution fusion | flops 1309409280 | bytes 5619712 | tf_op jit(solution)/shard_map/semd,semf->edf/dot_general | solution.py:176
  369.9 3.1 fusion.36
  373.0 1.8 reshape.257
  374.8 4.3 gather_fusion
  379.1 5.7 %fusion = f32[96,2048]{1,0:T(8,128)} fusion(bf16[768,2048]{1,0:T(8,128)(2,1)} %gather_fusion, f32[96,8]{1,0:T(8,128)S(1)} %fusion.95), kind=kLoop, calls=%fused_computation.4 | loop fusion | flops 4521984 | bytes 3935232 | tf_op jit(solution)/shard_map/reduce_sum | solution.py:259
  384.8 1.9 collective-permute-start
  386.7 5.7 %fusion.30 = bf16[1,1,2048,384]{3,2,1,0:T(8,128)(2,1)} fusion(bf16[32,1,26,2048]{3,2,0,1:T(8,128)(2,1)} %bitcast.251, bf16[32,1,26,384]{3,2,0,1:T(8,128)(2,1)S(1)} %get-tuple-element.22), kind=kOutput, calls=%fused_computation.42 | convolution fusion | flops 1309409280 | bytes 5619712 | tf_op jit(solution)/shard_map/semd,semf->edf/dot_general | solution.py:173
  392.5 21.4 %all-to-all-done.2 = bf16[32,1,26,1024]{3,2,1,0:T(8,128)(2,1)} async-done(((bf16[32,1,26,1024]{3,2,1,0:T(8,128)(2,1)}), bf16[32,1,26,1024]{3,2,1,0:T(8,128)(2,1)}, u32[]{:S(2)}, u32[]{:S(2)}) %all-to-all-start.2) | async-done | bytes 1703968 | tf_op jit(solution)/shard_map/all_to_all | solution.py:268
  413.9 2.8 reshape.262
  416.7 3.6 gather_fusion.1
  420.2 2.5 convert_reduce_fusion
  422.9 2.9 collective-permute-start.4
  425.8 2.5 collective-permute-start.5
  428.3 1.6 add_convert_fusion.1
  429.9 0.9 collective-permute-start.1
  431.0 4.3 collective-permute-done.5
  435.4 0.8 maximum_bitcast_fusion.6
  436.2 5.5 %collective-permute-done.1 = bf16[96,2048]{1,0:T(8,128)(2,1)S(1)} collective-permute-done((bf16[96,2048]{1,0:T(8,128)(2,1)S(1)}, bf16[96,2048]{1,0:T(8,128)(2,1)S(1)}, u32[]{:S(2)}, u32[]{:S(2)}) %collective-permute-start.1) | collective-permute-done | bytes 393248 | tf_op jit(solution)/shard_map/ppermute | solution.py:19
  441.7 0.7 copy.177
  (91 shorter events, 5.7 us)
Async XLA Ops:
  0.6 22.7 %copy-start = (bf16[1,96,2048]{2,1,0:T(8,128)(2,1)S(1)}, bf16[1,96,2048]{2,1,0:T(8,128)(2,1)}, u32[]{:S(2)}) copy-start(bf16[1,96,2048]{2,1,0:T(8,128)(2,1)} %param.13) | copy-start | bytes 1179652
  8.6 10.2 %copy-start.12 = (s32[1,96,8]{1,2,0:T(8,128)S(1)}, s32[1,96,8]{1,2,0:T(8,128)}, u32[]{:S(2)}) copy-start(s32[1,96,8]{1,2,0:T(8,128)} %param.14) | copy-start | bytes 9220
  8.6 14.0 %copy-start.11 = (s32[1,96,8]{1,2,0:T(8,128)S(1)}, s32[1,96,8]{1,2,0:T(8,128)}, u32[]{:S(2)}) copy-start(s32[1,96,8]{1,2,0:T(8,128)} %param.15) | copy-start | bytes 9220
  8.6 247.9 %all-to-all-start = ((bf16[32,13,2048]{2,1,0:T(8,128)(2,1)}), bf16[32,13,2048]{2,1,0:T(8,128)(2,1)S(1)}, u32[]{:S(2)}, u32[]{:S(2)}) async-start(bf16[32,13,2048]{2,1,0:T(8,128)(2,1)} %copy.135), calls=%async_computation | async-start | bytes 4194304 | tf_op jit(solution)/shard_map/all_to_all | solution.py:234
  24.4 4.2 copy-start.13
  24.4 4.3 copy-start.9
  270.3 6.3 %copy-start.4 = (bf16[32,13,2048]{2,0,1:T(8,128)(2,1)S(1)}, bf16[32,13,2048]{2,0,1:T(8,128)(2,1)}, u32[]{:S(2)}) copy-start(bf16[32,13,2048]{2,0,1:T(8,128)(2,1)} %fusion.28) | copy-start | bytes 5111812
  278.8 76.7 %all-to-all-start.1 = ((bf16[32,13,2048]{2,1,0:T(8,128)(2,1)}), bf16[32,13,2048]{2,1,0:T(8,128)(2,1)S(1)}, u32[]{:S(2)}, u32[]{:S(2)}) async-start(bf16[32,13,2048]{2,1,0:T(8,128)(2,1)} %copy.148), calls=%async_computation.1 | async-start | bytes 4194304 | tf_op jit(solution)/shard_map/all_to_all | solution.py:256
  290.3 5.2 %copy-start.5 = (bf16[1,1,384,2048]{3,2,1,0:T(8,128)(2,1)S(1)}, bf16[1,1,384,2048]{3,2,1,0:T(8,128)(2,1)}, u32[]{:S(2)}) copy-start(bf16[1,1,384,2048]{3,2,1,0:T(8,128)(2,1)} %param.19) | copy-start | bytes 4718596
  290.3 5.2 %copy-start.14 = (bf16[32,26,2048]{2,1,0:T(8,128)(2,1)S(1)}, bf16[32,26,2048]{2,1,0:T(8,128)(2,1)}, u32[]{:S(2)}) copy-start(bf16[32,26,2048]{2,1,0:T(8,128)(2,1)} %get-tuple-element.17) | copy-start | bytes 10223620
  290.3 5.2 %copy-start.18 = (f32[32,26,384]{2,1,0:T(8,128)S(1)}, f32[32,26,384]{2,1,0:T(8,128)}, u32[]{:S(2)}) copy-start(f32[32,26,384]{2,1,0:T(8,128)} %fusion.5) | copy-start | bytes 3833860
  295.5 2.8 copy-start.20
  298.3 49.1 %copy-start.3 = (bf16[32,1,26,384]{3,2,0,1:T(8,128)(2,1)}, bf16[32,1,26,384]{3,2,0,1:T(8,128)(2,1)S(1)}, u32[]{:S(2)}) copy-start(bf16[32,1,26,384]{3,2,0,1:T(8,128)(2,1)S(1)} %get-tuple-element.21) | copy-start | bytes 1916932
  298.5 31.1 %collective-permute-start.3 = (bf16[32,1,26,384]{3,0,2,1:T(8,128)(2,1)S(1)}, bf16[32,1,26,384]{3,0,2,1:T(8,128)(2,1)S(1)}, u32[]{:S(2)}, u32[]{:S(2)}) collective-permute-start(bf16[32,1,26,384]{3,0,2,1:T(8,128)(2,1)S(1)} %copy.152), channel_id=1, source_target_pairs={{0,1},{1,0},{2,3},{3,2},{4,5},{5,4},{6,7},{7,6},{8,9},{9,8},{10,11... | collective-permute-start | bytes 1916936 | tf_op jit(solution)/shard_map/ppermute | solution.py:23
  301.2 46.0 %collective-permute-start.2 = (bf16[32,1,26,384]{3,0,2,1:T(8,128)(2,1)S(1)}, bf16[32,1,26,384]{3,0,2,1:T(8,128)(2,1)S(1)}, u32[]{:S(2)}, u32[]{:S(2)}) collective-permute-start(bf16[32,1,26,384]{3,0,2,1:T(8,128)(2,1)S(1)} %copy.149), channel_id=1, source_target_pairs={{0,1},{1,0},{2,3},{3,2},{4,5},{5,4},{6,7},{7,6},{8,9},{9,8},{10,11... | collective-permute-start | bytes 1916936 | tf_op jit(solution)/shard_map/ppermute | solution.py:23
  347.6 1.4 copy-start.6
  347.6 1.9 copy-start.17
  349.5 1.7 copy-start.7
  349.5 1.9 copy-start.16
  355.5 1.4 copy-start.2
  356.9 57.0 %all-to-all-start.2 = ((bf16[32,1,26,1024]{3,2,1,0:T(8,128)(2,1)}), bf16[32,1,26,1024]{3,2,1,0:T(8,128)(2,1)}, u32[]{:S(2)}, u32[]{:S(2)}) async-start(bf16[32,1,26,1024]{3,2,1,0:T(8,128)(2,1)} %copy.155), calls=%async_computation.2 | async-start | bytes 4194304 | tf_op jit(solution)/shard_map/all_to_all | solution.py:268
  363.7 6.1 %copy-start.15 = (bf16[32,26,2048]{2,1,0:T(8,128)(2,1)S(1)}, bf16[32,26,2048]{2,1,0:T(8,128)(2,1)}, u32[]{:S(2)}) copy-start(bf16[32,26,2048]{2,1,0:T(8,128)(2,1)} %get-tuple-element.17) | copy-start | bytes 10223620
  363.8 6.1 %copy-start.19 = (f32[32,26,384]{2,1,0:T(8,128)S(1)}, f32[32,26,384]{2,1,0:T(8,128)}, u32[]{:S(2)}) copy-start(f32[32,26,384]{2,1,0:T(8,128)} %fusion.5) | copy-start | bytes 3833860
  363.8 6.1 %copy-start.21 = (f32[32,26,384]{2,1,0:T(8,128)S(1)}, f32[32,26,384]{2,1,0:T(8,128)}, u32[]{:S(2)}) copy-start(f32[32,26,384]{2,1,0:T(8,128)} %copy-done.20) | copy-start | bytes 3833860
  384.8 43.4 %collective-permute-start = (f32[96,2048]{1,0:T(8,128)}, f32[96,2048]{1,0:T(8,128)}, u32[]{:S(2)}, u32[]{:S(2)}) collective-permute-start(f32[96,2048]{1,0:T(8,128)} %fusion), channel_id=1, source_target_pairs={{0,1},{1,0},{2,3},{3,2},{4,5},{5,4},{6,7},{7,6},{8,9},{9,8},{10,11... | collective-permute-start | bytes 2359304 | tf_op jit(solution)/shard_map/ppermute | solution.py:23
  420.2 2.5 copy-start.10
  420.2 8.0 %copy-start.8 = (bf16[1,96,2048]{2,1,0:T(8,128)(2,1)S(1)}, bf16[1,96,2048]{2,1,0:T(8,128)(2,1)}, u32[]{:S(2)}) copy-start(bf16[1,96,2048]{2,1,0:T(8,128)(2,1)} %param.10) | copy-start | bytes 1179652
  422.9 8.2 %collective-permute-start.4 = (bf16[96,1024]{1,0:T(8,128)(2,1)S(1)}, bf16[96,1024]{1,0:T(8,128)(2,1)S(1)}, u32[]{:S(2)}, u32[]{:S(2)}) collective-permute-start(bf16[96,1024]{1,0:T(8,128)(2,1)S(1)} %fusion.82), channel_id=1, source_target_pairs={{64,0},{128,64},{192,128},{0,192},{65,1},{129,65},{193,129},{1,193... | collective-permute-start | bytes 589832 | tf_op jit(solution)/shard_map/ppermute | solution.py:19
  425.8 9.6 %collective-permute-start.5 = (bf16[96,1024]{1,0:T(8,128)(2,1)S(1)}, bf16[96,1024]{1,0:T(8,128)(2,1)S(1)}, u32[]{:S(2)}, u32[]{:S(2)}) collective-permute-start(bf16[96,1024]{1,0:T(8,128)(2,1)S(1)} %fusion.82), channel_id=1, source_target_pairs={{0,193},{1,192},{64,1},{65,0},{128,65},{129,64},{192,129},{193,128... | collective-permute-start | bytes 589832 | tf_op jit(solution)/shard_map/ppermute | solution.py:147
  428.3 14.2 %copy-start.1 = (bf16[1,96,2048]{2,1,0:T(8,128)(2,1)S(1)}, bf16[1,96,2048]{2,1,0:T(8,128)(2,1)}, u32[]{:S(2)}) copy-start(bf16[1,96,2048]{2,1,0:T(8,128)(2,1)} %param.13) | copy-start | bytes 1179652
  429.9 11.8 %collective-permute-start.1 = (bf16[96,2048]{1,0:T(8,128)(2,1)S(1)}, bf16[96,2048]{1,0:T(8,128)(2,1)S(1)}, u32[]{:S(2)}, u32[]{:S(2)}) collective-permute-start(bf16[96,2048]{1,0:T(8,128)(2,1)S(1)} %add_convert_fusion.1), channel_id=1, source_target_pairs={{192,0},{0,64},{64,128},{128,192},{193,1},{1,65},{65,129},{129,193... | collective-permute-start | bytes 1179656 | tf_op jit(solution)/shard_map/ppermute | solution.py:19
